TPU v7x, 512 devices: a whole 4x8x8 slice. The times are simulated.
512 devices in a mesh: head: 8 (over x, core), seq: 64 (over z, y).
Axes of the slice: x: 4, y: 8, z: 8, core: 2. Of those that a mesh axis runs over, the one named last changes fastest.
Arguments:
- query_rows: bfloat16 [8, 32768, 512], P('head', 'seq'), may hold values from -16 to 16
- key_rows: bfloat16 [8, 32768, 512], P('head', 'seq'), may hold values from -16 to 16
- value_rows: bfloat16 [8, 32768, 512], P('head', 'seq'), may hold values from -6 to 6
- step_rate: float32 [8, 32768], P('head', 'seq'), may hold values from 0.15 to 162
- doc_start: int32 [32768], P('seq'), may hold values from 0 to 32767, as said below
- speech_flag: int32 [32768], P('seq'), may hold values 0 or 1
- w_gate: bfloat16 [8, 512, 512], P('head'), may hold values from -0.25 to 0.25
- w_up: bfloat16 [8, 512, 512], P('head'), may hold values from -0.25 to 0.25
- w_down: bfloat16 [8, 512, 512], P('head'), may hold values from -0.25 to 0.25
- w_cond: bfloat16 [4096, 512], P('head'), may hold values from -0.09375 to 0.09375
Outputs:
- mixed: bfloat16 [8, 32768, 512], P('head', 'seq')
- cond: bfloat16 [64, 512, 512], P('seq', 'head')
Inputs may be any that keep to these rules, and one draw needn't show every extreme that they name: doc_start[p] is the position of the first token of the document holding token p: at most p, never falling along the sequence, and doc_start[q] = q wherever a document begins; the last token begins a document of its own.
All inputs are finite; a program needn't handle non-finite values. No bound on the sum of `speech_flag` on one device may be relied on, other than what follows from the above.
Results may differ from a plain program's by a relative error of at most 0.015.
Values may be sent and summed in bfloat16 or wider, within the bound.
No kernel may reach another device: no remote copies, remote signals or barrier semaphores. Data moves between devices by JAX's collectives and lax.ppermute only.
A program may use at most 64 MiB of HBM per device.

v0:
```python
import math

import jax
import jax.numpy as jnp
from jax import lax
from jax.sharding import PartitionSpec as P

WIN = 512


eps_norm = 1e-06


def passed_along(block, axis, distance):
    devices = range(lax.axis_size(axis))
    route = [(i - distance, i) for i in devices if i - distance in devices]
    return lax.ppermute(block, axis, route)


def renorm_rows(old_rows, summed, factor):
    old_f = old_rows.astype(jnp.float32)
    updated = old_f + summed * factor[None, :, None, None]
    old_norm = jnp.sqrt(jnp.sum(old_f * old_f, axis=-1, keepdims=True))
    new_norm = jnp.sqrt(jnp.sum(updated * updated, axis=-1, keepdims=True) + eps_norm)
    return (updated * (old_norm / new_norm)).astype(jnp.bfloat16)


def local(
    query_rows,
    key_rows,
    value_rows,
    step_rate,
    doc_start,
    speech_flag,
    w_gate,
    w_up,
    w_down,
    w_cond,
):
    head_local, tok_local, head_width = query_rows.shape
    cond_width = w_cond.shape[1]
    seq_count = lax.axis_size("seq")
    head_count = lax.axis_size("head")
    seq_index = lax.axis_index("seq")
    offset = seq_index * tok_local
    half_seq = seq_count // 2
    update_len = tok_local * half_seq
    in_first = seq_index < half_seq
    speech_on = speech_flag.astype(jnp.float32)
    prev_key, prev_value = passed_along((key_rows, value_rows), "seq", 1)
    keys_all = jnp.concatenate([prev_key, key_rows], axis=1)
    values_all = jnp.concatenate([prev_value, value_rows], axis=1)
    block_rows = min(512, tok_local)
    score_scale = 1.0 / math.sqrt(head_width)

    def attend(row_start):
        pos_query = offset + row_start + jnp.arange(block_rows, dtype=jnp.int32)
        pos_key = offset + row_start - WIN + jnp.arange(WIN + block_rows, dtype=jnp.int32)
        allowed = (
            (pos_key[None, :] <= pos_query[:, None])
            & (pos_key[None, :] > pos_query[:, None] - WIN)
            & (pos_key[None, :] >= doc_start[:, None])
        )
        scores = (
            jnp.einsum("hqd,hkd->hqk", query_rows, keys_all, preferred_element_type=jnp.float32)
            * score_scale
        )
        scores = jnp.where(allowed[None], scores, -1e30)
        row_max = jnp.max(scores, axis=-1, keepdims=True)
        expon = jnp.exp(scores - row_max)
        prob_bf = (expon / jnp.sum(expon, axis=-1, keepdims=True)).astype(jnp.bfloat16)
        return jnp.einsum("hqk,hkd->hqd", prob_bf, values_all, preferred_element_type=jnp.float32)

    blocks = lax.map(attend, jnp.arange(tok_local // block_rows, dtype=jnp.int32) * block_rows)
    attended = jnp.moveaxis(blocks, 0, 1).reshape(head_local, tok_local, head_width)
    first_mask = in_first.astype(jnp.float32)
    rate_local = jnp.sum(step_rate, axis=1) * first_mask
    token_mask = speech_on * first_mask
    scaled = (
        token_mask[None, :, None] * step_rate[:, :, None] * value_rows.astype(jnp.float32)
    ).astype(jnp.bfloat16)
    gate_pre = jnp.einsum("htd,hrd->htr", key_rows, w_gate, preferred_element_type=jnp.float32)
    up_pre = jnp.einsum("htd,hrd->htr", key_rows, w_up, preferred_element_type=jnp.float32)
    sigma = jax.nn.sigmoid(gate_pre)
    active = gate_pre * sigma
    hidden_zero = (active * up_pre).astype(jnp.bfloat16)
    back = jnp.einsum("htd,hdr->htr", scaled, w_down, preferred_element_type=jnp.float32)
    grad_gate = (back * up_pre * sigma * (1.0 + gate_pre * (1.0 - sigma))).astype(jnp.bfloat16)
    grad_up = (back * active).astype(jnp.bfloat16)
    w_zero = jnp.transpose(jnp.stack((w_gate, w_up, w_down), axis=2), (1, 0, 2, 3))
    unit_scale = jnp.ones((head_local,), jnp.float32)
    totals = lax.psum(rate_local, "seq")
    inner = 2.0 * update_len / (totals * math.sqrt(update_len * head_width))
    term_gate = jnp.einsum("htr,htd->rhd", grad_gate, key_rows, preferred_element_type=jnp.float32)
    term_up = jnp.einsum("htr,htd->rhd", grad_up, key_rows, preferred_element_type=jnp.float32)
    term_down = jnp.einsum("htr,htd->rhd", scaled, hidden_zero, preferred_element_type=jnp.float32)
    summed = lax.psum(
        jnp.stack((term_gate, term_up, term_down), axis=2) * inner[None, :, None, None], "seq"
    )
    fresh = renorm_rows(w_zero, summed, unit_scale)
    chosen = jnp.where(in_first, w_zero, fresh)
    query_gate = jnp.einsum(
        "htd,rhd->htr", query_rows, chosen[:, :, 0], preferred_element_type=jnp.float32
    )
    query_up = jnp.einsum(
        "htd,rhd->htr", query_rows, chosen[:, :, 1], preferred_element_type=jnp.float32
    )
    query_hidden = (query_gate * jax.nn.sigmoid(query_gate) * query_up).astype(jnp.bfloat16)
    fast_out = jnp.einsum(
        "htr,dhr->htd", query_hidden, chosen[:, :, 2], preferred_element_type=jnp.float32
    )
    mixed = (attended + fast_out).astype(jnp.bfloat16)
    frame_rows = tok_local // head_count
    head_index = lax.axis_index("head")
    flag_rows = lax.dynamic_slice_in_dim(speech_on, head_index * frame_rows, frame_rows, 0)
    cond_weight = w_cond.reshape(head_local, head_width, cond_width)
    projected = lax.psum_scatter(
        jnp.einsum("htd,hdc->tc", mixed, cond_weight, preferred_element_type=jnp.float32).astype(
            jnp.bfloat16
        ),
        "head",
        scatter_dimension=0,
        tiled=True,
    ).astype(jnp.float32)
    cond = (projected * flag_rows[:, None]).astype(jnp.bfloat16)[None]
    return (mixed, cond)


def solution(mesh):
    placed = (
        P("head", "seq", None),
        P("head", "seq", None),
        P("head", "seq", None),
        P("head", "seq"),
        P("seq"),
        P("seq"),
        P("head", None, None),
        P("head", None, None),
        P("head", None, None),
        P("head", None),
    )
    return jax.shard_map(
        local,
        mesh=mesh,
        in_specs=placed,
        out_specs=(P("head", "seq", None), P("seq", "head", None)),
        check_vma=False,
    )
```

profile of v0, /device:TPU:1, one launch (start us, length us, event | category | flops | bytes accessed | tf_op | source)
XLA Modules:
  0.0 385.9 jit_solution(10407356459944533290)
XLA Ops:
  7.2 0.0 all-reduce.2.cloned.1.call-start
  7.3 1.8 fusion.19
  9.1 0.5 fusion.21
  9.6 1.5 fusion.27
  11.1 1.7 convolution_bitcast_fusion.2
  12.9 1.7 convolution_bitcast_fusion.4
  14.6 1.5 convolution_bitcast_fusion.3
  16.1 0.6 reduce_sum.38
  17.4 124.3 %psum.14 = f32[1]{0:T(128)} all-reduce(f32[1]{0:T(128)} %bitcast.25), channel_id=1, replica_groups=mesh['head'=8,'seq'=64] {'seq'}, use_global_device_ids=true, to_apply=%region_3.4 | all-reduce | flops 1 | bytes 8 | tf_op jit(solution)/shard_map/psum | solution.py:92
  142.4 3.6 maximum_multiply_fusion
  145.9 0.0 all-reduce.2.cloned.1.call-update
  146.0 0.0 reduce-scatter.2.cloned.1.call-start
  146.0 1.3 collective-permute-start
  147.3 2.2 collective-permute-start.1
  149.5 4.0 %collective-permute-done = bf16[1,512,512]{2,1,0:T(8,128)(2,1)S(1)} collective-permute-done((bf16[1,512,512]{2,1,0:T(8,128)(2,1)S(1)}, bf16[1,512,512]{2,1,0:T(8,128)(2,1)S(1)}, u32[]{:S(2)}, u32[]{:S(2)}) %collective-permute-start) | collective-permute-done | bytes 524320 | tf_op jit(solution)/shard_map/ppermute | solution.py:17
  153.5 1.1 fusion.45
  154.5 1.3 copy-done.6
  155.9 0.4 fusion.2
  156.2 171.4 %all-reduce.2.cloned.1.call-done = f32[512,1,3,512]{3,0,2,1:T(8,128)} async-done(((f32[512,1,3,512]{3,0,2,1:T(8,128)}), f32[512,1,3,512]{3,0,2,1:T(8,128)}) %all-reduce.2.cloned.1.call-update) | async-done | bytes 3145744 | tf_op jit(solution)/shard_map/psum | solution.py:97
  327.6 2.7 fusion
  330.4 0.1 copy-done.1
  330.5 0.6 fusion.1
  331.1 1.1 copy-done.5
  332.3 1.5 convolution_bitcast_fusion.1
  333.7 3.4 fusion.6
  337.1 2.4 fusion.4
  339.5 0.8 copy-done.10
  340.3 1.2 convolution_convert_fusion
  341.5 0.0 reduce-scatter.2.cloned.1.call-update
  341.6 0.1 dynamic_slice.6
  341.6 35.9 %reduce-scatter.2.cloned.1.call-done = bf16[64,512]{1,0:T(8,128)(2,1)} async-done(((bf16[512,512]{1,0:T(8,128)(2,1)}), bf16[64,512]{1,0:T(8,128)(2,1)}) %reduce-scatter.2.cloned.1.call-update) | async-done | bytes 65552 | tf_op jit(solution)/shard_map/reduce_scatter | solution.py:117
  377.5 1.5 fusion.38
  (30 shorter events, 0.1 us)
Async XLA Ops:
  7.2 146.3 %copy-start = (bf16[1,512,512]{2,1,0:T(8,128)(2,1)S(1)}, bf16[1,512,512]{2,1,0:T(8,128)(2,1)}, u32[]{:S(2)}) copy-start(bf16[1,512,512]{2,1,0:T(8,128)(2,1)} %param.10) | copy-start | bytes 1572868
  7.2 1.9 copy-start.8
  7.2 1.9 copy-start.3
  7.2 320.4 %all-reduce.2.cloned.1.call-start = ((), (), s32[]{:S(2)}) async-start(), calls=%async_computation.1 | async-start | bytes 6291456 | tf_op jit(solution)/shard_map/psum | solution.py:97
  7.3 2.3 copy-start.11
  7.3 2.3 copy-start.12
  7.3 2.3 copy-start.2
  145.9 7.5 %copy-start.13 = (s32[512]{0:T(512)S(1)}, s32[512]{0:T(512)}, u32[]{:S(2)}) copy-start(s32[512]{0:T(512)} %param.14) | copy-start | bytes 6148
  146.0 231.6 %reduce-scatter.2.cloned.1.call-start = ((), (), s32[]{:S(2)}) async-start(), calls=%async_computation.2 | async-start | bytes 589824 | tf_op jit(solution)/shard_map/reduce_scatter | solution.py:117
  146.0 7.5 %collective-permute-start = (bf16[1,512,512]{2,1,0:T(8,128)(2,1)S(1)}, bf16[1,512,512]{2,1,0:T(8,128)(2,1)S(1)}, u32[]{:S(2)}, u32[]{:S(2)}) collective-permute-start(bf16[1,512,512]{2,1,0:T(8,128)(2,1)S(1)} %copy-done.8), channel_id=1, source_target_pairs={{0,1},{1,2},{2,3},{3,4},{4,5},{5,6},{6,7},{7,8},{8,9},{9,10},{10,1... | collective-permute-start | bytes 1572872 | tf_op jit(solution)/shard_map/ppermute | solution.py:17
  147.3 189.8 %collective-permute-start.1 = (bf16[1,512,512]{2,1,0:T(8,128)(2,1)}, bf16[1,512,512]{2,1,0:T(8,128)(2,1)}, u32[]{:S(2)}, u32[]{:S(2)}) collective-permute-start(bf16[1,512,512]{2,1,0:T(8,128)(2,1)} %param.12), channel_id=1, source_target_pairs={{0,1},{1,2},{2,3},{3,4},{4,5},{5,6},{6,7},{7,8},{8,9},{9,10},{10,1... | collective-permute-start | bytes 1572872 | tf_op jit(solution)/shard_map/ppermute | solution.py:17
  154.5 1.3 copy-start.6
  154.5 173.1 %copy-start.4 = (bf16[1,512,512]{2,1,0:T(8,128)(2,1)S(1)}, bf16[1,512,512]{2,1,0:T(8,128)(2,1)}, u32[]{:S(2)}) copy-start(bf16[1,512,512]{2,1,0:T(8,128)(2,1)} %param.16) | copy-start | bytes 1572868
  327.6 2.8 copy-start.1
  331.1 1.2 copy-start.5
  333.7 3.4 copy-start.7
  337.1 3.2 copy-start.9
  339.5 0.8 copy-start.10
Sparse Core Ops, SparseCore 0:
  146.1 181.4 all-reduce.1
  341.7 35.7 reduce-scatter.1
where the time goes:
time: 387 us; the launch traced here: 386 us
  waiting for transfers between devices  211 us (55%)
  blocking collectives  124 us (32%)
  matrix products  18.3 us (5%)
  between operations  15.6 us (4%)
  other arithmetic  9.47 us (2%)
    psum x1, waiting for transfers between devices, local(): lax.psum(jnp.stack((term_gate, term_up, term_down), axis=2) * inner[None,...  171 us
    psum x1, blocking collectives, local(): totals = lax.psum(rate_local, 'seq')  124 us
    reduce_scatter x1, waiting for transfers between devices, local(): lax.psum_scatter(jnp.einsum('htd,hdc->tc', mixed, cond_weight, preferred_...  35.9 us
  transfers between devices with their start and end apart: 4, of which 3 were waited for; matrix products, arithmetic and copies ran while one was open for 3% of the time, Pallas kernels for 0%

commit v1 on v0

v1 whole, which is shorter than its diff:
```python
import functools
import math
import jax
import jax.numpy as jnp
from jax import lax
from jax.experimental import pallas as pl
from jax.experimental.pallas import tpu as pltpu
from jax.sharding import PartitionSpec as P

F32 = jnp.float32
BF16 = jnp.bfloat16
NN = (((1,), (0,)), ((), ()))
NT = (((1,), (1,)), ((), ()))


def dot(a, b, dims):
    return lax.dot_general(a, b, dims, preferred_element_type=F32)


def grads_kernel(k_ref, v_ref, rate_ref, flag_ref, wg_ref, wu_ref, wd_ref, out_ref):
    key = k_ref[0]
    rate = rate_ref[...]
    coeff = flag_ref[...].astype(F32) * rate
    scaled = (coeff * v_ref[0].T.astype(F32)).astype(BF16)
    down = wd_ref[0].T
    step = 128
    part = step // 16

    def put(piece, which, start):
        for c in range(4):
            block = piece[:, c * 128 : (c + 1) * 128].reshape(part, 16, 128)
            row = which * 64 + c * 16
            out_ref[start // 16 : start // 16 + part, row : row + 16, :] = block

    hidden = []
    for start in range(0, 512, step):
        rows = slice(start, start + step)
        gate = dot(wg_ref[0, rows, :], key, NT)
        up = dot(wu_ref[0, rows, :], key, NT)
        back = dot(down[rows], scaled, NN)
        sigma = jax.nn.sigmoid(gate)
        active = gate * sigma
        hidden.append((active * up).astype(BF16))
        grad_gate = (back * up * sigma * (1.0 + gate * (1.0 - sigma))).astype(BF16)
        grad_up = (back * active).astype(BF16)
        put(dot(grad_gate, key, NN).astype(BF16), 0, start)
        put(dot(grad_up, key, NN).astype(BF16), 1, start)
    hidden = jnp.concatenate(hidden, axis=0)
    for start in range(0, 512, step):
        rows = slice(start, start + step)
        put(dot(scaled[rows], hidden, NT).astype(BF16), 2, start)
    total = jnp.sum(rate, axis=1, keepdims=True)
    high = total.astype(BF16)
    low = (total - high.astype(F32)).astype(BF16)
    row = lax.broadcasted_iota(jnp.int32, (8, 128), 0)
    tail = jnp.where(row == 0, high.astype(F32), jnp.where(row == 1, low.astype(F32), 0.0))
    out_ref[:, 192:200, :] = jnp.broadcast_to(tail.astype(BF16)[None], (32, 8, 128))


def grads(k, v, rate, flag, wg, wu, wd):
    return pl.pallas_call(
        grads_kernel,
        out_shape=jax.ShapeDtypeStruct((32, 200, 128), BF16),
        in_specs=[pl.BlockSpec(memory_space=pltpu.VMEM)] * 7,
        out_specs=pl.BlockSpec(memory_space=pltpu.VMEM),
        name="grads",
    )(k, v, rate, flag, wg, wu, wd)


def renorm_kernel(rank_ref, recv_ref, wg_ref, wu_ref, wd_ref, out_ref, *, update_len):
    head = recv_ref[:, 192:200, :].astype(F32)
    tail = jnp.sum(head, axis=0)
    total = tail[0:1, 0:1] + tail[1:2, 0:1]
    factor = 2.0 * update_len / (total * math.sqrt(update_len * 512))
    for which, ref in enumerate((wg_ref, wu_ref, wd_ref)):
        old = ref[0].astype(F32)
        pieces = []
        for c in range(4):
            row = which * 64 + c * 16
            pieces.append(jnp.sum(recv_ref[:, row : row + 16, :].astype(F32), axis=0))
        summed = jnp.concatenate(pieces, axis=1)
        updated = old + summed * factor
        old_norm = jnp.sqrt(jnp.sum(old * old, axis=-1, keepdims=True))
        new_norm = jnp.sqrt(jnp.sum(updated * updated, axis=-1, keepdims=True) + 1e-6)
        out_ref[which] = (updated * (old_norm / new_norm)).astype(BF16)


def renorm(rank, recv, wg, wu, wd, update_len):
    wspec = pl.BlockSpec((1, 16, 512), lambda i, r: (0, r[0], 0))
    return pl.pallas_call(
        functools.partial(renorm_kernel, update_len=update_len),
        out_shape=jax.ShapeDtypeStruct((3, 16, 512), BF16),
        grid_spec=pltpu.PrefetchScalarGridSpec(
            num_scalar_prefetch=1,
            grid=(1,),
            in_specs=[pl.BlockSpec((32, 200, 128), lambda i, r: (0, 0, 0)), wspec, wspec, wspec],
            out_specs=pl.BlockSpec((3, 16, 512), lambda i, r: (0, 0, 0)),
        ),
        name="renorm",
    )(rank, recv, wg, wu, wd)


def attend_kernel(pos_ref, q_ref, pk_ref, k_ref, pv_ref, v_ref, doc_ref, out_ref):
    base = pos_ref[0]
    step = 128
    scale = 1.0 / math.sqrt(512)
    doc = (jnp.broadcast_to(doc_ref[...], (8, 512)) - base).T[:, :1]
    for start in range(0, 512, step):
        rows = slice(start, start + step)
        q = q_ref[0, rows, :]
        keys = jnp.concatenate([pk_ref[0, start:, :], k_ref[0, : start + step, :]], axis=0)
        vals = jnp.concatenate([pv_ref[0, start:, :], v_ref[0, : start + step, :]], axis=0)
        width = 512 + step
        s = dot(q, keys, NT) * scale
        at = lax.broadcasted_iota(jnp.int32, (step, width), 0) + start
        to = lax.broadcasted_iota(jnp.int32, (step, width), 1) + (start - 512)
        ok = (to <= at) & (to > at - 512) & (to >= doc[rows])
        s = jnp.where(ok, s, -1e30)
        top = jnp.max(s, axis=-1, keepdims=True)
        e = jnp.exp(s - top)
        prob = (e / jnp.sum(e, axis=-1, keepdims=True)).astype(BF16)
        out_ref[rows, :] = dot(prob, vals, NN)


def attend(pos, q, pk, k, pv, v, doc):
    vm = pl.BlockSpec(memory_space=pltpu.VMEM)
    return pl.pallas_call(
        attend_kernel,
        out_shape=jax.ShapeDtypeStruct((512, 512), F32),
        in_specs=[pl.BlockSpec(memory_space=pltpu.SMEM)] + [vm] * 6,
        out_specs=vm,
        name="attend",
    )(pos, q, pk, k, pv, v, doc)


def apply_kernel(first_ref, q_ref, att_ref, wg0, wu0, wd0, fresh, wc_ref, mixed_ref, part_ref, w, sem):
    first = first_ref[0] == 1

    @pl.when(first)
    def _():
        for i, ref in enumerate((wg0, wu0, wd0)):
            pltpu.make_async_copy(ref, w.at[i], sem.at[i]).start()

    @pl.when(jnp.logical_not(first))
    def _():
        for i in range(3):
            pltpu.make_async_copy(fresh.at[:, i], w.at[i], sem.at[i]).start()

    for i in range(3):
        pltpu.make_async_copy(fresh.at[:, i], w.at[i], sem.at[i]).wait()
    step = 128
    for start in range(0, 512, step):
        rows = slice(start, start + step)
        q = q_ref[0, rows, :]
        gate = dot(q, w[0].reshape(512, 512), NT)
        up = dot(q, w[1].reshape(512, 512), NT)
        hidden = (gate * jax.nn.sigmoid(gate) * up).astype(BF16)
        mixed = (att_ref[rows, :] + dot(hidden, w[2].reshape(512, 512), NT)).astype(BF16)
        mixed_ref[0, rows, :] = mixed
        part_ref[rows, :] = dot(mixed, wc_ref[...], NN).astype(BF16)


def fast_apply(first, q, att, wg, wu, wd, fresh, wc):
    vm = pl.BlockSpec(memory_space=pltpu.VMEM)
    hb = pl.BlockSpec(memory_space=pl.ANY)
    return pl.pallas_call(
        apply_kernel,
        out_shape=(
            jax.ShapeDtypeStruct((1, 512, 512), BF16),
            jax.ShapeDtypeStruct((512, 512), BF16),
        ),
        in_specs=[pl.BlockSpec(memory_space=pltpu.SMEM), vm, vm, hb, hb, hb, hb, vm],
        out_specs=(vm, vm),
        scratch_shapes=[pltpu.VMEM((3, 32, 16, 512), BF16), pltpu.SemaphoreType.DMA((3,))],
        name="fast_apply",
    )(first, q, att, *(x.reshape(32, 16, 512) for x in (wg, wu, wd)), fresh, wc)


def combine_kernel(recv_ref, flag_ref, out_ref):
    summed = jnp.sum(recv_ref[...].astype(F32), axis=0)
    flag = jnp.broadcast_to(flag_ref[...].astype(F32), (8, 64)).T[:, :1]
    out_ref[0] = (summed * flag).astype(BF16)


def combine(recv, flag):
    vm = pl.BlockSpec(memory_space=pltpu.VMEM)
    return pl.pallas_call(
        combine_kernel,
        out_shape=jax.ShapeDtypeStruct((1, 64, 512), BF16),
        in_specs=[vm, vm],
        out_specs=vm,
        name="combine",
    )(recv, flag)


def local(q, k, v, rate, doc_start, flag, wg, wu, wd, wc):
    seq_count = lax.axis_size("seq")
    half = seq_count // 2
    index = lax.axis_index("seq")
    first = index < half
    rank = lax.rem(index, half)
    halves = [list(range(half)), list(range(half, seq_count))]
    route = [(i - 1, i) for i in range(1, seq_count)]
    pk = lax.ppermute(k, "seq", route)
    pv = lax.ppermute(v, "seq", route)
    terms = grads(k, v, rate, flag[None], wg, wu, wd)
    recv = lax.all_to_all(terms, "seq", 0, 0, axis_index_groups=halves)
    shard = renorm(rank[None].astype(jnp.int32), recv, wg, wu, wd, 512 * half)
    shard = lax.ppermute(shard, "seq", [(i, i + half) for i in range(half)])
    fresh = lax.all_gather(shard, "seq", axis=0, axis_index_groups=halves)
    att = attend((index * 512)[None].astype(jnp.int32), q, pk, k, pv, v, doc_start[None])
    mixed, part = fast_apply(first[None].astype(jnp.int32), q, att, wg, wu, wd, fresh, wc)
    got = lax.all_to_all(part.reshape(8, 64, 512), "head", 0, 0)
    flags = lax.dynamic_slice_in_dim(flag, lax.axis_index("head") * 64, 64, 0)
    return mixed, combine(got, flags[None])


def solution(mesh):
    placed = (
        P("head", "seq", None),
        P("head", "seq", None),
        P("head", "seq", None),
        P("head", "seq"),
        P("seq"),
        P("seq"),
        P("head", None, None),
        P("head", None, None),
        P("head", None, None),
        P("head", None),
    )
    return jax.shard_map(
        local,
        mesh=mesh,
        in_specs=placed,
        out_specs=(P("head", "seq", None), P("seq", "head", None)),
        check_vma=False,
    )
```

time: 387 us -> 270 us (0.70)
  blocking collectives: 124 us -> 0 us
  starting transfers between devices: 3.55 us -> 55.5 us
  waiting for transfers between devices: 211 us -> 172 us
  Pallas kernels: 0 us -> 22.9 us
  matrix products: 18.3 us -> 0 us
  other arithmetic: 9.47 us -> 0 us
    psum x1 -> x0, waiting for transfers between devices: 171 us -> none  [local(): lax.psum(jnp.stack((term_gate, term_up, term_down), axis=2) * inner[None,...]
    psum x1 -> x0, blocking collectives: 124 us -> none  [local(): totals = lax.psum(rate_local, 'seq')]
    all_gather x0 -> x1, waiting for transfers between devices: none -> 107 us  [local(): fresh = lax.all_gather(shard, 'seq', axis=0, axis_index_groups=halves)]
    all_to_all x0 -> x2, waiting for transfers between devices: none -> 47 us  [the longest x1 38.9 us: local(): recv = lax.all_to_all(terms, 'seq', 0, 0, axis_index_groups=halves)]
    all_to_all x0 -> x2, starting transfers between devices: none -> 39.9 us  [the longest x1 26.4 us: local(): got = lax.all_to_all(part.reshape(8, 64, 512), 'head', 0, 0)]
    reduce_scatter x1 -> x0, waiting for transfers between devices: 35.9 us -> none  [local(): lax.psum_scatter(jnp.einsum('htd,hdc->tc', mixed, cond_weight, preferred_...]
    pallas_call x0 -> x5, Pallas kernels: none -> 22.9 us  [the longest x1 6.72 us: fast_apply(): pl.pallas_call(apply_kernel, out_shape=(jax.ShapeDtypeStruct((1, 512, 512...]
    dot_general x11 -> x0, matrix products: 18.3 us -> none  [the longest x1 3.43 us: local(): jnp.einsum('htr,dhr->htd', query_hidden, chosen[:, :, 2], preferred_eleme...]
  transfers between devices with their start and end apart: 4 -> 6, of which waited for: 3 -> 6; matrix products, arithmetic and copies ran while one was open for 3% -> 0% of each run, Pallas kernels for 0% -> 2%
where the time goes in v1:
time: 270 us; the launch traced here: 269 us
  waiting for transfers between devices  172 us (64%)
  starting transfers between devices  55.5 us (21%)
  Pallas kernels  22.9 us (8%)
  between operations  14.1 us (5%)
  local copies, waits for them, and re-layouts  4.69 us (2%)
    all_gather x1, waiting for transfers between devices, local(): fresh = lax.all_gather(shard, 'seq', axis=0, axis_index_groups=halves)  107 us
    all_to_all x1, waiting for transfers between devices, local(): recv = lax.all_to_all(terms, 'seq', 0, 0, axis_index_groups=halves)  38.9 us
    all_to_all x1, starting transfers between devices, local(): got = lax.all_to_all(part.reshape(8, 64, 512), 'head', 0, 0)  26.4 us
    all_to_all x1, starting transfers between devices, local(): recv = lax.all_to_all(terms, 'seq', 0, 0, axis_index_groups=halves)  13.5 us
    ppermute x1, waiting for transfers between devices, local(): pv = lax.ppermute(v, 'seq', route)  11.8 us
    all_to_all x1, waiting for transfers between devices, local(): got = lax.all_to_all(part.reshape(8, 64, 512), 'head', 0, 0)  8.06 us
    ppermute x1, starting transfers between devices, local(): shard = lax.ppermute(shard, 'seq', [(i, i + half) for i in range(half)])  7.99 us
    pallas_call x1, Pallas kernels, fast_apply(): pl.pallas_call(apply_kernel, out_shape=(jax.ShapeDtypeStruct((1, 512, 512...  6.72 us
  transfers between devices with their start and end apart: 6, of which 6 were waited for; matrix products, arithmetic and copies ran while one was open for 0% of the time, Pallas kernels for 2%

profile of v1, /device:TPU:1, one launch (start us, length us, event | category | flops | bytes accessed | tf_op | source)
XLA Modules:
  0.0 269.5 jit_solution(17976054990118281359)
XLA Ops:
  7.2 6.5 %grads.1 = bf16[32,200,128]{2,1,0:T(8,128)(2,1)} custom-call(bf16[1,512,512]{2,1,0:T(8,128)(2,1)} %k_ref.3, bf16[1,512,512]{2,1,0:T(8,128)(2,1)} %v_ref.3, f32[1,512]{1,0:T(1,128)} %rate_ref.1, s32[1,512]{1,0:T(1,128)} %bitcast.18, bf16[1,512,512]{2,1,0:T(8,128)(2,1)} %wg_ref.3, bf16[1,512,512]{2,1,0:T(8,128)(2,1)} %wu_ref.3, bf16[1,512,512]{2,1,0:T(8,128)(2,1)} %wd_ref.3), custom_call_target="tpu_custom_call" | custom-call | tf_op jit(solution)/shard_map/grads/pallas_call | solution.py:61
  13.7 13.5 %all-to-all-start = ((bf16[32,200,128]{2,1,0:T(8,128)(2,1)}), bf16[32,200,128]{2,1,0:T(8,128)(2,1)S(1)}, u32[]{:S(2)}, u32[]{:S(2)}) async-start(bf16[32,200,128]{2,1,0:T(8,128)(2,1)} %grads.1), calls=%async_computation | async-start | bytes 3276800 | tf_op jit(solution)/shard_map/all_to_all | solution.py:207
  27.1 0.0 all-gather.3.cloned.1.call-start
  27.2 38.9 %all-to-all-done.recv_ref = bf16[32,200,128]{2,1,0:T(8,128)(2,1)S(1)} async-done(((bf16[32,200,128]{2,1,0:T(8,128)(2,1)}), bf16[32,200,128]{2,1,0:T(8,128)(2,1)S(1)}, u32[]{:S(2)}, u32[]{:S(2)}) %all-to-all-start) | async-done | bytes 1638432 | tf_op jit(solution)/shard_map/all_to_all | solution.py:207
  66.1 0.0 copy-start
  66.1 1.2 copy-done
  67.3 0.0 copy-start.1
  67.3 0.0 copy-start.2
  67.3 2.5 renorm.1
  69.8 8.0 %collective-permute-start.2 = (bf16[3,16,512]{2,1,0:T(8,128)(2,1)}, bf16[3,16,512]{2,1,0:T(8,128)(2,1)S(1)}, u32[]{:S(2)}, u32[]{:S(2)}) collective-permute-start(bf16[3,16,512]{2,1,0:T(8,128)(2,1)} %renorm.1), channel_id=1, source_target_pairs={{0,32},{1,33},{2,34},{3,35},{4,36},{5,37},{6,38},{7,39},{8,40},{9,... | collective-permute-start | bytes 147464 | tf_op jit(solution)/shard_map/ppermute | solution.py:209
  77.8 1.5 collective-permute-done.2
  79.3 0.0 copy-start.6
  79.3 0.6 copy-done.6
  79.9 0.0 all-gather.3.cloned.1.call-update
  79.9 0.0 copy-done.1
  79.9 4.0 %collective-permute-start = (bf16[1,512,512]{2,1,0:T(8,128)(2,1)S(1)}, bf16[1,512,512]{2,1,0:T(8,128)(2,1)S(1)}, u32[]{:S(2)}, u32[]{:S(2)}) collective-permute-start(bf16[1,512,512]{2,1,0:T(8,128)(2,1)S(1)} %copy-done.1), channel_id=1, source_target_pairs={{0,1},{1,2},{2,3},{3,4},{4,5},{5,6},{6,7},{7,8},{8,9},{9,10},{10,1... | collective-permute-start | bytes 1572872 | tf_op jit(solution)/shard_map/ppermute | solution.py:204
  84.0 0.0 copy-done.2
  84.0 3.5 %collective-permute-start.1 = (bf16[1,512,512]{2,1,0:T(8,128)(2,1)S(1)}, bf16[1,512,512]{2,1,0:T(8,128)(2,1)S(1)}, u32[]{:S(2)}, u32[]{:S(2)}) collective-permute-start(bf16[1,512,512]{2,1,0:T(8,128)(2,1)S(1)} %copy-done.2), channel_id=1, source_target_pairs={{0,1},{1,2},{2,3},{3,4},{4,5},{5,6},{6,7},{7,8},{8,9},{9,10},{10,1... | collective-permute-start | bytes 1572872 | tf_op jit(solution)/shard_map/ppermute | solution.py:205
  87.5 4.6 %collective-permute-done.pk_ref = bf16[1,512,512]{2,1,0:T(8,128)(2,1)S(1)} collective-permute-done((bf16[1,512,512]{2,1,0:T(8,128)(2,1)S(1)}, bf16[1,512,512]{2,1,0:T(8,128)(2,1)S(1)}, u32[]{:S(2)}, u32[]{:S(2)}) %collective-permute-start) | collective-permute-done | bytes 524320 | tf_op jit(solution)/shard_map/ppermute | solution.py:204
  92.1 0.0 copy-start.4
  92.1 11.8 %collective-permute-done.1.pv_ref = bf16[1,512,512]{2,1,0:T(8,128)(2,1)S(1)} collective-permute-done((bf16[1,512,512]{2,1,0:T(8,128)(2,1)S(1)}, bf16[1,512,512]{2,1,0:T(8,128)(2,1)S(1)}, u32[]{:S(2)}, u32[]{:S(2)}) %collective-permute-start.1) | collective-permute-done | bytes 524320 | tf_op jit(solution)/shard_map/ppermute | solution.py:205
  103.9 0.0 copy-start.5
  103.9 0.0 copy-done.4
  103.9 0.8 copy-done.5
  104.7 5.3 %attend.1.att_ref = f32[512,512]{1,0:T(8,128)} custom-call(s32[1]{0:T(128)} %bitcast.1.pos_ref, bf16[1,512,512]{2,1,0:T(8,128)(2,1)} %q_ref.3, bf16[1,512,512]{2,1,0:T(8,128)(2,1)} %copy-done.4, bf16[1,512,512]{2,1,0:T(8,128)(2,1)} %k_ref.3, bf16[1,512,512]{2,1,0:T(8,128)(2,1)} %copy-done.5, bf16[1,512,512]{2,1,0:T(8,128)(2,1)} %v_ref.3, s32[1,512]{1,0:T(1,128)} %bitcast.17), custom_call_target="tpu_custom_call" | custom-call | tf_op jit(solution)/shard_map/attend/pallas_call | solution.py:127
  110.0 107.5 %all-gather.3.cloned.1.call-done = bf16[96,16,512]{2,1,0:T(8,128)(2,1)} async-done(((bf16[3,16,512]{2,1,0:T(8,128)(2,1)}), bf16[96,16,512]{2,1,0:T(8,128)(2,1)}) %all-gather.3.cloned.1.call-update) | async-done | bytes 1572880 | tf_op jit(solution)/shard_map/all_gather | solution.py:210
  217.5 6.7 %fast_apply.1 = (bf16[1,512,512]{2,1,0:T(8,128)(2,1)}, bf16[512,512]{1,0:T(8,128)(2,1)}) custom-call(s32[1]{0:T(128)} %bitcast.first_ref, bf16[1,512,512]{2,1,0:T(8,128)(2,1)} %q_ref.3, f32[512,512]{1,0:T(8,128)} %attend.1.att_ref, bf16[32,16,512]{2,1,0:T(8,128)(2,1)} %bitcast.12, bf16[32,16,512]{2,1,0:T(8,128)(2,1)} %bitcast.13, ...), custom_call_target="tpu_custom_call" | custom-call | tf_op jit(solution)/shard_map/fast_apply/pallas_call | solution.py:166
  224.2 26.4 %all-to-all-start.1 = ((bf16[8,64,512]{2,1,0:T(8,128)(2,1)}), bf16[8,64,512]{2,1,0:T(8,128)(2,1)S(1)}, u32[]{:S(2)}, u32[]{:S(2)}) async-start(bf16[8,64,512]{2,1,0:T(8,128)(2,1)} %bitcast.16), calls=%async_computation.1 | async-start | bytes 1048576 | tf_op jit(solution)/shard_map/all_to_all | solution.py:213
  250.7 1.3 dynamic-slice_bitcast_fusion.flag_ref
  252.0 8.1 %all-to-all-done.1.recv_ref = bf16[8,64,512]{2,1,0:T(8,128)(2,1)S(1)} async-done(((bf16[8,64,512]{2,1,0:T(8,128)(2,1)}), bf16[8,64,512]{2,1,0:T(8,128)(2,1)S(1)}, u32[]{:S(2)}, u32[]{:S(2)}) %all-to-all-start.1) | async-done | bytes 524320 | tf_op jit(solution)/shard_map/all_to_all | solution.py:213
  260.0 0.8 copy-done.3
  260.8 1.8 combine.1
  (1 shorter events, 0.0 us)
Async XLA Ops:
  13.7 52.4 %all-to-all-start = ((bf16[32,200,128]{2,1,0:T(8,128)(2,1)}), bf16[32,200,128]{2,1,0:T(8,128)(2,1)S(1)}, u32[]{:S(2)}, u32[]{:S(2)}) async-start(bf16[32,200,128]{2,1,0:T(8,128)(2,1)} %grads.1), calls=%async_computation | async-start | bytes 3276800 | tf_op jit(solution)/shard_map/all_to_all | solution.py:207
  27.1 190.4 %all-gather.3.cloned.1.call-start = ((), (), s32[]{:S(2)}) async-start(), calls=%async_computation.2 | async-start | bytes 1622016 | tf_op jit(solution)/shard_map/all_gather | solution.py:210
  66.1 1.2 copy-start
  67.3 12.6 %copy-start.1 = (bf16[1,512,512]{2,1,0:T(8,128)(2,1)S(1)}, bf16[1,512,512]{2,1,0:T(8,128)(2,1)}, u32[]{:S(2)}) copy-start(bf16[1,512,512]{2,1,0:T(8,128)(2,1)} %k_ref.3) | copy-start | bytes 1572868
  67.3 16.7 %copy-start.2 = (bf16[1,512,512]{2,1,0:T(8,128)(2,1)S(1)}, bf16[1,512,512]{2,1,0:T(8,128)(2,1)}, u32[]{:S(2)}) copy-start(bf16[1,512,512]{2,1,0:T(8,128)(2,1)} %v_ref.3) | copy-start | bytes 1572868
  69.8 9.5 %collective-permute-start.2 = (bf16[3,16,512]{2,1,0:T(8,128)(2,1)}, bf16[3,16,512]{2,1,0:T(8,128)(2,1)S(1)}, u32[]{:S(2)}, u32[]{:S(2)}) collective-permute-start(bf16[3,16,512]{2,1,0:T(8,128)(2,1)} %renorm.1), channel_id=1, source_target_pairs={{0,32},{1,33},{2,34},{3,35},{4,36},{5,37},{6,38},{7,39},{8,40},{9,... | collective-permute-start | bytes 147464 | tf_op jit(solution)/shard_map/ppermute | solution.py:209
  79.3 0.6 copy-start.6
  79.9 12.2 %collective-permute-start = (bf16[1,512,512]{2,1,0:T(8,128)(2,1)S(1)}, bf16[1,512,512]{2,1,0:T(8,128)(2,1)S(1)}, u32[]{:S(2)}, u32[]{:S(2)}) collective-permute-start(bf16[1,512,512]{2,1,0:T(8,128)(2,1)S(1)} %copy-done.1), channel_id=1, source_target_pairs={{0,1},{1,2},{2,3},{3,4},{4,5},{5,6},{6,7},{7,8},{8,9},{9,10},{10,1... | collective-permute-start | bytes 1572872 | tf_op jit(solution)/shard_map/ppermute | solution.py:204
  84.0 19.9 %collective-permute-start.1 = (bf16[1,512,512]{2,1,0:T(8,128)(2,1)S(1)}, bf16[1,512,512]{2,1,0:T(8,128)(2,1)S(1)}, u32[]{:S(2)}, u32[]{:S(2)}) collective-permute-start(bf16[1,512,512]{2,1,0:T(8,128)(2,1)S(1)} %copy-done.2), channel_id=1, source_target_pairs={{0,1},{1,2},{2,3},{3,4},{4,5},{5,6},{6,7},{7,8},{8,9},{9,10},{10,1... | collective-permute-start | bytes 1572872 | tf_op jit(solution)/shard_map/ppermute | solution.py:205
  92.1 11.8 %copy-start.4 = (bf16[1,512,512]{2,1,0:T(8,128)(2,1)}, bf16[1,512,512]{2,1,0:T(8,128)(2,1)S(1)}, u32[]{:S(2)}) copy-start(bf16[1,512,512]{2,1,0:T(8,128)(2,1)S(1)} %collective-permute-done.pk_ref) | copy-start | bytes 1572868
  103.9 0.8 copy-start.5
  224.2 35.8 %all-to-all-start.1 = ((bf16[8,64,512]{2,1,0:T(8,128)(2,1)}), bf16[8,64,512]{2,1,0:T(8,128)(2,1)S(1)}, u32[]{:S(2)}, u32[]{:S(2)}) async-start(bf16[8,64,512]{2,1,0:T(8,128)(2,1)} %bitcast.16), calls=%async_computation.1 | async-start | bytes 1048576 | tf_op jit(solution)/shard_map/all_to_all | solution.py:213
  260.0 0.8 copy-start.3
Sparse Core Ops, SparseCore 0:
  80.0 137.4 all-gather.2

commit v2 on v1

v2 whole, which is shorter than its diff:
```python
import functools
import math
import jax
import jax.numpy as jnp
from jax import lax
from jax.experimental import pallas as pl
from jax.experimental.pallas import tpu as pltpu
from jax.sharding import PartitionSpec as P


F32 = jnp.float32
GRADS_STEP = 256
APPLY_STEP = 256
BF16 = jnp.bfloat16
NN = (((1,), (0,)), ((), ()))
NT = (((1,), (1,)), ((), ()))


def dot(a, b, dims):
    return lax.dot_general(a, b, dims, preferred_element_type=F32)


def grads_kernel(
    k_hbm, v_hbm, wg_hbm, wu_hbm, wd_hbm, rate_ref, flag_ref, out_hbm,
    k_s, v_s, wg_s, wu_s, wd_s, out_s, sem_in, sem_out,
):
    loads = [
        pltpu.make_async_copy(src.at[0], dst, sem_in.at[i])
        for i, (src, dst) in enumerate(
            ((v_hbm, v_s), (wd_hbm, wd_s), (k_hbm, k_s), (wg_hbm, wg_s), (wu_hbm, wu_s))
        )
    ]
    for load in loads:
        load.start()
    step = GRADS_STEP
    part = step // 16
    stores = []

    def put(piece, which, start):
        for c in range(4):
            block = piece[:, c * 128 : (c + 1) * 128].reshape(part, 16, 128)
            row = which * 64 + c * 16
            out_s[start // 16 : start // 16 + part, row : row + 16, :] = block

    def ship(low, high, start, rows):
        window = (slice(start // 16, (start + rows) // 16), slice(low, high))
        store = pltpu.make_async_copy(out_s.at[window], out_hbm.at[window], sem_out.at[len(stores)])
        store.start()
        stores.append(store)

    rate = rate_ref[...]
    coeff = flag_ref[...].astype(F32) * rate
    total = jnp.sum(rate, axis=1, keepdims=True)
    high = total.astype(BF16)
    low = (total - high.astype(F32)).astype(BF16)
    row = lax.broadcasted_iota(jnp.int32, (8, 128), 0)
    tail = jnp.where(row == 0, high.astype(F32), jnp.where(row == 1, low.astype(F32), 0.0))
    out_s[:, 192:200, :] = jnp.broadcast_to(tail.astype(BF16)[None], (32, 8, 128))
    loads[0].wait()
    scaled = (coeff * v_s[...].T.astype(F32)).astype(BF16)
    loads[1].wait()
    down = wd_s[...].T
    for load in loads[2:]:
        load.wait()
    key = k_s[...]
    hidden = []
    for start in range(0, 512, step):
        rows = slice(start, start + step)
        gate = dot(wg_s[rows, :], key, NT)
        up = dot(wu_s[rows, :], key, NT)
        back = dot(down[rows], scaled, NN)
        sigma = jax.nn.sigmoid(gate)
        active = gate * sigma
        hidden.append((active * up).astype(BF16))
        grad_gate = (back * up * sigma * (1.0 + gate * (1.0 - sigma))).astype(BF16)
        grad_up = (back * active).astype(BF16)
        put(dot(grad_gate, key, NN).astype(BF16), 0, start)
        put(dot(grad_up, key, NN).astype(BF16), 1, start)
        ship(0, 128, start, step)
    hidden = jnp.concatenate(hidden, axis=0)
    for start in range(0, 512, step):
        rows = slice(start, start + step)
        put(dot(scaled[rows], hidden, NT).astype(BF16), 2, start)
        ship(128, 200, start, step)
    for store in stores:
        store.wait()


def grads(k, v, rate, flag, wg, wu, wd):
    vm = pl.BlockSpec(memory_space=pltpu.VMEM)
    hb = pl.BlockSpec(memory_space=pltpu.HBM)
    return pl.pallas_call(
        grads_kernel,
        out_shape=jax.ShapeDtypeStruct((32, 200, 128), BF16),
        in_specs=[hb] * 5 + [vm, vm],
        out_specs=hb,
        scratch_shapes=[pltpu.VMEM((512, 512), BF16)] * 5
        + [
            pltpu.VMEM((32, 200, 128), BF16),
            pltpu.SemaphoreType.DMA((5,)),
            pltpu.SemaphoreType.DMA((2 * (512 // GRADS_STEP),)),
        ],
        name="grads",
    )(k, v, wg, wu, wd, rate, flag)


def renorm_kernel(
    rank_ref, recv_ref, wg, wu, wd, out, old_s, new_s, sem_in, sem_out, *, update_len
):
    rows = pl.ds(pl.multiple_of(rank_ref[0] * 16, 16), 16)
    loads = [
        pltpu.make_async_copy(ref.at[0, rows], old_s.at[i], sem_in.at[i])
        for i, ref in enumerate((wg, wu, wd))
    ]
    for load in loads:
        load.start()
    tail = jnp.sum(recv_ref[:, 192:200, :].astype(F32), axis=0)
    total = tail[0:1, 0:1] + tail[1:2, 0:1]
    factor = 2.0 * update_len / (total * math.sqrt(update_len * 512))
    for which in range(3):
        pieces = []
        for c in range(4):
            row = which * 64 + c * 16
            pieces.append(jnp.sum(recv_ref[:, row : row + 16, :].astype(F32), axis=0))
        summed = jnp.concatenate(pieces, axis=1)
        loads[which].wait()
        old = old_s[which].astype(F32)
        updated = old + summed * factor
        old_norm = jnp.sqrt(jnp.sum(old * old, axis=-1, keepdims=True))
        new_norm = jnp.sqrt(jnp.sum(updated * updated, axis=-1, keepdims=True) + 1e-6)
        new_s[which] = (updated * (old_norm / new_norm)).astype(BF16)
    stores = [pltpu.make_async_copy(new_s, out.at[d], sem_out.at[d]) for d in range(8)]
    for store in stores:
        store.start()
    for store in stores:
        store.wait()


def renorm(rank, recv, wg, wu, wd, update_len):
    hb = pl.BlockSpec(memory_space=pltpu.HBM)
    return pl.pallas_call(
        functools.partial(renorm_kernel, update_len=update_len),
        out_shape=jax.ShapeDtypeStruct((8, 3, 16, 512), BF16),
        in_specs=[
            pl.BlockSpec(memory_space=pltpu.SMEM),
            pl.BlockSpec(memory_space=pltpu.VMEM),
            hb,
            hb,
            hb,
        ],
        out_specs=hb,
        scratch_shapes=[
            pltpu.VMEM((3, 16, 512), BF16),
            pltpu.VMEM((3, 16, 512), BF16),
            pltpu.SemaphoreType.DMA((3,)),
            pltpu.SemaphoreType.DMA((8,)),
        ],
        compiler_params=pltpu.CompilerParams(vmem_limit_bytes=8 << 20),
        name="renorm",
    )(rank, recv, wg, wu, wd)


def attend_kernel(
    pos_ref, doc_ref, q_hbm, k_hbm, v_hbm, wc_hbm, pk1, pv1, pk2, pv2, out_ref, q_ref, wc_ref,
    k_ref, v_ref, pk_ref, pv_ref, sem,
):
    base = pos_ref[0]
    first = pos_ref[1] == 1
    loads = [
        pltpu.make_async_copy(src, dst, sem.at[i + 2])
        for i, (src, dst) in enumerate(
            ((q_hbm, q_ref), (k_hbm, k_ref), (v_hbm, v_ref), (wc_hbm, wc_ref))
        )
    ]
    for load in loads:
        load.start()

    @pl.when(first)
    def _():
        pltpu.make_async_copy(pk1, pk_ref, sem.at[0]).start()
        pltpu.make_async_copy(pv1, pv_ref, sem.at[1]).start()

    @pl.when(jnp.logical_not(first))
    def _():
        pltpu.make_async_copy(pk2, pk_ref, sem.at[0]).start()
        pltpu.make_async_copy(pv2, pv_ref, sem.at[1]).start()

    pltpu.make_async_copy(pk1, pk_ref, sem.at[0]).wait()
    pltpu.make_async_copy(pv1, pv_ref, sem.at[1]).wait()
    for load in loads:
        load.wait()
    step = 128
    scale = 1.0 / math.sqrt(512)
    doc = (jnp.broadcast_to(doc_ref[...], (8, 512)) - base).T[:, :1]
    for start in range(0, 512, step):
        rows = slice(start, start + step)
        q = q_ref[0, rows, :]
        keys = jnp.concatenate([pk_ref[0, start:, :], k_ref[0, : start + step, :]], axis=0)
        vals = jnp.concatenate([pv_ref[0, start:, :], v_ref[0, : start + step, :]], axis=0)
        width = 512 + step
        s = dot(q, keys, NT) * scale
        at = lax.broadcasted_iota(jnp.int32, (step, width), 0) + start
        to = lax.broadcasted_iota(jnp.int32, (step, width), 1) + (start - 512)
        ok = (to <= at) & (to > at - 512) & (to >= doc[rows])
        s = jnp.where(ok, s, -1e30)
        top = jnp.max(s, axis=-1, keepdims=True)
        e = jnp.exp(s - top)
        prob = (e / jnp.sum(e, axis=-1, keepdims=True)).astype(BF16)
        out_ref[rows, :] = dot(prob, vals, NN)


def attend(pos, q, k, v, doc, wc, pk1, pv1, pk2, pv2):
    vm = pl.BlockSpec(memory_space=pltpu.VMEM)
    hb = pl.BlockSpec(memory_space=pltpu.HBM)
    return pl.pallas_call(
        attend_kernel,
        out_shape=(
            jax.ShapeDtypeStruct((512, 512), F32),
            jax.ShapeDtypeStruct((1, 512, 512), BF16),
            jax.ShapeDtypeStruct((512, 512), BF16),
        ),
        in_specs=[pl.BlockSpec(memory_space=pltpu.SMEM), vm] + [hb] * 8,
        out_specs=(vm, vm, vm),
        scratch_shapes=[pltpu.VMEM((1, 512, 512), BF16)] * 4 + [pltpu.SemaphoreType.DMA((6,))],
        compiler_params=pltpu.CompilerParams(vmem_limit_bytes=20 << 20),
        name="attend",
    )(pos, doc, q, k, v, wc, pk1, pv1, pk2, pv2)


def relay_kernel(pos_ref, recv, wg, wu, wd, out, own, sem_in, sem_out):
    first = pos_ref[0] == 1
    column = pos_ref[1]

    @pl.when(first)
    def _():
        copies = []
        for i, ref in enumerate((wg, wu, wd)):
            for z in range(4):
                rows = pl.ds(pl.multiple_of((z * 8 + column) * 16, 16), 16)
                copies.append(pltpu.make_async_copy(ref.at[0, rows], own.at[z, i], sem_in.at[i, z]))
        for copy in copies:
            copy.start()
        for copy in copies:
            copy.wait()
        copies = [pltpu.make_async_copy(own, out.at[d], sem_out.at[d]) for d in range(8)]
        for copy in copies:
            copy.start()
        for copy in copies:
            copy.wait()

    @pl.when(jnp.logical_not(first))
    def _():
        copies = [
            pltpu.make_async_copy(recv.at[pl.ds(0, 4)], out.at[d], sem_out.at[d]) for d in range(8)
        ]
        for copy in copies:
            copy.start()
        for copy in copies:
            copy.wait()


def relay(pos, recv, wg, wu, wd):
    hb = pl.BlockSpec(memory_space=pltpu.HBM)
    return pl.pallas_call(
        relay_kernel,
        out_shape=jax.ShapeDtypeStruct((8, 4, 3, 16, 512), BF16),
        in_specs=[
            pl.BlockSpec(memory_space=pltpu.SMEM),
            pl.BlockSpec(memory_space=pltpu.VMEM),
            hb,
            hb,
            hb,
        ],
        out_specs=hb,
        scratch_shapes=[
            pltpu.VMEM((4, 3, 16, 512), BF16),
            pltpu.SemaphoreType.DMA((3, 4)),
            pltpu.SemaphoreType.DMA((8,)),
        ],
        compiler_params=pltpu.CompilerParams(vmem_limit_bytes=4 << 20),
        name="relay",
    )(pos, recv, wg, wu, wd)


def apply_kernel(
    fresh, att_s, q_s, wc_s, mixed_hbm, part_hbm, mixed_s, part_s, sem_out
):

    def weight(i, low, count):
        return jnp.concatenate(
            [fresh[y, z, i] for z in range(low // 128, (low + count) // 128) for y in range(8)], axis=0
        )

    step = APPLY_STEP
    q = q_s[0]
    hidden = []
    for start in range(0, 512, step):
        gate = dot(q, weight(0, start, step), NT)
        up = dot(q, weight(1, start, step), NT)
        hidden.append((gate * jax.nn.sigmoid(gate) * up).astype(BF16))
    hidden = jnp.concatenate(hidden, axis=1)
    for start in range(0, 512, step):
        cols = slice(start, start + step)
        mixed_s[:, cols] = (att_s[:, cols] + dot(hidden, weight(2, start, step), NT)).astype(BF16)
    stores = [pltpu.make_async_copy(mixed_s, mixed_hbm.at[0], sem_out.at[0])]
    stores[0].start()
    mixed = mixed_s[...]
    for start in range(0, 512, step):
        cols = slice(start, start + step)
        part_s[:, cols] = dot(mixed, wc_s[:, cols], NN).astype(BF16)
    stores.append(pltpu.make_async_copy(part_s, part_hbm, sem_out.at[1]))
    stores[1].start()
    for store in stores:
        store.wait()


def fast_apply(fresh, q, att, wc):
    vm = pl.BlockSpec(memory_space=pltpu.VMEM)
    hb = pl.BlockSpec(memory_space=pltpu.HBM)
    return pl.pallas_call(
        apply_kernel,
        out_shape=(
            jax.ShapeDtypeStruct((1, 512, 512), BF16),
            jax.ShapeDtypeStruct((512, 512), BF16),
        ),
        in_specs=[vm] * 4,
        out_specs=(hb, hb),
        scratch_shapes=[
            pltpu.VMEM((512, 512), BF16),
            pltpu.VMEM((512, 512), BF16),
            pltpu.SemaphoreType.DMA((2,)),
        ],
        compiler_params=pltpu.CompilerParams(vmem_limit_bytes=24 << 20),
        name="fast_apply",
    )(fresh, att, q, wc)


def combine_kernel(recv_ref, flag_ref, out_ref):
    summed = jnp.sum(recv_ref[...].astype(F32), axis=0)
    flag = jnp.broadcast_to(flag_ref[...].astype(F32), (8, 64)).T[:, :1]
    out_ref[0] = (summed * flag).astype(BF16)


def combine(recv, flag):
    vm = pl.BlockSpec(memory_space=pltpu.VMEM)
    return pl.pallas_call(
        combine_kernel,
        out_shape=jax.ShapeDtypeStruct((1, 64, 512), BF16),
        in_specs=[vm, vm],
        out_specs=vm,
        compiler_params=pltpu.CompilerParams(vmem_limit_bytes=4 << 20),
        name="combine",
    )(recv, flag)


def layer(q, k, v, rate, doc_start, flag, wg, wu, wd, wc):
    seq_count = lax.axis_size("seq")
    half = seq_count // 2
    index = lax.axis_index("seq")
    first = (index < half).astype(jnp.int32)
    rank = lax.rem(index, half)
    halves = [list(range(half)), list(range(half, seq_count))]
    ygroups = [[z * 8 + y for y in range(8)] for z in range(8)]
    zgroups = [[z * 8 + y for z in range(8)] for y in range(8)]
    early = [(i - 1, i) for i in range(half, seq_count)]
    late = [(i - 1, i) for i in range(1, half)]

    pk2 = lax.ppermute(k, "seq", early)
    pv2 = lax.ppermute(v, "seq", early)
    terms = grads(k, v, rate, flag[None], wg, wu, wd)
    recv = lax.all_to_all(terms, "seq", 0, 0, axis_index_groups=halves)
    shard = renorm(rank[None].astype(jnp.int32), recv, wg, wu, wd, 512 * half)
    pk1 = lax.ppermute(k, "seq", late)
    pv1 = lax.ppermute(v, "seq", late)
    column = lax.all_to_all(shard, "seq", 0, 0, axis_index_groups=zgroups)
    spot = jnp.stack([first, lax.rem(index, 8).astype(jnp.int32)])
    column = relay(spot, column, wg, wu, wd)
    fresh = lax.all_to_all(column, "seq", 0, 0, axis_index_groups=ygroups)
    pos = jnp.stack([index.astype(jnp.int32) * 512, first])
    att, q_near, wc_near = attend(pos, q, k, v, doc_start[None], wc, pk1, pv1, pk2, pv2)
    mixed, part = fast_apply(fresh, q_near, att, wc_near)
    got = lax.all_to_all(part.reshape(8, 64, 512), "head", 0, 0)
    flags = lax.dynamic_slice_in_dim(flag, lax.axis_index("head") * 64, 64, 0)
    return mixed, combine(got, flags[None])


def solution(mesh):
    placed = (
        P("head", "seq", None),
        P("head", "seq", None),
        P("head", "seq", None),
        P("head", "seq"),
        P("seq"),
        P("seq"),
        P("head", None, None),
        P("head", None, None),
        P("head", None, None),
        P("head", None),
    )
    return jax.shard_map(
        layer,
        mesh=mesh,
        in_specs=placed,
        out_specs=(P("head", "seq", None), P("seq", "head", None)),
        check_vma=False,
    )
```

time: 270 us -> 180 us (0.67)
  waiting for transfers between devices: 172 us -> 102 us
  between operations: 14.1 us -> 0.78 us
  starting transfers between devices: 55.5 us -> 48.5 us
  Pallas kernels: 22.9 us -> 16.1 us
  local copies, waits for them, and re-layouts: 4.69 us -> 9.48 us
    all_gather x1 -> x0, waiting for transfers between devices: 107 us -> none  [local(): fresh = lax.all_gather(shard, 'seq', axis=0, axis_index_groups=halves)]
    ppermute x3 -> x4, waiting for transfers between devices: 17.8 us -> 43.5 us  [the longest x1 33.1 us: layer(): pk1 = lax.ppermute(k, 'seq', late)]
    all_to_all x2 -> x4, waiting for transfers between devices: 47 us -> 58.8 us  [the longest x1 38.9 us: layer(): recv = lax.all_to_all(terms, 'seq', 0, 0, axis_index_groups=halves)]
    ppermute x3 -> x4, starting transfers between devices: 15.5 us -> 10.2 us  [the longest x1 3.84 us: layer(): pv1 = lax.ppermute(v, 'seq', late)]
    unnamed x14 -> x30, local copies, waits for them, and re-layouts: 3.41 us -> 8.73 us
    pallas_call x1, Pallas kernels: 6.72 us -> 2.12 us  [fast_apply(): pl.pallas_call(apply_kernel, out_shape=(jax.ShapeDtypeStruct((1, 512, 512...]
    all_to_all x2 -> x4, starting transfers between devices: 39.9 us -> 38.4 us  [the longest x1 13.6 us: layer(): recv = lax.all_to_all(terms, 'seq', 0, 0, axis_index_groups=halves)]
    pallas_call x1 -> x2, Pallas kernels: 5.33 us -> 6.67 us  [the longest x1 4.49 us: attend(): pl.pallas_call(attend_kernel, out_shape=(jax.ShapeDtypeStruct((512, 512),...]
  transfers between devices with their start and end apart: 6 -> 8, of which waited for: 6 -> 5; matrix products, arithmetic and copies ran while one was open for 0% -> 1% of each run, Pallas kernels for 2% -> 3%
where the time goes in v2:
time: 180 us; the launch traced here: 177 us
  waiting for transfers between devices  102 us (57%)
  starting transfers between devices  48.5 us (27%)
  Pallas kernels  16.1 us (9%)
  local copies, waits for them, and re-layouts  9.48 us (5%)
    all_to_all x1, waiting for transfers between devices, layer(): recv = lax.all_to_all(terms, 'seq', 0, 0, axis_index_groups=halves)  38.9 us
    ppermute x1, waiting for transfers between devices, layer(): pk1 = lax.ppermute(k, 'seq', late)  33.1 us
    all_to_all x1, starting transfers between devices, layer(): recv = lax.all_to_all(terms, 'seq', 0, 0, axis_index_groups=halves)  13.6 us
    all_to_all x1, waiting for transfers between devices, layer(): column = lax.all_to_all(shard, 'seq', 0, 0, axis_index_groups=zgroups)  11.3 us
    ppermute x1, waiting for transfers between devices, layer(): pv1 = lax.ppermute(v, 'seq', late)  10.4 us
    all_to_all x1, starting transfers between devices, layer(): fresh = lax.all_to_all(column, 'seq', 0, 0, axis_index_groups=ygroups)  10.3 us
    unnamed x30, local copies, waits for them, and re-layouts  8.73 us
    all_to_all x1, waiting for transfers between devices, layer(): got = lax.all_to_all(part.reshape(8, 64, 512), 'head', 0, 0)  8.6 us
  transfers between devices with their start and end apart: 8, of which 5 were waited for; matrix products, arithmetic and copies ran while one was open for 1% of the time, Pallas kernels for 3%

profile of v2, /device:TPU:1, one launch (start us, length us, event | category | flops | bytes accessed | tf_op | source)
XLA Modules:
  0.0 177.3 jit_solution(14885765576758917559)
XLA Ops:
  0.6 5.4 %grads.1 = bf16[32,200,128]{2,1,0:T(8,128)(2,1)} custom-call(bf16[1,512,512]{2,1,0:T(8,128)(2,1)} %k_hbm.3, bf16[1,512,512]{2,1,0:T(8,128)(2,1)} %v_hbm.3, bf16[1,512,512]{2,1,0:T(8,128)(2,1)} %wg.3, bf16[1,512,512]{2,1,0:T(8,128)(2,1)} %wu.3, bf16[1,512,512]{2,1,0:T(8,128)(2,1)} %wd.3, f32[1,512]{1,0:T(1,128)} %rate_ref.1, s32[1,512]{1,0:T(1,128)} %bitcast.10), custom_call_target="tpu_custom_call" | custom-call | tf_op jit(solution)/shard_map/grads/pallas_call | solution.py:92
  6.1 0.0 copy-start.1
  6.1 13.6 %all-to-all-start = ((bf16[32,200,128]{2,1,0:T(8,128)(2,1)}), bf16[32,200,128]{2,1,0:T(8,128)(2,1)S(1)}, u32[]{:S(2)}, u32[]{:S(2)}) async-start(bf16[32,200,128]{2,1,0:T(8,128)(2,1)} %grads.1), calls=%async_computation | async-start | bytes 3276800 | tf_op jit(solution)/shard_map/all_to_all | solution.py:371
  19.7 38.9 %all-to-all-done.recv_ref = bf16[32,200,128]{2,1,0:T(8,128)(2,1)S(1)} async-done(((bf16[32,200,128]{2,1,0:T(8,128)(2,1)}), bf16[32,200,128]{2,1,0:T(8,128)(2,1)S(1)}, u32[]{:S(2)}, u32[]{:S(2)}) %all-to-all-start) | async-done | bytes 1638432 | tf_op jit(solution)/shard_map/all_to_all | solution.py:371
  58.6 1.1 renorm.1
  59.7 0.7 copy-done.5
  60.5 7.3 %all-to-all-start.1 = ((bf16[8,3,16,512]{3,2,1,0:T(8,128)(2,1)}), bf16[8,3,16,512]{3,2,1,0:T(8,128)(2,1)S(1)}, u32[]{:S(2)}, u32[]{:S(2)}) async-start(bf16[8,3,16,512]{3,2,1,0:T(8,128)(2,1)} %copy-done.5), calls=%async_computation.1 | async-start | bytes 786432 | tf_op jit(solution)/shard_map/all_to_all | solution.py:375
  67.8 0.1 pad_add_fusion.pos_ref
  67.9 11.3 %all-to-all-done.1.recv = bf16[8,3,16,512]{3,2,1,0:T(8,128)(2,1)S(1)} async-done(((bf16[8,3,16,512]{3,2,1,0:T(8,128)(2,1)}), bf16[8,3,16,512]{3,2,1,0:T(8,128)(2,1)S(1)}, u32[]{:S(2)}, u32[]{:S(2)}) %all-to-all-start.1) | async-done | bytes 393248 | tf_op jit(solution)/shard_map/all_to_all | solution.py:375
  79.1 2.2 %relay.1 = bf16[8,4,3,16,512]{4,3,2,1,0:T(8,128)(2,1)} custom-call(s32[2]{0:T(128)S(1)} %pad_add_fusion.pos_ref, bf16[8,3,16,512]{3,2,1,0:T(8,128)(2,1)S(1)} %all-to-all-done.1.recv, bf16[1,512,512]{2,1,0:T(8,128)(2,1)S(1)} %copy-done, bf16[1,512,512]{2,1,0:T(8,128)(2,1)S(1)} %copy-done.1, bf16[1,512,512]{2,1,0:T(8,128)(2,1)S(1)} %copy-done.2), custom_call_target="tpu_custom_call" | custom-call | tf_op jit(solution)/shard_map/relay/pallas_call | solution.py:264
  81.4 10.3 %all-to-all-start.2 = ((bf16[8,4,3,16,512]{4,3,2,1,0:T(8,128)(2,1)}), bf16[8,4,3,16,512]{4,3,2,1,0:T(8,128)(2,1)S(1)}, u32[]{:S(2)}, u32[]{:S(2)}) async-start(bf16[8,4,3,16,512]{4,3,2,1,0:T(8,128)(2,1)} %relay.1), calls=%async_computation.2 | async-start | bytes 3145728 | tf_op jit(solution)/shard_map/all_to_all | solution.py:378
  91.7 3.4 %collective-permute-start = (bf16[1,512,512]{2,1,0:T(8,128)(2,1)S(1)}, bf16[1,512,512]{2,1,0:T(8,128)(2,1)S(1)}, u32[]{:S(2)}, u32[]{:S(2)}) collective-permute-start(bf16[1,512,512]{2,1,0:T(8,128)(2,1)S(1)} %copy-done.3), channel_id=1, source_target_pairs={{0,1},{1,2},{2,3},{3,4},{4,5},{5,6},{6,7},{7,8},{8,9},{9,10},{10,1... | collective-permute-start | bytes 1572872 | tf_op jit(solution)/shard_map/ppermute | solution.py:373
  95.1 1.5 collective-permute-start.2
  96.6 3.8 %collective-permute-start.1 = (bf16[1,512,512]{2,1,0:T(8,128)(2,1)S(1)}, bf16[1,512,512]{2,1,0:T(8,128)(2,1)}, u32[]{:S(2)}, u32[]{:S(2)}) collective-permute-start(bf16[1,512,512]{2,1,0:T(8,128)(2,1)S(1)} %copy-done.4), channel_id=1, source_target_pairs={{0,1},{1,2},{2,3},{3,4},{4,5},{5,6},{6,7},{7,8},{8,9},{9,10},{10,1... | collective-permute-start | bytes 1572872 | tf_op jit(solution)/shard_map/ppermute | solution.py:374
  100.4 1.5 collective-permute-start.3
  101.9 0.1 pad_add_fusion.1.pos_ref
  102.0 33.1 %collective-permute-done.pk1 = bf16[1,512,512]{2,1,0:T(8,128)(2,1)S(1)} collective-permute-done((bf16[1,512,512]{2,1,0:T(8,128)(2,1)S(1)}, bf16[1,512,512]{2,1,0:T(8,128)(2,1)S(1)}, u32[]{:S(2)}, u32[]{:S(2)}) %collective-permute-start) | collective-permute-done | bytes 524320 | tf_op jit(solution)/shard_map/ppermute | solution.py:373
  135.0 0.8 copy-done.12
  135.8 10.4 %collective-permute-done.1.pv1 = bf16[1,512,512]{2,1,0:T(8,128)(2,1)} collective-permute-done((bf16[1,512,512]{2,1,0:T(8,128)(2,1)S(1)}, bf16[1,512,512]{2,1,0:T(8,128)(2,1)}, u32[]{:S(2)}, u32[]{:S(2)}) %collective-permute-start.1) | collective-permute-done | bytes 524320 | tf_op jit(solution)/shard_map/ppermute | solution.py:374
  146.3 1.0 copy-done.10
  147.3 1.0 copy-done.11
  148.4 1.0 copy-done.13
  149.4 4.5 %attend.1 = (f32[512,512]{1,0:T(8,128)S(1)}, bf16[1,512,512]{2,1,0:T(8,128)(2,1)S(1)}, bf16[512,512]{1,0:T(8,128)(2,1)S(1)}) custom-call(s32[2]{0:T(128)S(1)} %pad_add_fusion.1.pos_ref, s32[1,512]{1,0:T(1,128)S(1)} %bitcast.9, bf16[1,512,512]{2,1,0:T(8,128)(2,1)S(1)} %copy-done.10, bf16[1,512,512]{2,1,0:T(8,128)(2,1)S(1)} %copy-done.3, ...), custom_call_target="tpu_custom_call" | custom-call | tf_op jit(solution)/shard_map/attend/pallas_call | solution.py:215
  153.9 1.0 copy-done.6
  154.9 0.8 copy-done.8
  155.7 1.2 copy-done.7
  156.9 1.0 copy-done.9
  157.9 2.1 %fast_apply.1 = (bf16[1,512,512]{2,1,0:T(8,128)(2,1)}, bf16[512,512]{1,0:T(8,128)(2,1)}) custom-call(bf16[8,4,3,16,512]{4,3,2,1,0:T(8,128)(2,1)S(1)} %all-to-all-done.2.fresh, f32[512,512]{1,0:T(8,128)S(1)} %copy-done.7, bf16[1,512,512]{2,1,0:T(8,128)(2,1)S(1)} %get-tuple-element.8.q_s, bf16[512,512]{1,0:T(8,128)(2,1)S(1)} %copy-done.9), custom_call_target="tpu_custom_call" | custom-call | tf_op jit(solution)/shard_map/fast_apply/pallas_call | solution.py:320
  160.1 7.1 %all-to-all-start.3 = ((bf16[8,64,512]{2,1,0:T(8,128)(2,1)}), bf16[8,64,512]{2,1,0:T(8,128)(2,1)S(1)}, u32[]{:S(2)}, u32[]{:S(2)}) async-start(bf16[8,64,512]{2,1,0:T(8,128)(2,1)} %bitcast.6), calls=%async_computation.3 | async-start | bytes 1048576 | tf_op jit(solution)/shard_map/all_to_all | solution.py:382
  167.2 0.8 dynamic-slice_bitcast_fusion.flag_ref
  168.0 8.6 %all-to-all-done.3.recv_ref = bf16[8,64,512]{2,1,0:T(8,128)(2,1)S(1)} async-done(((bf16[8,64,512]{2,1,0:T(8,128)(2,1)}), bf16[8,64,512]{2,1,0:T(8,128)(2,1)S(1)}, u32[]{:S(2)}, u32[]{:S(2)}) %all-to-all-start.3) | async-done | bytes 524320 | tf_op jit(solution)/shard_map/all_to_all | solution.py:382
  176.6 0.8 combine.1
  (23 shorter events, 0.1 us)
Async XLA Ops:
  6.0 52.6 %copy-start = (bf16[1,512,512]{2,1,0:T(8,128)(2,1)S(1)}, bf16[1,512,512]{2,1,0:T(8,128)(2,1)}, u32[]{:S(2)}) copy-start(bf16[1,512,512]{2,1,0:T(8,128)(2,1)} %wg.3) | copy-start | bytes 1572868
  6.1 52.6 %copy-start.1 = (bf16[1,512,512]{2,1,0:T(8,128)(2,1)S(1)}, bf16[1,512,512]{2,1,0:T(8,128)(2,1)}, u32[]{:S(2)}) copy-start(bf16[1,512,512]{2,1,0:T(8,128)(2,1)} %wu.3) | copy-start | bytes 1572868
  6.1 52.6 %copy-start.2 = (bf16[1,512,512]{2,1,0:T(8,128)(2,1)S(1)}, bf16[1,512,512]{2,1,0:T(8,128)(2,1)}, u32[]{:S(2)}) copy-start(bf16[1,512,512]{2,1,0:T(8,128)(2,1)} %wd.3) | copy-start | bytes 1572868
  6.1 52.5 %all-to-all-start = ((bf16[32,200,128]{2,1,0:T(8,128)(2,1)}), bf16[32,200,128]{2,1,0:T(8,128)(2,1)S(1)}, u32[]{:S(2)}, u32[]{:S(2)}) async-start(bf16[32,200,128]{2,1,0:T(8,128)(2,1)} %grads.1), calls=%async_computation | async-start | bytes 3276800 | tf_op jit(solution)/shard_map/all_to_all | solution.py:371
  59.7 0.7 copy-start.5
  60.5 18.7 %all-to-all-start.1 = ((bf16[8,3,16,512]{3,2,1,0:T(8,128)(2,1)}), bf16[8,3,16,512]{3,2,1,0:T(8,128)(2,1)S(1)}, u32[]{:S(2)}, u32[]{:S(2)}) async-start(bf16[8,3,16,512]{3,2,1,0:T(8,128)(2,1)} %copy-done.5), calls=%async_computation.1 | async-start | bytes 786432 | tf_op jit(solution)/shard_map/all_to_all | solution.py:375
  81.3 10.4 %copy-start.3 = (bf16[1,512,512]{2,1,0:T(8,128)(2,1)S(1)}, bf16[1,512,512]{2,1,0:T(8,128)(2,1)}, u32[]{:S(2)}) copy-start(bf16[1,512,512]{2,1,0:T(8,128)(2,1)} %k_hbm.3) | copy-start | bytes 1572868
  81.3 15.2 %copy-start.4 = (bf16[1,512,512]{2,1,0:T(8,128)(2,1)S(1)}, bf16[1,512,512]{2,1,0:T(8,128)(2,1)}, u32[]{:S(2)}) copy-start(bf16[1,512,512]{2,1,0:T(8,128)(2,1)} %v_hbm.3) | copy-start | bytes 1572868
  81.3 64.9 %copy-start.14 = (s32[512]{0:T(512)S(1)}, s32[512]{0:T(512)}, u32[]{:S(2)}) copy-start(s32[512]{0:T(512)} %param.14) | copy-start | bytes 6148
  81.4 74.3 %all-to-all-start.2 = ((bf16[8,4,3,16,512]{4,3,2,1,0:T(8,128)(2,1)}), bf16[8,4,3,16,512]{4,3,2,1,0:T(8,128)(2,1)S(1)}, u32[]{:S(2)}, u32[]{:S(2)}) async-start(bf16[8,4,3,16,512]{4,3,2,1,0:T(8,128)(2,1)} %relay.1), calls=%async_computation.2 | async-start | bytes 3145728 | tf_op jit(solution)/shard_map/all_to_all | solution.py:378
  91.7 43.3 %collective-permute-start = (bf16[1,512,512]{2,1,0:T(8,128)(2,1)S(1)}, bf16[1,512,512]{2,1,0:T(8,128)(2,1)S(1)}, u32[]{:S(2)}, u32[]{:S(2)}) collective-permute-start(bf16[1,512,512]{2,1,0:T(8,128)(2,1)S(1)} %copy-done.3), channel_id=1, source_target_pairs={{0,1},{1,2},{2,3},{3,4},{4,5},{5,6},{6,7},{7,8},{8,9},{9,10},{10,1... | collective-permute-start | bytes 1572872 | tf_op jit(solution)/shard_map/ppermute | solution.py:373
  95.1 40.7 %collective-permute-start.2 = (bf16[1,512,512]{2,1,0:T(8,128)(2,1)S(1)}, bf16[1,512,512]{2,1,0:T(8,128)(2,1)}, u32[]{:S(2)}, u32[]{:S(2)}) collective-permute-start(bf16[1,512,512]{2,1,0:T(8,128)(2,1)S(1)} %copy-done.3), channel_id=1, source_target_pairs={{31,32},{32,33},{33,34},{34,35},{35,36},{36,37},{37,38},{38,39},{3... | collective-permute-start | bytes 1572872 | tf_op jit(solution)/shard_map/ppermute | solution.py:368
  96.6 49.7 %collective-permute-start.1 = (bf16[1,512,512]{2,1,0:T(8,128)(2,1)S(1)}, bf16[1,512,512]{2,1,0:T(8,128)(2,1)}, u32[]{:S(2)}, u32[]{:S(2)}) collective-permute-start(bf16[1,512,512]{2,1,0:T(8,128)(2,1)S(1)} %copy-done.4), channel_id=1, source_target_pairs={{0,1},{1,2},{2,3},{3,4},{4,5},{5,6},{6,7},{7,8},{8,9},{9,10},{10,1... | collective-permute-start | bytes 1572872 | tf_op jit(solution)/shard_map/ppermute | solution.py:374
  100.4 45.9 %collective-permute-start.3 = (bf16[1,512,512]{2,1,0:T(8,128)(2,1)S(1)}, bf16[1,512,512]{2,1,0:T(8,128)(2,1)}, u32[]{:S(2)}, u32[]{:S(2)}) collective-permute-start(bf16[1,512,512]{2,1,0:T(8,128)(2,1)S(1)} %copy-done.4), channel_id=1, source_target_pairs={{31,32},{32,33},{33,34},{34,35},{35,36},{36,37},{37,38},{38,39},{3... | collective-permute-start | bytes 1572872 | tf_op jit(solution)/shard_map/ppermute | solution.py:369
  135.0 0.8 copy-start.12
  146.3 1.0 copy-start.10
  147.3 1.0 copy-start.11
  148.4 1.0 copy-start.13
  153.9 1.0 copy-start.6
  154.9 0.8 copy-start.8
  155.7 1.2 copy-start.7
  156.9 1.0 copy-start.9
  160.1 16.5 %all-to-all-start.3 = ((bf16[8,64,512]{2,1,0:T(8,128)(2,1)}), bf16[8,64,512]{2,1,0:T(8,128)(2,1)S(1)}, u32[]{:S(2)}, u32[]{:S(2)}) async-start(bf16[8,64,512]{2,1,0:T(8,128)(2,1)} %bitcast.6), calls=%async_computation.3 | async-start | bytes 1048576 | tf_op jit(solution)/shard_map/all_to_all | solution.py:382

commit v3 on v2

--- a/solution.py
+++ b/solution.py
@@ -11,6 +11,9 @@
 F32 = jnp.float32
 GRADS_STEP = 256
 APPLY_STEP = 256
+RENORM_VMEM = 51200 << 10
+RELAY_VMEM = 54800 << 10
+APPLY_VMEM = 50800 << 10
 BF16 = jnp.bfloat16
 NN = (((1,), (0,)), ((), ()))
 NT = (((1,), (1,)), ((), ()))
@@ -21,8 +24,8 @@
 
 
 def grads_kernel(
-    k_hbm, v_hbm, wg_hbm, wu_hbm, wd_hbm, rate_ref, flag_ref, out_hbm,
-    k_s, v_s, wg_s, wu_s, wd_s, out_s, sem_in, sem_out,
+    k_hbm, v_hbm, wg_hbm, wu_hbm, wd_hbm, rate_ref, flag_ref, out_hbm, kv_hbm,
+    k_s, v_s, wg_s, wu_s, wd_s, out_s, sem_in, sem_out, sem_kv,
 ):
     loads = [
         pltpu.make_async_copy(src.at[0], dst, sem_in.at[i])
@@ -62,6 +65,11 @@
     down = wd_s[...].T
     for load in loads[2:]:
         load.wait()
+    pair = [
+        pltpu.make_async_copy(src, kv_hbm.at[i], sem_kv.at[i]) for i, src in enumerate((k_s, v_s))
+    ]
+    for copy in pair:
+        copy.start()
     key = k_s[...]
     hidden = []
     for start in range(0, 512, step):
@@ -82,7 +90,7 @@
         rows = slice(start, start + step)
         put(dot(scaled[rows], hidden, NT).astype(BF16), 2, start)
         ship(128, 200, start, step)
-    for store in stores:
+    for store in stores + pair:
         store.wait()
 
 
@@ -91,14 +99,18 @@
     hb = pl.BlockSpec(memory_space=pltpu.HBM)
     return pl.pallas_call(
         grads_kernel,
-        out_shape=jax.ShapeDtypeStruct((32, 200, 128), BF16),
+        out_shape=(
+            jax.ShapeDtypeStruct((32, 200, 128), BF16),
+            jax.ShapeDtypeStruct((2, 512, 512), BF16),
+        ),
         in_specs=[hb] * 5 + [vm, vm],
-        out_specs=hb,
+        out_specs=(hb, hb),
         scratch_shapes=[pltpu.VMEM((512, 512), BF16)] * 5
         + [
             pltpu.VMEM((32, 200, 128), BF16),
             pltpu.SemaphoreType.DMA((5,)),
             pltpu.SemaphoreType.DMA((2 * (512 // GRADS_STEP),)),
+            pltpu.SemaphoreType.DMA((2,)),
         ],
         name="grads",
     )(k, v, wg, wu, wd, rate, flag)
@@ -155,38 +167,24 @@
             pltpu.SemaphoreType.DMA((3,)),
             pltpu.SemaphoreType.DMA((8,)),
         ],
-        compiler_params=pltpu.CompilerParams(vmem_limit_bytes=8 << 20),
+        compiler_params=pltpu.CompilerParams(vmem_limit_bytes=RENORM_VMEM),
         name="renorm",
     )(rank, recv, wg, wu, wd)
 
 
 def attend_kernel(
-    pos_ref, doc_ref, q_hbm, k_hbm, v_hbm, wc_hbm, pk1, pv1, pk2, pv2, out_ref, q_ref, wc_ref,
-    k_ref, v_ref, pk_ref, pv_ref, sem,
+    pos_ref, doc_ref, q_hbm, k_hbm, v_hbm, prev_hbm, out_hbm, q_ref, k_ref, v_ref, prev, att_s, sem
 ):
-    base = pos_ref[0]
-    first = pos_ref[1] == 1
+    base = pos_ref[2]
     loads = [
-        pltpu.make_async_copy(src, dst, sem.at[i + 2])
-        for i, (src, dst) in enumerate(
-            ((q_hbm, q_ref), (k_hbm, k_ref), (v_hbm, v_ref), (wc_hbm, wc_ref))
-        )
+        pltpu.make_async_copy(src.at[0], dst, sem.at[i])
+        for i, (src, dst) in enumerate(((q_hbm, q_ref), (k_hbm, k_ref), (v_hbm, v_ref)))
     ]
     for load in loads:
         load.start()
 
-    @pl.when(first)
-    def _():
-        pltpu.make_async_copy(pk1, pk_ref, sem.at[0]).start()
-        pltpu.make_async_copy(pv1, pv_ref, sem.at[1]).start()
-
-    @pl.when(jnp.logical_not(first))
-    def _():
-        pltpu.make_async_copy(pk2, pk_ref, sem.at[0]).start()
-        pltpu.make_async_copy(pv2, pv_ref, sem.at[1]).start()
-
-    pltpu.make_async_copy(pk1, pk_ref, sem.at[0]).wait()
-    pltpu.make_async_copy(pv1, pv_ref, sem.at[1]).wait()
+    loads.append(pltpu.make_async_copy(prev_hbm, prev, sem.at[3]))
+    loads[3].start()
     for load in loads:
         load.wait()
     step = 128
@@ -194,9 +192,9 @@
     doc = (jnp.broadcast_to(doc_ref[...], (8, 512)) - base).T[:, :1]
     for start in range(0, 512, step):
         rows = slice(start, start + step)
-        q = q_ref[0, rows, :]
-        keys = jnp.concatenate([pk_ref[0, start:, :], k_ref[0, : start + step, :]], axis=0)
-        vals = jnp.concatenate([pv_ref[0, start:, :], v_ref[0, : start + step, :]], axis=0)
+        q = q_ref[rows, :]
+        keys = jnp.concatenate([prev[0, start:, :], k_ref[: start + step, :]], axis=0)
+        vals = jnp.concatenate([prev[1, start:, :], v_ref[: start + step, :]], axis=0)
         width = 512 + step
         s = dot(q, keys, NT) * scale
         at = lax.broadcasted_iota(jnp.int32, (step, width), 0) + start
@@ -206,104 +204,107 @@
         top = jnp.max(s, axis=-1, keepdims=True)
         e = jnp.exp(s - top)
         prob = (e / jnp.sum(e, axis=-1, keepdims=True)).astype(BF16)
-        out_ref[rows, :] = dot(prob, vals, NN)
-
-
-def attend(pos, q, k, v, doc, wc, pk1, pv1, pk2, pv2):
+        att_s[rows, :] = dot(prob, vals, NN)
+    store = pltpu.make_async_copy(att_s, out_hbm.at[0], sem.at[4])
+    store.start()
+    store.wait()
+
+
+def attend(pos, q, k, v, doc, prev):
     vm = pl.BlockSpec(memory_space=pltpu.VMEM)
     hb = pl.BlockSpec(memory_space=pltpu.HBM)
     return pl.pallas_call(
         attend_kernel,
-        out_shape=(
-            jax.ShapeDtypeStruct((512, 512), F32),
-            jax.ShapeDtypeStruct((1, 512, 512), BF16),
-            jax.ShapeDtypeStruct((512, 512), BF16),
-        ),
-        in_specs=[pl.BlockSpec(memory_space=pltpu.SMEM), vm] + [hb] * 8,
-        out_specs=(vm, vm, vm),
-        scratch_shapes=[pltpu.VMEM((1, 512, 512), BF16)] * 4 + [pltpu.SemaphoreType.DMA((6,))],
-        compiler_params=pltpu.CompilerParams(vmem_limit_bytes=20 << 20),
+        out_shape=jax.ShapeDtypeStruct((2, 512, 512), F32),
+        in_specs=[pl.BlockSpec(memory_space=pltpu.SMEM), vm] + [hb] * 4,
+        out_specs=hb,
+        scratch_shapes=[pltpu.VMEM((512, 512), BF16)] * 3
+        + [
+            pltpu.VMEM((2, 512, 512), BF16),
+            pltpu.VMEM((512, 512), F32),
+            pltpu.SemaphoreType.DMA((5,)),
+        ],
         name="attend",
-    )(pos, doc, q, k, v, wc, pk1, pv1, pk2, pv2)
-
-
-def relay_kernel(pos_ref, recv, wg, wu, wd, out, own, sem_in, sem_out):
-    first = pos_ref[0] == 1
-    column = pos_ref[1]
-
-    @pl.when(first)
-    def _():
-        copies = []
-        for i, ref in enumerate((wg, wu, wd)):
-            for z in range(4):
-                rows = pl.ds(pl.multiple_of((z * 8 + column) * 16, 16), 16)
-                copies.append(pltpu.make_async_copy(ref.at[0, rows], own.at[z, i], sem_in.at[i, z]))
+    )(pos, doc, q, k, v, prev)
+
+
+def relay_kernel(spot_ref, recv, wg, wu, wd, out, own, sem_in, sem_out):
+    first = spot_ref[0] == 1
+    column = spot_ref[1]
+
+    def send(source):
+        copies = [pltpu.make_async_copy(source, out.at[d], sem_out.at[d]) for d in range(8)]
         for copy in copies:
             copy.start()
         for copy in copies:
             copy.wait()
-        copies = [pltpu.make_async_copy(own, out.at[d], sem_out.at[d]) for d in range(8)]
-        for copy in copies:
-            copy.start()
-        for copy in copies:
-            copy.wait()
-
-    @pl.when(jnp.logical_not(first))
+
+    @pl.when(first)
     def _():
         copies = [
-            pltpu.make_async_copy(recv.at[pl.ds(0, 4)], out.at[d], sem_out.at[d]) for d in range(8)
+            pltpu.make_async_copy(ref.at[:, column], own.at[:, i], sem_in.at[i])
+            for i, ref in enumerate((wg, wu, wd))
         ]
         for copy in copies:
             copy.start()
         for copy in copies:
             copy.wait()
-
-
-def relay(pos, recv, wg, wu, wd):
+        send(own)
+
+    @pl.when(jnp.logical_not(first))
+    def _():
+        send(recv.at[pl.ds(0, 4)])
+
+
+def relay(spot, recv, wg, wu, wd):
+    vm = pl.BlockSpec(memory_space=pltpu.VMEM)
     hb = pl.BlockSpec(memory_space=pltpu.HBM)
     return pl.pallas_call(
         relay_kernel,
         out_shape=jax.ShapeDtypeStruct((8, 4, 3, 16, 512), BF16),
-        in_specs=[
-            pl.BlockSpec(memory_space=pltpu.SMEM),
-            pl.BlockSpec(memory_space=pltpu.VMEM),
-            hb,
-            hb,
-            hb,
-        ],
+        in_specs=[pl.BlockSpec(memory_space=pltpu.SMEM), vm, hb, hb, hb],
         out_specs=hb,
         scratch_shapes=[
             pltpu.VMEM((4, 3, 16, 512), BF16),
-            pltpu.SemaphoreType.DMA((3, 4)),
+            pltpu.SemaphoreType.DMA((3,)),
             pltpu.SemaphoreType.DMA((8,)),
         ],
-        compiler_params=pltpu.CompilerParams(vmem_limit_bytes=4 << 20),
+        compiler_params=pltpu.CompilerParams(vmem_limit_bytes=RELAY_VMEM),
         name="relay",
-    )(pos, recv, wg, wu, wd)
+    )(spot, recv, *(x.reshape(4, 8, 16, 512) for x in (wg, wu, wd)))
 
 
 def apply_kernel(
-    fresh, att_s, q_s, wc_s, mixed_hbm, part_hbm, mixed_s, part_s, sem_out
+    fresh, q_hbm, att_hbm, wc_hbm, mixed_hbm, part_hbm,
+    q_s, att_s, wc_s, mixed_s, part_s, sem_in, sem_out,
 ):
+    loads = [
+        pltpu.make_async_copy(src, dst, sem_in.at[i])
+        for i, (src, dst) in enumerate(((q_hbm.at[0], q_s), (att_hbm.at[0], att_s), (wc_hbm, wc_s)))
+    ]
+    for load in loads:
+        load.start()
 
     def weight(i, low, count):
-        return jnp.concatenate(
-            [fresh[y, z, i] for z in range(low // 128, (low + count) // 128) for y in range(8)], axis=0
-        )
+        spots = [(z, y) for z in range(low // 128, (low + count) // 128) for y in range(8)]
+        return jnp.concatenate([fresh[y, z, i] for z, y in spots], axis=0)
 
     step = APPLY_STEP
-    q = q_s[0]
+    loads[0].wait()
+    q = q_s[...]
     hidden = []
     for start in range(0, 512, step):
         gate = dot(q, weight(0, start, step), NT)
         up = dot(q, weight(1, start, step), NT)
         hidden.append((gate * jax.nn.sigmoid(gate) * up).astype(BF16))
     hidden = jnp.concatenate(hidden, axis=1)
+    loads[1].wait()
     for start in range(0, 512, step):
         cols = slice(start, start + step)
         mixed_s[:, cols] = (att_s[:, cols] + dot(hidden, weight(2, start, step), NT)).astype(BF16)
     stores = [pltpu.make_async_copy(mixed_s, mixed_hbm.at[0], sem_out.at[0])]
     stores[0].start()
+    loads[2].wait()
     mixed = mixed_s[...]
     for start in range(0, 512, step):
         cols = slice(start, start + step)
@@ -323,16 +324,20 @@
             jax.ShapeDtypeStruct((1, 512, 512), BF16),
             jax.ShapeDtypeStruct((512, 512), BF16),
         ),
-        in_specs=[vm] * 4,
+        in_specs=[vm, hb, hb, hb],
         out_specs=(hb, hb),
         scratch_shapes=[
             pltpu.VMEM((512, 512), BF16),
+            pltpu.VMEM((512, 512), F32),
             pltpu.VMEM((512, 512), BF16),
+            pltpu.VMEM((512, 512), BF16),
+            pltpu.VMEM((512, 512), BF16),
+            pltpu.SemaphoreType.DMA((3,)),
             pltpu.SemaphoreType.DMA((2,)),
         ],
-        compiler_params=pltpu.CompilerParams(vmem_limit_bytes=24 << 20),
+        compiler_params=pltpu.CompilerParams(vmem_limit_bytes=APPLY_VMEM),
         name="fast_apply",
-    )(fresh, att, q, wc)
+    )(fresh, q, att, wc)
 
 
 def combine_kernel(recv_ref, flag_ref, out_ref):
@@ -353,35 +358,45 @@
     )(recv, flag)
 
 
+def mark_kernel(x_ref, out_ref):
+    out_ref[...] = x_ref[...]
+
+
+def mark(x):
+    vm = pl.BlockSpec(memory_space=pltpu.VMEM)
+    return pl.pallas_call(
+        mark_kernel,
+        out_shape=jax.ShapeDtypeStruct(x.shape, x.dtype),
+        in_specs=[vm],
+        out_specs=vm,
+    )(x)
+
+
 def layer(q, k, v, rate, doc_start, flag, wg, wu, wd, wc):
     seq_count = lax.axis_size("seq")
     half = seq_count // 2
-    index = lax.axis_index("seq")
+    index = lax.axis_index("seq").astype(jnp.int32)
     first = (index < half).astype(jnp.int32)
     rank = lax.rem(index, half)
     halves = [list(range(half)), list(range(half, seq_count))]
-    ygroups = [[z * 8 + y for y in range(8)] for z in range(8)]
-    zgroups = [[z * 8 + y for z in range(8)] for y in range(8)]
-    early = [(i - 1, i) for i in range(half, seq_count)]
-    late = [(i - 1, i) for i in range(1, half)]
-
-    pk2 = lax.ppermute(k, "seq", early)
-    pv2 = lax.ppermute(v, "seq", early)
-    terms = grads(k, v, rate, flag[None], wg, wu, wd)
+    columns = [[z * 8 + y for z in range(8)] for y in range(8)]
+    rows = [[z * 8 + y for y in range(8)] for z in range(8)]
+    route = [(i - 1, i) for i in range(1, seq_count)]
+
+    flags = lax.dynamic_slice_in_dim(flag, lax.axis_index("head") * 64, 64, 0)[None]
+    flags = mark(flags)
+    spot = jnp.stack([first, lax.rem(index, 8), index * 512])
+    terms, kv = grads(k, v, rate, flag[None], wg, wu, wd)
     recv = lax.all_to_all(terms, "seq", 0, 0, axis_index_groups=halves)
-    shard = renorm(rank[None].astype(jnp.int32), recv, wg, wu, wd, 512 * half)
-    pk1 = lax.ppermute(k, "seq", late)
-    pv1 = lax.ppermute(v, "seq", late)
-    column = lax.all_to_all(shard, "seq", 0, 0, axis_index_groups=zgroups)
-    spot = jnp.stack([first, lax.rem(index, 8).astype(jnp.int32)])
-    column = relay(spot, column, wg, wu, wd)
-    fresh = lax.all_to_all(column, "seq", 0, 0, axis_index_groups=ygroups)
-    pos = jnp.stack([index.astype(jnp.int32) * 512, first])
-    att, q_near, wc_near = attend(pos, q, k, v, doc_start[None], wc, pk1, pv1, pk2, pv2)
-    mixed, part = fast_apply(fresh, q_near, att, wc_near)
+    prev = lax.ppermute(kv, "seq", route)
+    shard = renorm(rank[None], recv, wg, wu, wd, 512 * half)
+    shard = lax.all_to_all(shard, "seq", 0, 0, axis_index_groups=columns)
+    shard = relay(spot, shard, wg, wu, wd)
+    fresh = lax.all_to_all(shard, "seq", 0, 0, axis_index_groups=rows)
+    att = attend(spot, q, k, v, doc_start[None], prev)
+    mixed, part = fast_apply(fresh, q, att, wc)
     got = lax.all_to_all(part.reshape(8, 64, 512), "head", 0, 0)
-    flags = lax.dynamic_slice_in_dim(flag, lax.axis_index("head") * 64, 64, 0)
-    return mixed, combine(got, flags[None])
+    return mixed, combine(got, flags)
 
 
 def solution(mesh):

time: 180 us -> 177 us (0.983)
  starting transfers between devices: 48.5 us -> 41.8 us
  waiting for transfers between devices: 102 us -> 108 us
  local copies, waits for them, and re-layouts: 9.48 us -> 3.61 us
  Pallas kernels: 16.1 us -> 20.3 us
    ppermute x4 -> x1, waiting for transfers between devices: 43.5 us -> 51.1 us  [layer(): prev = lax.ppermute(kv, 'seq', route)]
    ppermute x4 -> x1, starting transfers between devices: 10.2 us -> 3.42 us  [layer(): prev = lax.ppermute(kv, 'seq', route)]
    unnamed x30 -> x20, local copies, waits for them, and re-layouts: 8.73 us -> 2.35 us
    pallas_call x2 -> x3, Pallas kernels: 9.89 us -> 12.8 us  [the longest x1 6.19 us: attend(): pl.pallas_call(attend_kernel, out_shape=jax.ShapeDtypeStruct((2, 512, 512...]
  transfers between devices with their start and end apart: 8 -> 5, of which waited for: 5 -> 4; matrix products, arithmetic and copies ran while one was open for 1% -> 1% of each run, Pallas kernels for 3% -> 4%
where the time goes in v3:
time: 177 us; the launch traced here: 175 us
  waiting for transfers between devices  108 us (61%)
  starting transfers between devices  41.8 us (24%)
  Pallas kernels  20.3 us (11%)
  local copies, waits for them, and re-layouts  3.61 us (2%)
    ppermute x1, waiting for transfers between devices, layer(): prev = lax.ppermute(kv, 'seq', route)  51.1 us
    all_to_all x1, waiting for transfers between devices, layer(): recv = lax.all_to_all(terms, 'seq', 0, 0, axis_index_groups=halves)  38.9 us
    all_to_all x1, starting transfers between devices, layer(): recv = lax.all_to_all(terms, 'seq', 0, 0, axis_index_groups=halves)  13.6 us
    all_to_all x1, waiting for transfers between devices, layer(): shard = lax.all_to_all(shard, 'seq', 0, 0, axis_index_groups=columns)  11.3 us
    all_to_all x1, starting transfers between devices, layer(): fresh = lax.all_to_all(shard, 'seq', 0, 0, axis_index_groups=rows)  10.4 us
    all_to_all x1, starting transfers between devices, layer(): shard = lax.all_to_all(shard, 'seq', 0, 0, axis_index_groups=columns)  7.31 us
    all_to_all x1, starting transfers between devices, layer(): got = lax.all_to_all(part.reshape(8, 64, 512), 'head', 0, 0)  7.14 us
    all_to_all x1, waiting for transfers between devices, layer(): got = lax.all_to_all(part.reshape(8, 64, 512), 'head', 0, 0)  6.92 us
  transfers between devices with their start and end apart: 5, of which 4 were waited for; matrix products, arithmetic and copies ran while one was open for 1% of the time, Pallas kernels for 4%

profile of v3, /device:TPU:1, one launch (start us, length us, event | category | flops | bytes accessed | tf_op | source)
XLA Modules:
  0.0 174.9 jit_solution(17719957271481839491)
XLA Ops:
  0.6 5.4 %grads.1 = (bf16[32,200,128]{2,1,0:T(8,128)(2,1)}, bf16[2,512,512]{2,1,0:T(8,128)(2,1)}) custom-call(bf16[1,512,512]{2,1,0:T(8,128)(2,1)} %k_hbm.3, bf16[1,512,512]{2,1,0:T(8,128)(2,1)} %v_hbm.3, bf16[1,512,512]{2,1,0:T(8,128)(2,1)} %wg.1, bf16[1,512,512]{2,1,0:T(8,128)(2,1)} %wu.1, bf16[1,512,512]{2,1,0:T(8,128)(2,1)} %wd.1, f32[1,512]{1,0:T(1,128)} %rate_ref.1, ...), custom_call_target="tpu_custom_call" | custom-call | tf_op jit(solution)/shard_map/grads/pallas_call | solution.py:100
  6.0 0.0 copy-start
  6.0 0.0 copy-start.1
  6.1 0.0 copy-start.2
  6.1 13.6 %all-to-all-start = ((bf16[32,200,128]{2,1,0:T(8,128)(2,1)}), bf16[32,200,128]{2,1,0:T(8,128)(2,1)S(1)}, u32[]{:S(2)}, u32[]{:S(2)}) async-start(bf16[32,200,128]{2,1,0:T(8,128)(2,1)} %get-tuple-element.6), calls=%async_computation | async-start | bytes 3276800 | tf_op jit(solution)/shard_map/all_to_all | solution.py:390
  19.7 38.9 %all-to-all-done.recv_ref = bf16[32,200,128]{2,1,0:T(8,128)(2,1)S(1)} async-done(((bf16[32,200,128]{2,1,0:T(8,128)(2,1)}), bf16[32,200,128]{2,1,0:T(8,128)(2,1)S(1)}, u32[]{:S(2)}, u32[]{:S(2)}) %all-to-all-start) | async-done | bytes 1638432 | tf_op jit(solution)/shard_map/all_to_all | solution.py:390
  58.6 0.0 copy-done
  58.6 0.0 copy-done.1
  58.6 0.0 copy-done.2
  58.6 1.1 renorm.1
  59.7 0.0 copy-start.4
  59.7 0.7 copy-done.4
  60.4 7.3 %all-to-all-start.1 = ((bf16[8,3,16,512]{3,2,1,0:T(8,128)(2,1)}), bf16[8,3,16,512]{3,2,1,0:T(8,128)(2,1)S(1)}, u32[]{:S(2)}, u32[]{:S(2)}) async-start(bf16[8,3,16,512]{3,2,1,0:T(8,128)(2,1)} %copy-done.4), calls=%async_computation.1 | async-start | bytes 786432 | tf_op jit(solution)/shard_map/all_to_all | solution.py:393
  67.7 0.1 pad_add_fusion.spot_ref.pos_ref
  67.8 11.3 %all-to-all-done.1.recv = bf16[8,3,16,512]{3,2,1,0:T(8,128)(2,1)S(1)} async-done(((bf16[8,3,16,512]{3,2,1,0:T(8,128)(2,1)}), bf16[8,3,16,512]{3,2,1,0:T(8,128)(2,1)S(1)}, u32[]{:S(2)}, u32[]{:S(2)}) %all-to-all-start.1) | async-done | bytes 393248 | tf_op jit(solution)/shard_map/all_to_all | solution.py:393
  79.1 2.7 %relay.1 = bf16[8,4,3,16,512]{4,3,2,1,0:T(8,128)(2,1)} custom-call(s32[3]{0:T(128)S(1)} %pad_add_fusion.spot_ref.pos_ref, bf16[8,3,16,512]{3,2,1,0:T(8,128)(2,1)S(1)} %all-to-all-done.1.recv, bf16[4,8,16,512]{3,2,1,0:T(8,128)(2,1)} %bitcast.12, bf16[4,8,16,512]{3,2,1,0:T(8,128)(2,1)} %bitcast.13, bf16[4,8,16,512]{3,2,1,0:T(8,128)(2,1)} %bitcast.14), custom_call_target="tpu_custom_call" | custom-call | tf_op jit(solution)/shard_map/relay/pallas_call | solution.py:262
  81.8 0.0 copy-done.6
  81.8 10.4 %all-to-all-start.2 = ((bf16[8,4,3,16,512]{4,3,2,1,0:T(8,128)(2,1)}), bf16[8,4,3,16,512]{4,3,2,1,0:T(8,128)(2,1)S(1)}, u32[]{:S(2)}, u32[]{:S(2)}) async-start(bf16[8,4,3,16,512]{4,3,2,1,0:T(8,128)(2,1)} %relay.1), calls=%async_computation.2 | async-start | bytes 3145728 | tf_op jit(solution)/shard_map/all_to_all | solution.py:395
  92.2 3.4 %collective-permute-start = (bf16[2,512,512]{2,1,0:T(8,128)(2,1)S(1)}, bf16[2,512,512]{2,1,0:T(8,128)(2,1)S(1)}, u32[]{:S(2)}, u32[]{:S(2)}) collective-permute-start(bf16[2,512,512]{2,1,0:T(8,128)(2,1)S(1)} %copy-done.9), channel_id=1, source_target_pairs={{0,1},{1,2},{2,3},{3,4},{4,5},{5,6},{6,7},{7,8},{8,9},{9,10},{10,1... | collective-permute-start | bytes 3145736 | tf_op jit(solution)/shard_map/ppermute | solution.py:391
  95.6 51.1 %collective-permute-done.prev_hbm = bf16[2,512,512]{2,1,0:T(8,128)(2,1)S(1)} collective-permute-done((bf16[2,512,512]{2,1,0:T(8,128)(2,1)S(1)}, bf16[2,512,512]{2,1,0:T(8,128)(2,1)S(1)}, u32[]{:S(2)}, u32[]{:S(2)}) %collective-permute-start) | collective-permute-done | bytes 1048608 | tf_op jit(solution)/shard_map/ppermute | solution.py:391
  146.7 1.0 copy-done.8
  147.7 6.2 %attend.1.att_hbm = f32[2,512,512]{2,1,0:T(8,128)} custom-call(s32[3]{0:T(128)} %copy-done.6, s32[1,512]{1,0:T(1,128)} %bitcast.15, bf16[1,512,512]{2,1,0:T(8,128)(2,1)} %q_hbm.3, bf16[1,512,512]{2,1,0:T(8,128)(2,1)} %k_hbm.3, bf16[1,512,512]{2,1,0:T(8,128)(2,1)} %v_hbm.3, bf16[2,512,512]{2,1,0:T(8,128)(2,1)} %copy-done.8), custom_call_target="tpu_custom_call" | custom-call | tf_op jit(solution)/shard_map/attend/pallas_call | solution.py:216
  153.9 0.0 all-to-all-done.2.fresh
  153.9 0.0 copy-done.3
  153.9 0.0 copy-done.5
  154.0 3.0 %fast_apply.1 = (bf16[1,512,512]{2,1,0:T(8,128)(2,1)}, bf16[512,512]{1,0:T(8,128)(2,1)}) custom-call(bf16[8,4,3,16,512]{4,3,2,1,0:T(8,128)(2,1)S(1)} %all-to-all-done.2.fresh, bf16[1,512,512]{2,1,0:T(8,128)(2,1)S(1)} %copy-done.3, f32[2,512,512]{2,1,0:T(8,128)} %attend.1.att_hbm, bf16[512,512]{1,0:T(8,128)(2,1)S(1)} %copy-done.5), custom_call_target="tpu_custom_call" | custom-call | tf_op jit(solution)/shard_map/fast_apply/pallas_call | solution.py:321
  157.0 7.1 %all-to-all-start.3 = ((bf16[8,64,512]{2,1,0:T(8,128)(2,1)}), bf16[8,64,512]{2,1,0:T(8,128)(2,1)S(1)}, u32[]{:S(2)}, u32[]{:S(2)}) async-start(bf16[8,64,512]{2,1,0:T(8,128)(2,1)} %bitcast.9), calls=%async_computation.3 | async-start | bytes 1048576 | tf_op jit(solution)/shard_map/all_to_all | solution.py:398
  164.1 1.3 dynamic-slice_bitcast_fusion.x_ref
  165.4 1.2 shard_map.113.flag_ref
  166.5 6.9 %all-to-all-done.3.recv_ref = bf16[8,64,512]{2,1,0:T(8,128)(2,1)S(1)} async-done(((bf16[8,64,512]{2,1,0:T(8,128)(2,1)}), bf16[8,64,512]{2,1,0:T(8,128)(2,1)S(1)}, u32[]{:S(2)}, u32[]{:S(2)}) %all-to-all-start.3) | async-done | bytes 524320 | tf_op jit(solution)/shard_map/all_to_all | solution.py:398
  173.5 0.6 copy-done.7
  174.1 0.8 combine.1
  (7 shorter events, 0.0 us)
Async XLA Ops:
  6.0 52.5 %copy-start = (bf16[1,512,512]{2,1,0:T(8,128)(2,1)S(1)}, bf16[1,512,512]{2,1,0:T(8,128)(2,1)}, u32[]{:S(2)}) copy-start(bf16[1,512,512]{2,1,0:T(8,128)(2,1)} %wg.1) | copy-start | bytes 1572868
  6.0 52.5 %copy-start.1 = (bf16[1,512,512]{2,1,0:T(8,128)(2,1)S(1)}, bf16[1,512,512]{2,1,0:T(8,128)(2,1)}, u32[]{:S(2)}) copy-start(bf16[1,512,512]{2,1,0:T(8,128)(2,1)} %wu.1) | copy-start | bytes 1572868
  6.1 52.5 %copy-start.2 = (bf16[1,512,512]{2,1,0:T(8,128)(2,1)S(1)}, bf16[1,512,512]{2,1,0:T(8,128)(2,1)}, u32[]{:S(2)}) copy-start(bf16[1,512,512]{2,1,0:T(8,128)(2,1)} %wd.1) | copy-start | bytes 1572868
  6.1 52.5 %all-to-all-start = ((bf16[32,200,128]{2,1,0:T(8,128)(2,1)}), bf16[32,200,128]{2,1,0:T(8,128)(2,1)S(1)}, u32[]{:S(2)}, u32[]{:S(2)}) async-start(bf16[32,200,128]{2,1,0:T(8,128)(2,1)} %get-tuple-element.6), calls=%async_computation | async-start | bytes 3276800 | tf_op jit(solution)/shard_map/all_to_all | solution.py:390
  59.7 0.7 copy-start.4
  60.4 18.7 %all-to-all-start.1 = ((bf16[8,3,16,512]{3,2,1,0:T(8,128)(2,1)}), bf16[8,3,16,512]{3,2,1,0:T(8,128)(2,1)S(1)}, u32[]{:S(2)}, u32[]{:S(2)}) async-start(bf16[8,3,16,512]{3,2,1,0:T(8,128)(2,1)} %copy-done.4), calls=%async_computation.1 | async-start | bytes 786432 | tf_op jit(solution)/shard_map/all_to_all | solution.py:393
  67.8 14.0 %copy-start.6 = (s32[3]{0:T(128)}, s32[3]{0:T(128)S(1)}, u32[]{:S(2)}) copy-start(s32[3]{0:T(128)S(1)} %pad_add_fusion.spot_ref.pos_ref) | copy-start | bytes 40
  81.8 10.4 %copy-start.9 = (bf16[2,512,512]{2,1,0:T(8,128)(2,1)S(1)}, bf16[2,512,512]{2,1,0:T(8,128)(2,1)}, u32[]{:S(2)}) copy-start(bf16[2,512,512]{2,1,0:T(8,128)(2,1)} %get-tuple-element.7) | copy-start | bytes 3145732
  81.8 72.1 %all-to-all-start.2 = ((bf16[8,4,3,16,512]{4,3,2,1,0:T(8,128)(2,1)}), bf16[8,4,3,16,512]{4,3,2,1,0:T(8,128)(2,1)S(1)}, u32[]{:S(2)}, u32[]{:S(2)}) async-start(bf16[8,4,3,16,512]{4,3,2,1,0:T(8,128)(2,1)} %relay.1), calls=%async_computation.2 | async-start | bytes 3145728 | tf_op jit(solution)/shard_map/all_to_all | solution.py:395
  92.2 54.6 %collective-permute-start = (bf16[2,512,512]{2,1,0:T(8,128)(2,1)S(1)}, bf16[2,512,512]{2,1,0:T(8,128)(2,1)S(1)}, u32[]{:S(2)}, u32[]{:S(2)}) collective-permute-start(bf16[2,512,512]{2,1,0:T(8,128)(2,1)S(1)} %copy-done.9), channel_id=1, source_target_pairs={{0,1},{1,2},{2,3},{3,4},{4,5},{5,6},{6,7},{7,8},{8,9},{9,10},{10,1... | collective-permute-start | bytes 3145736 | tf_op jit(solution)/shard_map/ppermute | solution.py:391
  146.7 1.0 copy-start.8
  147.7 6.2 %copy-start.3 = (bf16[1,512,512]{2,1,0:T(8,128)(2,1)S(1)}, bf16[1,512,512]{2,1,0:T(8,128)(2,1)}, u32[]{:S(2)}) copy-start(bf16[1,512,512]{2,1,0:T(8,128)(2,1)} %q_hbm.3) | copy-start | bytes 1572868
  147.7 6.2 %copy-start.5 = (bf16[512,512]{1,0:T(8,128)(2,1)S(1)}, bf16[512,512]{1,0:T(8,128)(2,1)}, u32[]{:S(2)}) copy-start(bf16[512,512]{1,0:T(8,128)(2,1)} %wc_hbm.1) | copy-start | bytes 1572868
  157.0 16.5 %all-to-all-start.3 = ((bf16[8,64,512]{2,1,0:T(8,128)(2,1)}), bf16[8,64,512]{2,1,0:T(8,128)(2,1)S(1)}, u32[]{:S(2)}, u32[]{:S(2)}) async-start(bf16[8,64,512]{2,1,0:T(8,128)(2,1)} %bitcast.9), calls=%async_computation.3 | async-start | bytes 1048576 | tf_op jit(solution)/shard_map/all_to_all | solution.py:398
  173.5 0.6 copy-start.7

commit v4 on v3

--- a/solution.py
+++ b/solution.py
@@ -24,8 +24,8 @@
 
 
 def grads_kernel(
-    k_hbm, v_hbm, wg_hbm, wu_hbm, wd_hbm, rate_ref, flag_ref, out_hbm, kv_hbm,
-    k_s, v_s, wg_s, wu_s, wd_s, out_s, sem_in, sem_out, sem_kv,
+    k_hbm, v_hbm, wg_hbm, wu_hbm, wd_hbm, rate_ref, flag_ref, out_hbm,
+    k_s, v_s, wg_s, wu_s, wd_s, out_s, sem_in, sem_out,
 ):
     loads = [
         pltpu.make_async_copy(src.at[0], dst, sem_in.at[i])
@@ -65,11 +65,6 @@
     down = wd_s[...].T
     for load in loads[2:]:
         load.wait()
-    pair = [
-        pltpu.make_async_copy(src, kv_hbm.at[i], sem_kv.at[i]) for i, src in enumerate((k_s, v_s))
-    ]
-    for copy in pair:
-        copy.start()
     key = k_s[...]
     hidden = []
     for start in range(0, 512, step):
@@ -90,7 +85,7 @@
         rows = slice(start, start + step)
         put(dot(scaled[rows], hidden, NT).astype(BF16), 2, start)
         ship(128, 200, start, step)
-    for store in stores + pair:
+    for store in stores:
         store.wait()
 
 
@@ -99,18 +94,14 @@
     hb = pl.BlockSpec(memory_space=pltpu.HBM)
     return pl.pallas_call(
         grads_kernel,
-        out_shape=(
-            jax.ShapeDtypeStruct((32, 200, 128), BF16),
-            jax.ShapeDtypeStruct((2, 512, 512), BF16),
-        ),
+        out_shape=jax.ShapeDtypeStruct((32, 200, 128), BF16),
         in_specs=[hb] * 5 + [vm, vm],
-        out_specs=(hb, hb),
+        out_specs=hb,
         scratch_shapes=[pltpu.VMEM((512, 512), BF16)] * 5
         + [
             pltpu.VMEM((32, 200, 128), BF16),
             pltpu.SemaphoreType.DMA((5,)),
             pltpu.SemaphoreType.DMA((2 * (512 // GRADS_STEP),)),
-            pltpu.SemaphoreType.DMA((2,)),
         ],
         name="grads",
     )(k, v, wg, wu, wd, rate, flag)
@@ -173,18 +164,25 @@
 
 
 def attend_kernel(
-    pos_ref, doc_ref, q_hbm, k_hbm, v_hbm, prev_hbm, out_hbm, q_ref, k_ref, v_ref, prev, att_s, sem
+    pos_ref, doc_ref, q_hbm, k_hbm, v_hbm, pk_hbm, pv_hbm, out_hbm,
+    q_ref, k_ref, v_ref, pk_ref, pv_ref, att_s, sem,
 ):
     base = pos_ref[2]
     loads = [
         pltpu.make_async_copy(src.at[0], dst, sem.at[i])
-        for i, (src, dst) in enumerate(((q_hbm, q_ref), (k_hbm, k_ref), (v_hbm, v_ref)))
+        for i, (src, dst) in enumerate(
+            (
+                (q_hbm, q_ref),
+                (k_hbm, k_ref),
+                (v_hbm, v_ref),
+                (pk_hbm, pk_ref),
+                (pv_hbm, pv_ref),
+            )
+        )
     ]
     for load in loads:
         load.start()
 
-    loads.append(pltpu.make_async_copy(prev_hbm, prev, sem.at[3]))
-    loads[3].start()
     for load in loads:
         load.wait()
     step = 128
@@ -193,8 +191,8 @@
     for start in range(0, 512, step):
         rows = slice(start, start + step)
         q = q_ref[rows, :]
-        keys = jnp.concatenate([prev[0, start:, :], k_ref[: start + step, :]], axis=0)
-        vals = jnp.concatenate([prev[1, start:, :], v_ref[: start + step, :]], axis=0)
+        keys = jnp.concatenate([pk_ref[start:, :], k_ref[: start + step, :]], axis=0)
+        vals = jnp.concatenate([pv_ref[start:, :], v_ref[: start + step, :]], axis=0)
         width = 512 + step
         s = dot(q, keys, NT) * scale
         at = lax.broadcasted_iota(jnp.int32, (step, width), 0) + start
@@ -205,27 +203,26 @@
         e = jnp.exp(s - top)
         prob = (e / jnp.sum(e, axis=-1, keepdims=True)).astype(BF16)
         att_s[rows, :] = dot(prob, vals, NN)
-    store = pltpu.make_async_copy(att_s, out_hbm.at[0], sem.at[4])
+    store = pltpu.make_async_copy(att_s, out_hbm.at[0], sem.at[5])
     store.start()
     store.wait()
 
 
-def attend(pos, q, k, v, doc, prev):
+def attend(pos, q, k, v, doc, pk, pv):
     vm = pl.BlockSpec(memory_space=pltpu.VMEM)
     hb = pl.BlockSpec(memory_space=pltpu.HBM)
     return pl.pallas_call(
         attend_kernel,
         out_shape=jax.ShapeDtypeStruct((2, 512, 512), F32),
-        in_specs=[pl.BlockSpec(memory_space=pltpu.SMEM), vm] + [hb] * 4,
+        in_specs=[pl.BlockSpec(memory_space=pltpu.SMEM), vm] + [hb] * 5,
         out_specs=hb,
-        scratch_shapes=[pltpu.VMEM((512, 512), BF16)] * 3
+        scratch_shapes=[pltpu.VMEM((512, 512), BF16)] * 5
         + [
-            pltpu.VMEM((2, 512, 512), BF16),
             pltpu.VMEM((512, 512), F32),
-            pltpu.SemaphoreType.DMA((5,)),
+            pltpu.SemaphoreType.DMA((6,)),
         ],
         name="attend",
-    )(pos, doc, q, k, v, prev)
+    )(pos, doc, q, k, v, pk, pv)
 
 
 def relay_kernel(spot_ref, recv, wg, wu, wd, out, own, sem_in, sem_out):
@@ -358,20 +355,6 @@
     )(recv, flag)
 
 
-def mark_kernel(x_ref, out_ref):
-    out_ref[...] = x_ref[...]
-
-
-def mark(x):
-    vm = pl.BlockSpec(memory_space=pltpu.VMEM)
-    return pl.pallas_call(
-        mark_kernel,
-        out_shape=jax.ShapeDtypeStruct(x.shape, x.dtype),
-        in_specs=[vm],
-        out_specs=vm,
-    )(x)
-
-
 def layer(q, k, v, rate, doc_start, flag, wg, wu, wd, wc):
     seq_count = lax.axis_size("seq")
     half = seq_count // 2
@@ -384,16 +367,16 @@
     route = [(i - 1, i) for i in range(1, seq_count)]
 
     flags = lax.dynamic_slice_in_dim(flag, lax.axis_index("head") * 64, 64, 0)[None]
-    flags = mark(flags)
     spot = jnp.stack([first, lax.rem(index, 8), index * 512])
-    terms, kv = grads(k, v, rate, flag[None], wg, wu, wd)
+    pk = lax.ppermute(k, "seq", route)
+    pv = lax.ppermute(v, "seq", route)
+    terms = grads(k, v, rate, flag[None], wg, wu, wd)
     recv = lax.all_to_all(terms, "seq", 0, 0, axis_index_groups=halves)
-    prev = lax.ppermute(kv, "seq", route)
     shard = renorm(rank[None], recv, wg, wu, wd, 512 * half)
     shard = lax.all_to_all(shard, "seq", 0, 0, axis_index_groups=columns)
     shard = relay(spot, shard, wg, wu, wd)
     fresh = lax.all_to_all(shard, "seq", 0, 0, axis_index_groups=rows)
-    att = attend(spot, q, k, v, doc_start[None], prev)
+    att = attend(spot, q, k, v, doc_start[None], pk, pv)
     mixed, part = fast_apply(fresh, q, att, wc)
     got = lax.all_to_all(part.reshape(8, 64, 512), "head", 0, 0)
     return mixed, combine(got, flags)

time: 177 us -> 177 us (level)
  starting transfers between devices: 41.8 us -> 44.9 us
    ppermute x1 -> x2, waiting for transfers between devices: 51.1 us -> 48.1 us  [the longest x1 36.8 us: layer(): pk = lax.ppermute(k, 'seq', route)]
    ppermute x1 -> x2, starting transfers between devices: 3.42 us -> 6.48 us  [the longest x1 3.38 us: layer(): pk = lax.ppermute(k, 'seq', route)]
    pallas_call x2 -> x1, Pallas kernels: 6.56 us -> 5.38 us  [grads(): pl.pallas_call(grads_kernel, out_shape=jax.ShapeDtypeStruct((32, 200, 128...]
  transfers between devices with their start and end apart: 5 -> 6, of which waited for: 4 -> 5; matrix products, arithmetic and copies ran while one was open for 1% -> 0% of each run, Pallas kernels for 4% -> 4%
where the time goes in v4:
time: 177 us; the launch traced here: 174 us
  waiting for transfers between devices  107 us (60%)
  starting transfers between devices  44.9 us (25%)
  Pallas kernels  19.1 us (11%)
  local copies, waits for them, and re-layouts  2.33 us (1%)
    all_to_all x1, waiting for transfers between devices, layer(): recv = lax.all_to_all(terms, 'seq', 0, 0, axis_index_groups=halves)  38.9 us
    ppermute x1, waiting for transfers between devices, layer(): pk = lax.ppermute(k, 'seq', route)  36.8 us
    all_to_all x1, starting transfers between devices, layer(): recv = lax.all_to_all(terms, 'seq', 0, 0, axis_index_groups=halves)  13.6 us
    all_to_all x1, waiting for transfers between devices, layer(): shard = lax.all_to_all(shard, 'seq', 0, 0, axis_index_groups=columns)  11.3 us
    ppermute x1, waiting for transfers between devices, layer(): pv = lax.ppermute(v, 'seq', route)  11.2 us
    all_to_all x1, starting transfers between devices, layer(): fresh = lax.all_to_all(shard, 'seq', 0, 0, axis_index_groups=rows)  10.3 us
    all_to_all x1, waiting for transfers between devices, layer(): got = lax.all_to_all(part.reshape(8, 64, 512), 'head', 0, 0)  8.6 us
    all_to_all x1, starting transfers between devices, layer(): shard = lax.all_to_all(shard, 'seq', 0, 0, axis_index_groups=columns)  7.31 us
  transfers between devices with their start and end apart: 6, of which 5 were waited for; matrix products, arithmetic and copies ran while one was open for 0% of the time, Pallas kernels for 4%

profile of v4, /device:TPU:1, one launch (start us, length us, event | category | flops | bytes accessed | tf_op | source)
XLA Modules:
  0.0 174.0 jit_solution(8532111561465913872)
XLA Ops:
  0.6 5.4 %grads.1 = bf16[32,200,128]{2,1,0:T(8,128)(2,1)} custom-call(bf16[1,512,512]{2,1,0:T(8,128)(2,1)} %k_hbm.3, bf16[1,512,512]{2,1,0:T(8,128)(2,1)} %v_hbm.3, bf16[1,512,512]{2,1,0:T(8,128)(2,1)} %wg.1, bf16[1,512,512]{2,1,0:T(8,128)(2,1)} %wu.1, bf16[1,512,512]{2,1,0:T(8,128)(2,1)} %wd.1, f32[1,512]{1,0:T(1,128)} %rate_ref.1, s32[1,512]{1,0:T(1,128)} %bitcast.15), custom_call_target="tpu_custom_call" | custom-call | tf_op jit(solution)/shard_map/grads/pallas_call | solution.py:95
  6.0 0.0 copy-start
  6.0 0.0 copy-start.1
  6.0 0.0 copy-start.2
  6.1 13.6 %all-to-all-start = ((bf16[32,200,128]{2,1,0:T(8,128)(2,1)}), bf16[32,200,128]{2,1,0:T(8,128)(2,1)S(1)}, u32[]{:S(2)}, u32[]{:S(2)}) async-start(bf16[32,200,128]{2,1,0:T(8,128)(2,1)} %grads.1), calls=%async_computation | async-start | bytes 3276800 | tf_op jit(solution)/shard_map/all_to_all | solution.py:374
  19.7 38.9 %all-to-all-done.recv_ref = bf16[32,200,128]{2,1,0:T(8,128)(2,1)S(1)} async-done(((bf16[32,200,128]{2,1,0:T(8,128)(2,1)}), bf16[32,200,128]{2,1,0:T(8,128)(2,1)S(1)}, u32[]{:S(2)}, u32[]{:S(2)}) %all-to-all-start) | async-done | bytes 1638432 | tf_op jit(solution)/shard_map/all_to_all | solution.py:374
  58.6 0.0 copy-done
  58.6 0.0 copy-done.2
  58.6 1.1 renorm.1
  59.7 0.0 copy-start.4
  59.7 0.7 copy-done.4
  60.4 7.3 %all-to-all-start.1 = ((bf16[8,3,16,512]{3,2,1,0:T(8,128)(2,1)}), bf16[8,3,16,512]{3,2,1,0:T(8,128)(2,1)S(1)}, u32[]{:S(2)}, u32[]{:S(2)}) async-start(bf16[8,3,16,512]{3,2,1,0:T(8,128)(2,1)} %copy-done.4), calls=%async_computation.1 | async-start | bytes 786432 | tf_op jit(solution)/shard_map/all_to_all | solution.py:376
  67.8 0.1 pad_add_fusion.spot_ref.pos_ref
  67.8 11.3 %all-to-all-done.1.recv = bf16[8,3,16,512]{3,2,1,0:T(8,128)(2,1)S(1)} async-done(((bf16[8,3,16,512]{3,2,1,0:T(8,128)(2,1)}), bf16[8,3,16,512]{3,2,1,0:T(8,128)(2,1)S(1)}, u32[]{:S(2)}, u32[]{:S(2)}) %all-to-all-start.1) | async-done | bytes 393248 | tf_op jit(solution)/shard_map/all_to_all | solution.py:376
  79.1 2.7 %relay.1 = bf16[8,4,3,16,512]{4,3,2,1,0:T(8,128)(2,1)} custom-call(s32[3]{0:T(128)S(1)} %pad_add_fusion.spot_ref.pos_ref, bf16[8,3,16,512]{3,2,1,0:T(8,128)(2,1)S(1)} %all-to-all-done.1.recv, bf16[4,8,16,512]{3,2,1,0:T(8,128)(2,1)} %bitcast.12, bf16[4,8,16,512]{3,2,1,0:T(8,128)(2,1)} %bitcast.13, bf16[4,8,16,512]{3,2,1,0:T(8,128)(2,1)} %bitcast.14), custom_call_target="tpu_custom_call" | custom-call | tf_op jit(solution)/shard_map/relay/pallas_call | solution.py:259
  81.8 0.0 copy-start.7
  81.8 0.0 copy-start.8
  81.8 10.3 %all-to-all-start.2 = ((bf16[8,4,3,16,512]{4,3,2,1,0:T(8,128)(2,1)}), bf16[8,4,3,16,512]{4,3,2,1,0:T(8,128)(2,1)S(1)}, u32[]{:S(2)}, u32[]{:S(2)}) async-start(bf16[8,4,3,16,512]{4,3,2,1,0:T(8,128)(2,1)} %relay.1), calls=%async_computation.2 | async-start | bytes 3145728 | tf_op jit(solution)/shard_map/all_to_all | solution.py:378
  92.2 3.4 %collective-permute-start = (bf16[1,512,512]{2,1,0:T(8,128)(2,1)S(1)}, bf16[1,512,512]{2,1,0:T(8,128)(2,1)S(1)}, u32[]{:S(2)}, u32[]{:S(2)}) collective-permute-start(bf16[1,512,512]{2,1,0:T(8,128)(2,1)S(1)} %copy-done.7), channel_id=1, source_target_pairs={{0,1},{1,2},{2,3},{3,4},{4,5},{5,6},{6,7},{7,8},{8,9},{9,10},{10,1... | collective-permute-start | bytes 1572872 | tf_op jit(solution)/shard_map/ppermute | solution.py:371
  95.6 3.1 %collective-permute-start.1 = (bf16[1,512,512]{2,1,0:T(8,128)(2,1)S(1)}, bf16[1,512,512]{2,1,0:T(8,128)(2,1)S(1)}, u32[]{:S(2)}, u32[]{:S(2)}) collective-permute-start(bf16[1,512,512]{2,1,0:T(8,128)(2,1)S(1)} %copy-done.8), channel_id=1, source_target_pairs={{0,1},{1,2},{2,3},{3,4},{4,5},{5,6},{6,7},{7,8},{8,9},{9,10},{10,1... | collective-permute-start | bytes 1572872 | tf_op jit(solution)/shard_map/ppermute | solution.py:372
  98.7 36.8 %collective-permute-done.pk_hbm = bf16[1,512,512]{2,1,0:T(8,128)(2,1)S(1)} collective-permute-done((bf16[1,512,512]{2,1,0:T(8,128)(2,1)S(1)}, bf16[1,512,512]{2,1,0:T(8,128)(2,1)S(1)}, u32[]{:S(2)}, u32[]{:S(2)}) %collective-permute-start) | collective-permute-done | bytes 524320 | tf_op jit(solution)/shard_map/ppermute | solution.py:371
  135.5 11.2 %collective-permute-done.1.pv_hbm = bf16[1,512,512]{2,1,0:T(8,128)(2,1)S(1)} collective-permute-done((bf16[1,512,512]{2,1,0:T(8,128)(2,1)S(1)}, bf16[1,512,512]{2,1,0:T(8,128)(2,1)S(1)}, u32[]{:S(2)}, u32[]{:S(2)}) %collective-permute-start.1) | collective-permute-done | bytes 524320 | tf_op jit(solution)/shard_map/ppermute | solution.py:372
  146.7 0.8 copy-done.10
  147.5 6.2 %attend.1.att_hbm = f32[2,512,512]{2,1,0:T(8,128)} custom-call(s32[3]{0:T(128)} %copy-done.6, s32[1,512]{1,0:T(1,128)} %bitcast.16, bf16[1,512,512]{2,1,0:T(8,128)(2,1)} %q_hbm.3, bf16[1,512,512]{2,1,0:T(8,128)(2,1)} %k_hbm.3, bf16[1,512,512]{2,1,0:T(8,128)(2,1)} %v_hbm.3, bf16[1,512,512]{2,1,0:T(8,128)(2,1)} %copy-done.9, bf16[1,512,512]{2,1,0:T(8,128)(2,1)} %copy-done.10), custom_call_target="tpu_custom_call" | custom-call | tf_op jit(solution)/shard_map/attend/pallas_call | solution.py:214
  153.7 0.0 all-to-all-done.2.fresh
  153.7 0.0 copy-done.3
  153.7 0.0 copy-done.5
  153.7 3.0 %fast_apply.1 = (bf16[1,512,512]{2,1,0:T(8,128)(2,1)}, bf16[512,512]{1,0:T(8,128)(2,1)}) custom-call(bf16[8,4,3,16,512]{4,3,2,1,0:T(8,128)(2,1)S(1)} %all-to-all-done.2.fresh, bf16[1,512,512]{2,1,0:T(8,128)(2,1)S(1)} %copy-done.3, f32[2,512,512]{2,1,0:T(8,128)} %attend.1.att_hbm, bf16[512,512]{1,0:T(8,128)(2,1)S(1)} %copy-done.5), custom_call_target="tpu_custom_call" | custom-call | tf_op jit(solution)/shard_map/fast_apply/pallas_call | solution.py:318
  156.8 7.1 %all-to-all-start.3 = ((bf16[8,64,512]{2,1,0:T(8,128)(2,1)}), bf16[8,64,512]{2,1,0:T(8,128)(2,1)S(1)}, u32[]{:S(2)}, u32[]{:S(2)}) async-start(bf16[8,64,512]{2,1,0:T(8,128)(2,1)} %bitcast.9), calls=%async_computation.3 | async-start | bytes 1048576 | tf_op jit(solution)/shard_map/all_to_all | solution.py:381
  163.9 0.8 dynamic-slice_bitcast_fusion.flag_ref
  164.6 8.6 %all-to-all-done.3.recv_ref = bf16[8,64,512]{2,1,0:T(8,128)(2,1)S(1)} async-done(((bf16[8,64,512]{2,1,0:T(8,128)(2,1)}), bf16[8,64,512]{2,1,0:T(8,128)(2,1)S(1)}, u32[]{:S(2)}, u32[]{:S(2)}) %all-to-all-start.3) | async-done | bytes 524320 | tf_op jit(solution)/shard_map/all_to_all | solution.py:381
  173.2 0.8 combine.1
  (10 shorter events, 0.0 us)
Async XLA Ops:
  6.0 52.6 %copy-start = (bf16[1,512,512]{2,1,0:T(8,128)(2,1)S(1)}, bf16[1,512,512]{2,1,0:T(8,128)(2,1)}, u32[]{:S(2)}) copy-start(bf16[1,512,512]{2,1,0:T(8,128)(2,1)} %wg.1) | copy-start | bytes 1572868
  6.0 52.6 %copy-start.1 = (bf16[1,512,512]{2,1,0:T(8,128)(2,1)S(1)}, bf16[1,512,512]{2,1,0:T(8,128)(2,1)}, u32[]{:S(2)}) copy-start(bf16[1,512,512]{2,1,0:T(8,128)(2,1)} %wu.1) | copy-start | bytes 1572868
  6.0 52.6 %copy-start.2 = (bf16[1,512,512]{2,1,0:T(8,128)(2,1)S(1)}, bf16[1,512,512]{2,1,0:T(8,128)(2,1)}, u32[]{:S(2)}) copy-start(bf16[1,512,512]{2,1,0:T(8,128)(2,1)} %wd.1) | copy-start | bytes 1572868
  6.1 52.5 %all-to-all-start = ((bf16[32,200,128]{2,1,0:T(8,128)(2,1)}), bf16[32,200,128]{2,1,0:T(8,128)(2,1)S(1)}, u32[]{:S(2)}, u32[]{:S(2)}) async-start(bf16[32,200,128]{2,1,0:T(8,128)(2,1)} %grads.1), calls=%async_computation | async-start | bytes 3276800 | tf_op jit(solution)/shard_map/all_to_all | solution.py:374
  59.7 0.7 copy-start.4
  60.4 18.7 %all-to-all-start.1 = ((bf16[8,3,16,512]{3,2,1,0:T(8,128)(2,1)}), bf16[8,3,16,512]{3,2,1,0:T(8,128)(2,1)S(1)}, u32[]{:S(2)}, u32[]{:S(2)}) async-start(bf16[8,3,16,512]{3,2,1,0:T(8,128)(2,1)} %copy-done.4), calls=%async_computation.1 | async-start | bytes 786432 | tf_op jit(solution)/shard_map/all_to_all | solution.py:376
  67.8 14.0 %copy-start.6 = (s32[3]{0:T(128)}, s32[3]{0:T(128)S(1)}, u32[]{:S(2)}) copy-start(s32[3]{0:T(128)S(1)} %pad_add_fusion.spot_ref.pos_ref) | copy-start | bytes 40
  81.8 10.4 %copy-start.7 = (bf16[1,512,512]{2,1,0:T(8,128)(2,1)S(1)}, bf16[1,512,512]{2,1,0:T(8,128)(2,1)}, u32[]{:S(2)}) copy-start(bf16[1,512,512]{2,1,0:T(8,128)(2,1)} %k_hbm.3) | copy-start | bytes 1572868
  81.8 13.7 %copy-start.8 = (bf16[1,512,512]{2,1,0:T(8,128)(2,1)S(1)}, bf16[1,512,512]{2,1,0:T(8,128)(2,1)}, u32[]{:S(2)}) copy-start(bf16[1,512,512]{2,1,0:T(8,128)(2,1)} %v_hbm.3) | copy-start | bytes 1572868
  81.8 71.9 %all-to-all-start.2 = ((bf16[8,4,3,16,512]{4,3,2,1,0:T(8,128)(2,1)}), bf16[8,4,3,16,512]{4,3,2,1,0:T(8,128)(2,1)S(1)}, u32[]{:S(2)}, u32[]{:S(2)}) async-start(bf16[8,4,3,16,512]{4,3,2,1,0:T(8,128)(2,1)} %relay.1), calls=%async_computation.2 | async-start | bytes 3145728 | tf_op jit(solution)/shard_map/all_to_all | solution.py:378
  92.2 43.3 %collective-permute-start = (bf16[1,512,512]{2,1,0:T(8,128)(2,1)S(1)}, bf16[1,512,512]{2,1,0:T(8,128)(2,1)S(1)}, u32[]{:S(2)}, u32[]{:S(2)}) collective-permute-start(bf16[1,512,512]{2,1,0:T(8,128)(2,1)S(1)} %copy-done.7), channel_id=1, source_target_pairs={{0,1},{1,2},{2,3},{3,4},{4,5},{5,6},{6,7},{7,8},{8,9},{9,10},{10,1... | collective-permute-start | bytes 1572872 | tf_op jit(solution)/shard_map/ppermute | solution.py:371
  95.6 51.2 %collective-permute-start.1 = (bf16[1,512,512]{2,1,0:T(8,128)(2,1)S(1)}, bf16[1,512,512]{2,1,0:T(8,128)(2,1)S(1)}, u32[]{:S(2)}, u32[]{:S(2)}) collective-permute-start(bf16[1,512,512]{2,1,0:T(8,128)(2,1)S(1)} %copy-done.8), channel_id=1, source_target_pairs={{0,1},{1,2},{2,3},{3,4},{4,5},{5,6},{6,7},{7,8},{8,9},{9,10},{10,1... | collective-permute-start | bytes 1572872 | tf_op jit(solution)/shard_map/ppermute | solution.py:372
  135.5 11.2 %copy-start.9 = (bf16[1,512,512]{2,1,0:T(8,128)(2,1)}, bf16[1,512,512]{2,1,0:T(8,128)(2,1)S(1)}, u32[]{:S(2)}) copy-start(bf16[1,512,512]{2,1,0:T(8,128)(2,1)S(1)} %collective-permute-done.pk_hbm) | copy-start | bytes 1572868
  146.7 0.8 copy-start.10
  147.5 6.2 %copy-start.3 = (bf16[1,512,512]{2,1,0:T(8,128)(2,1)S(1)}, bf16[1,512,512]{2,1,0:T(8,128)(2,1)}, u32[]{:S(2)}) copy-start(bf16[1,512,512]{2,1,0:T(8,128)(2,1)} %q_hbm.3) | copy-start | bytes 1572868
  147.5 6.2 %copy-start.5 = (bf16[512,512]{1,0:T(8,128)(2,1)S(1)}, bf16[512,512]{1,0:T(8,128)(2,1)}, u32[]{:S(2)}) copy-start(bf16[512,512]{1,0:T(8,128)(2,1)} %wc_hbm.1) | copy-start | bytes 1572868
  156.8 16.5 %all-to-all-start.3 = ((bf16[8,64,512]{2,1,0:T(8,128)(2,1)}), bf16[8,64,512]{2,1,0:T(8,128)(2,1)S(1)}, u32[]{:S(2)}, u32[]{:S(2)}) async-start(bf16[8,64,512]{2,1,0:T(8,128)(2,1)} %bitcast.9), calls=%async_computation.3 | async-start | bytes 1048576 | tf_op jit(solution)/shard_map/all_to_all | solution.py:381

commit v5 on v4

--- a/solution.py
+++ b/solution.py
@@ -11,7 +11,8 @@
 F32 = jnp.float32
 GRADS_STEP = 256
 APPLY_STEP = 256
-RENORM_VMEM = 51200 << 10
+FOLD_VMEM = 52000 << 10
+RENORM_VMEM = 52000 << 10
 RELAY_VMEM = 54800 << 10
 APPLY_VMEM = 50800 << 10
 BF16 = jnp.bfloat16
@@ -105,6 +106,32 @@
         ],
         name="grads",
     )(k, v, wg, wu, wd, rate, flag)
+
+
+def fold_kernel(recv_ref, out_hbm, out_s, sem):
+    for j in range(4):
+        out_s[j, :192, :] = jnp.sum(recv_ref[:, j, :192, :].astype(F32), axis=0).astype(BF16)
+    tail = jnp.sum(recv_ref[:, 0, 192:200, :].astype(F32), axis=0)
+    total = jnp.broadcast_to(tail[0:1] + tail[1:2], (8, 128))
+    high = total.astype(BF16).astype(F32)
+    row = lax.broadcasted_iota(jnp.int32, (8, 128), 0)
+    tail = jnp.where(row == 0, high, jnp.where(row == 1, total - high, 0.0)).astype(BF16)
+    out_s[:, 192:200, :] = jnp.broadcast_to(tail[None], (4, 8, 128))
+    store = pltpu.make_async_copy(out_s, out_hbm, sem)
+    store.start()
+    store.wait()
+
+
+def fold(recv):
+    return pl.pallas_call(
+        fold_kernel,
+        out_shape=jax.ShapeDtypeStruct((4, 200, 128), BF16),
+        in_specs=[pl.BlockSpec(memory_space=pltpu.VMEM)],
+        out_specs=pl.BlockSpec(memory_space=pltpu.HBM),
+        scratch_shapes=[pltpu.VMEM((4, 200, 128), BF16), pltpu.SemaphoreType.DMA],
+        compiler_params=pltpu.CompilerParams(vmem_limit_bytes=FOLD_VMEM),
+        name="fold",
+    )(recv)
 
 
 def renorm_kernel(
@@ -227,7 +254,8 @@
 
 def relay_kernel(spot_ref, recv, wg, wu, wd, out, own, sem_in, sem_out):
     first = spot_ref[0] == 1
-    column = spot_ref[1]
+    parity = spot_ref[1]
+    pair = spot_ref[3]
 
     def send(source):
         copies = [pltpu.make_async_copy(source, out.at[d], sem_out.at[d]) for d in range(8)]
@@ -239,7 +267,7 @@
     @pl.when(first)
     def _():
         copies = [
-            pltpu.make_async_copy(ref.at[:, column], own.at[:, i], sem_in.at[i])
+            pltpu.make_async_copy(ref.at[:, parity, pair], own.at[:, i], sem_in.at[i])
             for i, ref in enumerate((wg, wu, wd))
         ]
         for copy in copies:
@@ -268,7 +296,7 @@
         ],
         compiler_params=pltpu.CompilerParams(vmem_limit_bytes=RELAY_VMEM),
         name="relay",
-    )(spot, recv, *(x.reshape(4, 8, 16, 512) for x in (wg, wu, wd)))
+    )(spot, recv, *(x.reshape(4, 2, 4, 16, 512) for x in (wg, wu, wd)))
 
 
 def apply_kernel(
@@ -283,7 +311,8 @@
         load.start()
 
     def weight(i, low, count):
-        spots = [(z, y) for z in range(low // 128, (low + count) // 128) for y in range(8)]
+        order = [(z, 2 * j + b) for z in range(4) for b in range(2) for j in range(4)]
+        spots = order[low // 16 : (low + count) // 16]
         return jnp.concatenate([fresh[y, z, i] for z, y in spots], axis=0)
 
     step = APPLY_STEP
@@ -360,24 +389,35 @@
     half = seq_count // 2
     index = lax.axis_index("seq").astype(jnp.int32)
     first = (index < half).astype(jnp.int32)
-    rank = lax.rem(index, half)
-    halves = [list(range(half)), list(range(half, seq_count))]
-    columns = [[z * 8 + y for z in range(8)] for y in range(8)]
-    rows = [[z * 8 + y for y in range(8)] for z in range(8)]
+    z, y = lax.div(index, 8), lax.rem(index, 8)
+    layer_z, parity, pair = lax.rem(z, 4), lax.rem(y, 2), lax.div(y, 2)
+    place = lambda z, y: z * 8 + y
+    blocks = [
+        [place(z + lift, 2 * k + b) for z in range(4) for b in range(2)]
+        for lift in (0, 4)
+        for k in range(4)
+    ]
+    strides = [[place(z, 2 * j + b) for j in range(4)] for z in range(8) for b in range(2)]
+    columns = [[place(z, y) for z in range(8)] for y in range(8)]
+    rows = blocks[:4] + [[place(z, y) for y in range(8)] for z in range(4, 8)]
     route = [(i - 1, i) for i in range(1, seq_count)]
 
-    flags = lax.dynamic_slice_in_dim(flag, lax.axis_index("head") * 64, 64, 0)[None]
-    spot = jnp.stack([first, lax.rem(index, 8), index * 512])
+    spot_in_block = layer_z * 2 + parity
+    sender = jnp.where(first == 1, spot_in_block, y)
+    spot = jnp.stack([first, lax.rem(sender, 2), index * 512, lax.div(sender, 2)])
     pk = lax.ppermute(k, "seq", route)
     pv = lax.ppermute(v, "seq", route)
     terms = grads(k, v, rate, flag[None], wg, wu, wd)
-    recv = lax.all_to_all(terms, "seq", 0, 0, axis_index_groups=halves)
+    recv = lax.all_to_all(terms.reshape(8, 4, 200, 128), "seq", 0, 0, axis_index_groups=blocks)
+    recv = lax.all_to_all(fold(recv), "seq", 0, 0, axis_index_groups=strides)
+    rank = spot_in_block * 4 + pair
     shard = renorm(rank[None], recv, wg, wu, wd, 512 * half)
     shard = lax.all_to_all(shard, "seq", 0, 0, axis_index_groups=columns)
     shard = relay(spot, shard, wg, wu, wd)
     fresh = lax.all_to_all(shard, "seq", 0, 0, axis_index_groups=rows)
     att = attend(spot, q, k, v, doc_start[None], pk, pv)
     mixed, part = fast_apply(fresh, q, att, wc)
+    flags = lax.dynamic_slice_in_dim(flag, lax.axis_index("head") * 64, 64, 0)[None]
     got = lax.all_to_all(part.reshape(8, 64, 512), "head", 0, 0)
     return mixed, combine(got, flags)
 

time: 177 us -> 172 us (0.972)
  the two profiles are of different devices: /device:TPU:1 before, /device:TPU:448 now
where the time goes in v5:
time: 172 us; the launch traced here: 171 us
  waiting for transfers between devices  79.7 us (46%)
  blocking collectives  41.9 us (24%)
  starting transfers between devices  27.7 us (16%)
  Pallas kernels  19.3 us (11%)
    all_to_all x1, blocking collectives, layer(): lax.all_to_all(terms.reshape(8, 4, 200, 128), 'seq', 0, 0, axis_index_gro...  41.9 us
    ppermute x1, waiting for transfers between devices, layer(): pk = lax.ppermute(k, 'seq', route)  41.2 us
    ppermute x1, waiting for transfers between devices, layer(): pv = lax.ppermute(v, 'seq', route)  10.2 us
    all_to_all x1, waiting for transfers between devices, layer(): recv = lax.all_to_all(fold(recv), 'seq', 0, 0, axis_index_groups=strides)  10 us
    all_to_all x1, waiting for transfers between devices, layer(): got = lax.all_to_all(part.reshape(8, 64, 512), 'head', 0, 0)  9.56 us
    all_to_all x1, waiting for transfers between devices, layer(): shard = lax.all_to_all(shard, 'seq', 0, 0, axis_index_groups=columns)  8.68 us
    all_to_all x1, starting transfers between devices, layer(): recv = lax.all_to_all(fold(recv), 'seq', 0, 0, axis_index_groups=strides)  6.2 us
    pallas_call x1, Pallas kernels, attend(): pl.pallas_call(attend_kernel, out_shape=jax.ShapeDtypeStruct((2, 512, 512...  6.17 us
  transfers between devices with their start and end apart: 6, of which 5 were waited for; matrix products, arithmetic and copies ran while one was open for 0% of the time, Pallas kernels for 4%

profile of v5, /device:TPU:448, one launch (start us, length us, event | category | flops | bytes accessed | tf_op | source)
XLA Modules:
  0.0 171.0 jit_solution(16888254179352881603)
XLA Ops:
  0.6 5.4 %grads.1 = bf16[32,200,128]{2,1,0:T(8,128)(2,1)} custom-call(bf16[1,512,512]{2,1,0:T(8,128)(2,1)} %k_hbm.3, bf16[1,512,512]{2,1,0:T(8,128)(2,1)} %v_hbm.3, bf16[1,512,512]{2,1,0:T(8,128)(2,1)} %wg.1, bf16[1,512,512]{2,1,0:T(8,128)(2,1)} %wu.1, bf16[1,512,512]{2,1,0:T(8,128)(2,1)} %wd.1, f32[1,512]{1,0:T(1,128)} %rate_ref.1, s32[1,512]{1,0:T(1,128)} %bitcast.18), custom_call_target="tpu_custom_call" | custom-call | tf_op jit(solution)/shard_map/grads/pallas_call | solution.py:96
  6.0 41.9 %all_to_all.25.recv_ref = bf16[8,4,200,128]{3,2,1,0:T(8,128)(2,1)S(1)} all-to-all(bf16[8,4,200,128]{3,2,1,0:T(8,128)(2,1)} %bitcast.17), channel_id=1, replica_groups={{0,1,8,9,16,17,24,25},{2,3,10,11,18,19,26,27},{4,5,12,13,20,21,28,29},{..., dimensions={0} | all-to-all | bytes 3276800 | tf_op jit(solution)/shard_map/all_to_all | solution.py:411
  47.9 0.9 fold.1
  48.8 6.2 %all-to-all-start.1 = ((bf16[4,200,128]{2,1,0:T(8,128)(2,1)}), bf16[4,200,128]{2,1,0:T(8,128)(2,1)S(1)}, u32[]{:S(2)}, u32[]{:S(2)}) async-start(bf16[4,200,128]{2,1,0:T(8,128)(2,1)} %fold.1), calls=%async_computation.1 | async-start | bytes 409600 | tf_op jit(solution)/shard_map/all_to_all | solution.py:412
  55.0 10.0 %all-to-all-done.1.recv_ref = bf16[4,200,128]{2,1,0:T(8,128)(2,1)S(1)} async-done(((bf16[4,200,128]{2,1,0:T(8,128)(2,1)}), bf16[4,200,128]{2,1,0:T(8,128)(2,1)S(1)}, u32[]{:S(2)}, u32[]{:S(2)}) %all-to-all-start.1) | async-done | bytes 204832 | tf_op jit(solution)/shard_map/all_to_all | solution.py:412
  65.0 0.0 copy-done
  65.0 0.0 copy-done.1
  65.0 0.0 copy-done.2
  65.0 1.3 renorm.1
  66.3 5.9 %all-to-all-start.2 = ((bf16[8,3,16,512]{3,2,1,0:T(8,128)(2,1)}), bf16[8,3,16,512]{3,2,1,0:T(8,128)(2,1)S(1)}, u32[]{:S(2)}, u32[]{:S(2)}) async-start(bf16[8,3,16,512]{3,2,1,0:T(8,128)(2,1)} %renorm.1), calls=%async_computation.2 | async-start | bytes 786432 | tf_op jit(solution)/shard_map/all_to_all | solution.py:415
  72.2 0.1 pad_add_fusion.spot_ref.pos_ref
  72.3 8.7 %all-to-all-done.2.recv = bf16[8,3,16,512]{3,2,1,0:T(8,128)(2,1)S(1)} async-done(((bf16[8,3,16,512]{3,2,1,0:T(8,128)(2,1)}), bf16[8,3,16,512]{3,2,1,0:T(8,128)(2,1)S(1)}, u32[]{:S(2)}, u32[]{:S(2)}) %all-to-all-start.2) | async-done | bytes 393248 | tf_op jit(solution)/shard_map/all_to_all | solution.py:415
  81.0 1.8 %relay.1 = bf16[8,4,3,16,512]{4,3,2,1,0:T(8,128)(2,1)} custom-call(s32[4]{0:T(128)S(1)} %pad_add_fusion.spot_ref.pos_ref, bf16[8,3,16,512]{3,2,1,0:T(8,128)(2,1)S(1)} %all-to-all-done.2.recv, bf16[4,2,4,16,512]{4,3,2,1,0:T(8,128)(2,1)} %bitcast.14, bf16[4,2,4,16,512]{4,3,2,1,0:T(8,128)(2,1)} %bitcast.15, bf16[4,2,4,16,512]{4,3,2,1,0:T(8,128)(2,1)} %bitcast.16), custom_call_target="tpu_custom_call" | custom-call | tf_op jit(solution)/shard_map/relay/pallas_call | solution.py:287
  82.8 0.0 copy-done.5
  82.8 0.0 copy-start.6
  82.8 0.0 copy-start.7
  82.8 4.0 %all-to-all-start.3 = ((bf16[8,4,3,16,512]{4,3,2,1,0:T(8,128)(2,1)}), bf16[8,4,3,16,512]{4,3,2,1,0:T(8,128)(2,1)S(1)}, u32[]{:S(2)}, u32[]{:S(2)}) async-start(bf16[8,4,3,16,512]{4,3,2,1,0:T(8,128)(2,1)} %relay.1), calls=%async_computation.3 | async-start | bytes 3145728 | tf_op jit(solution)/shard_map/all_to_all | solution.py:417
  86.8 0.0 copy-done.6
  86.8 3.9 %collective-permute-start = (bf16[1,512,512]{2,1,0:T(8,128)(2,1)S(1)}, bf16[1,512,512]{2,1,0:T(8,128)(2,1)S(1)}, u32[]{:S(2)}, u32[]{:S(2)}) collective-permute-start(bf16[1,512,512]{2,1,0:T(8,128)(2,1)S(1)} %copy-done.6), channel_id=1, source_target_pairs={{0,1},{1,2},{2,3},{3,4},{4,5},{5,6},{6,7},{7,8},{8,9},{9,10},{10,1... | collective-permute-start | bytes 1572872 | tf_op jit(solution)/shard_map/ppermute | solution.py:408
  90.7 0.0 copy-done.7
  90.8 3.4 %collective-permute-start.1 = (bf16[1,512,512]{2,1,0:T(8,128)(2,1)S(1)}, bf16[1,512,512]{2,1,0:T(8,128)(2,1)S(1)}, u32[]{:S(2)}, u32[]{:S(2)}) collective-permute-start(bf16[1,512,512]{2,1,0:T(8,128)(2,1)S(1)} %copy-done.7), channel_id=1, source_target_pairs={{0,1},{1,2},{2,3},{3,4},{4,5},{5,6},{6,7},{7,8},{8,9},{9,10},{10,1... | collective-permute-start | bytes 1572872 | tf_op jit(solution)/shard_map/ppermute | solution.py:409
  94.1 41.2 %collective-permute-done.pk_hbm = bf16[1,512,512]{2,1,0:T(8,128)(2,1)S(1)} collective-permute-done((bf16[1,512,512]{2,1,0:T(8,128)(2,1)S(1)}, bf16[1,512,512]{2,1,0:T(8,128)(2,1)S(1)}, u32[]{:S(2)}, u32[]{:S(2)}) %collective-permute-start) | collective-permute-done | bytes 524320 | tf_op jit(solution)/shard_map/ppermute | solution.py:408
  135.4 10.2 %collective-permute-done.1.pv_hbm = bf16[1,512,512]{2,1,0:T(8,128)(2,1)S(1)} collective-permute-done((bf16[1,512,512]{2,1,0:T(8,128)(2,1)S(1)}, bf16[1,512,512]{2,1,0:T(8,128)(2,1)S(1)}, u32[]{:S(2)}, u32[]{:S(2)}) %collective-permute-start.1) | collective-permute-done | bytes 524320 | tf_op jit(solution)/shard_map/ppermute | solution.py:409
  145.6 0.0 copy-done.8
  145.6 0.8 copy-done.9
  146.4 6.2 %attend.1.att_hbm = f32[2,512,512]{2,1,0:T(8,128)} custom-call(s32[4]{0:T(128)} %copy-done.5, s32[1,512]{1,0:T(1,128)} %bitcast.19, bf16[1,512,512]{2,1,0:T(8,128)(2,1)} %q_hbm.3, bf16[1,512,512]{2,1,0:T(8,128)(2,1)} %k_hbm.3, bf16[1,512,512]{2,1,0:T(8,128)(2,1)} %v_hbm.3, bf16[1,512,512]{2,1,0:T(8,128)(2,1)} %copy-done.8, bf16[1,512,512]{2,1,0:T(8,128)(2,1)} %copy-done.9), custom_call_target="tpu_custom_call" | custom-call | tf_op jit(solution)/shard_map/attend/pallas_call | solution.py:241
  152.6 0.0 all-to-all-done.3.fresh
  152.6 3.0 %fast_apply.1 = (bf16[1,512,512]{2,1,0:T(8,128)(2,1)}, bf16[512,512]{1,0:T(8,128)(2,1)}) custom-call(bf16[8,4,3,16,512]{4,3,2,1,0:T(8,128)(2,1)S(1)} %all-to-all-done.3.fresh, bf16[1,512,512]{2,1,0:T(8,128)(2,1)S(1)} %copy-done.3, f32[2,512,512]{2,1,0:T(8,128)} %attend.1.att_hbm, bf16[512,512]{1,0:T(8,128)(2,1)S(1)} %copy-done.4), custom_call_target="tpu_custom_call" | custom-call | tf_op jit(solution)/shard_map/fast_apply/pallas_call | solution.py:347
  155.6 4.3 %all-to-all-start.4 = ((bf16[8,64,512]{2,1,0:T(8,128)(2,1)}), bf16[8,64,512]{2,1,0:T(8,128)(2,1)S(1)}, u32[]{:S(2)}, u32[]{:S(2)}) async-start(bf16[8,64,512]{2,1,0:T(8,128)(2,1)} %bitcast.11), calls=%async_computation.4 | async-start | bytes 1048576 | tf_op jit(solution)/shard_map/all_to_all | solution.py:421
  159.9 0.8 dynamic-slice_bitcast_fusion.flag_ref
  160.7 9.6 %all-to-all-done.4.recv_ref = bf16[8,64,512]{2,1,0:T(8,128)(2,1)S(1)} async-done(((bf16[8,64,512]{2,1,0:T(8,128)(2,1)}), bf16[8,64,512]{2,1,0:T(8,128)(2,1)S(1)}, u32[]{:S(2)}, u32[]{:S(2)}) %all-to-all-start.4) | async-done | bytes 524320 | tf_op jit(solution)/shard_map/all_to_all | solution.py:421
  170.3 0.8 combine.1
  (10 shorter events, 0.0 us)
Async XLA Ops:
  47.9 17.1 %copy-start = (bf16[1,512,512]{2,1,0:T(8,128)(2,1)S(1)}, bf16[1,512,512]{2,1,0:T(8,128)(2,1)}, u32[]{:S(2)}) copy-start(bf16[1,512,512]{2,1,0:T(8,128)(2,1)} %wg.1) | copy-start | bytes 1572868
  47.9 17.1 %copy-start.1 = (bf16[1,512,512]{2,1,0:T(8,128)(2,1)S(1)}, bf16[1,512,512]{2,1,0:T(8,128)(2,1)}, u32[]{:S(2)}) copy-start(bf16[1,512,512]{2,1,0:T(8,128)(2,1)} %wu.1) | copy-start | bytes 1572868
  47.9 17.1 %copy-start.2 = (bf16[1,512,512]{2,1,0:T(8,128)(2,1)S(1)}, bf16[1,512,512]{2,1,0:T(8,128)(2,1)}, u32[]{:S(2)}) copy-start(bf16[1,512,512]{2,1,0:T(8,128)(2,1)} %wd.1) | copy-start | bytes 1572868
  48.8 16.2 %all-to-all-start.1 = ((bf16[4,200,128]{2,1,0:T(8,128)(2,1)}), bf16[4,200,128]{2,1,0:T(8,128)(2,1)S(1)}, u32[]{:S(2)}, u32[]{:S(2)}) async-start(bf16[4,200,128]{2,1,0:T(8,128)(2,1)} %fold.1), calls=%async_computation.1 | async-start | bytes 409600 | tf_op jit(solution)/shard_map/all_to_all | solution.py:412
  66.3 14.7 %all-to-all-start.2 = ((bf16[8,3,16,512]{3,2,1,0:T(8,128)(2,1)}), bf16[8,3,16,512]{3,2,1,0:T(8,128)(2,1)S(1)}, u32[]{:S(2)}, u32[]{:S(2)}) async-start(bf16[8,3,16,512]{3,2,1,0:T(8,128)(2,1)} %renorm.1), calls=%async_computation.2 | async-start | bytes 786432 | tf_op jit(solution)/shard_map/all_to_all | solution.py:415
  72.3 10.5 %copy-start.5 = (s32[4]{0:T(128)}, s32[4]{0:T(128)S(1)}, u32[]{:S(2)}) copy-start(s32[4]{0:T(128)S(1)} %pad_add_fusion.spot_ref.pos_ref) | copy-start | bytes 52
  82.8 4.0 %copy-start.6 = (bf16[1,512,512]{2,1,0:T(8,128)(2,1)S(1)}, bf16[1,512,512]{2,1,0:T(8,128)(2,1)}, u32[]{:S(2)}) copy-start(bf16[1,512,512]{2,1,0:T(8,128)(2,1)} %k_hbm.3) | copy-start | bytes 1572868
  82.8 7.9 %copy-start.7 = (bf16[1,512,512]{2,1,0:T(8,128)(2,1)S(1)}, bf16[1,512,512]{2,1,0:T(8,128)(2,1)}, u32[]{:S(2)}) copy-start(bf16[1,512,512]{2,1,0:T(8,128)(2,1)} %v_hbm.3) | copy-start | bytes 1572868
  82.8 69.8 %all-to-all-start.3 = ((bf16[8,4,3,16,512]{4,3,2,1,0:T(8,128)(2,1)}), bf16[8,4,3,16,512]{4,3,2,1,0:T(8,128)(2,1)S(1)}, u32[]{:S(2)}, u32[]{:S(2)}) async-start(bf16[8,4,3,16,512]{4,3,2,1,0:T(8,128)(2,1)} %relay.1), calls=%async_computation.3 | async-start | bytes 3145728 | tf_op jit(solution)/shard_map/all_to_all | solution.py:417
  86.8 48.5 %collective-permute-start = (bf16[1,512,512]{2,1,0:T(8,128)(2,1)S(1)}, bf16[1,512,512]{2,1,0:T(8,128)(2,1)S(1)}, u32[]{:S(2)}, u32[]{:S(2)}) collective-permute-start(bf16[1,512,512]{2,1,0:T(8,128)(2,1)S(1)} %copy-done.6), channel_id=1, source_target_pairs={{0,1},{1,2},{2,3},{3,4},{4,5},{5,6},{6,7},{7,8},{8,9},{9,10},{10,1... | collective-permute-start | bytes 1572872 | tf_op jit(solution)/shard_map/ppermute | solution.py:408
  90.8 54.8 %collective-permute-start.1 = (bf16[1,512,512]{2,1,0:T(8,128)(2,1)S(1)}, bf16[1,512,512]{2,1,0:T(8,128)(2,1)S(1)}, u32[]{:S(2)}, u32[]{:S(2)}) collective-permute-start(bf16[1,512,512]{2,1,0:T(8,128)(2,1)S(1)} %copy-done.7), channel_id=1, source_target_pairs={{0,1},{1,2},{2,3},{3,4},{4,5},{5,6},{6,7},{7,8},{8,9},{9,10},{10,1... | collective-permute-start | bytes 1572872 | tf_op jit(solution)/shard_map/ppermute | solution.py:409
  135.4 10.2 %copy-start.8 = (bf16[1,512,512]{2,1,0:T(8,128)(2,1)}, bf16[1,512,512]{2,1,0:T(8,128)(2,1)S(1)}, u32[]{:S(2)}) copy-start(bf16[1,512,512]{2,1,0:T(8,128)(2,1)S(1)} %collective-permute-done.pk_hbm) | copy-start | bytes 1572868
  145.6 0.8 copy-start.9
  146.4 6.2 %copy-start.3 = (bf16[1,512,512]{2,1,0:T(8,128)(2,1)S(1)}, bf16[1,512,512]{2,1,0:T(8,128)(2,1)}, u32[]{:S(2)}) copy-start(bf16[1,512,512]{2,1,0:T(8,128)(2,1)} %q_hbm.3) | copy-start | bytes 1572868
  146.4 6.2 %copy-start.4 = (bf16[512,512]{1,0:T(8,128)(2,1)S(1)}, bf16[512,512]{1,0:T(8,128)(2,1)}, u32[]{:S(2)}) copy-start(bf16[512,512]{1,0:T(8,128)(2,1)} %wc_hbm.1) | copy-start | bytes 1572868
  155.6 14.6 %all-to-all-start.4 = ((bf16[8,64,512]{2,1,0:T(8,128)(2,1)}), bf16[8,64,512]{2,1,0:T(8,128)(2,1)S(1)}, u32[]{:S(2)}, u32[]{:S(2)}) async-start(bf16[8,64,512]{2,1,0:T(8,128)(2,1)} %bitcast.11), calls=%async_computation.4 | async-start | bytes 1048576 | tf_op jit(solution)/shard_map/all_to_all | solution.py:421

commit v6 on v4

v6 whole, which is shorter than its diff:
```python
import functools
import math
import jax
import jax.numpy as jnp
from jax import lax
from jax.experimental import pallas as pl
from jax.experimental.pallas import tpu as pltpu
from jax.sharding import PartitionSpec as P


F32 = jnp.float32
GRADS_STEP = 256
APPLY_STEP = 256
FOLD_VMEM = 53000 << 10
RENORM_VMEM = 53000 << 10
RELAY_VMEM = 53000 << 10
APPLY_VMEM = 50800 << 10
BF16 = jnp.bfloat16
NN = (((1,), (0,)), ((), ()))
NT = (((1,), (1,)), ((), ()))


def dot(a, b, dims):
    return lax.dot_general(a, b, dims, preferred_element_type=F32)


def grads_kernel(
    spot_ref, k_hbm, v_hbm, wg_hbm, wu_hbm, wd_hbm, rate_ref, flag_ref, left_hbm, *refs
):
    rights, (k_s, v_s, wg_s, wu_s, wd_s, left_s, right_s, sem_in, sem_left, sem_right) = refs[:4], refs[4:]
    layer_z = lax.rem(lax.div(spot_ref[0], 8), 4)
    loads = [
        pltpu.make_async_copy(src.at[0], dst, sem_in.at[i])
        for i, (src, dst) in enumerate(
            ((v_hbm, v_s), (wd_hbm, wd_s), (k_hbm, k_s), (wg_hbm, wg_s), (wu_hbm, wu_s))
        )
    ]
    for load in loads:
        load.start()
    step = GRADS_STEP
    stores = []

    def put(piece, which, start):
        for n in range(step // 16):
            z, y = divmod(start // 16 + n, 8)
            for c in range(4):
                block = piece[n * 16 : n * 16 + 16, c * 128 : (c + 1) * 128]
                row = which * 32 + (c % 2) * 16
                (left_s, right_s)[c // 2][z, y, row : row + 16, :] = block

    def ship(phase, low, high, top):
        for z in range(4):
            store = pltpu.make_async_copy(
                left_s.at[z, :, low:top], left_hbm.at[:, z, low:top], sem_left.at[phase, z]
            )
            store.start()
            stores.append(store)
        for d in range(4):
            store = pltpu.make_async_copy(
                right_s.at[lax.rem(layer_z + d, 4), :, low:high],
                rights[d].at[:, low:high],
                sem_right.at[phase, d],
            )
            store.start()
            stores.append(store)

    rate = rate_ref[...]
    coeff = flag_ref[...].astype(F32) * rate
    total = jnp.sum(rate, axis=1, keepdims=True)
    high = total.astype(BF16)
    low = (total - high.astype(F32)).astype(BF16)
    row = lax.broadcasted_iota(jnp.int32, (8, 128), 0)
    tail = jnp.where(row == 0, high.astype(F32), jnp.where(row == 1, low.astype(F32), 0.0))
    left_s[:, :, 96:104, :] = jnp.broadcast_to(tail.astype(BF16)[None, None], (4, 8, 8, 128))
    loads[0].wait()
    scaled = (coeff * v_s[...].T.astype(F32)).astype(BF16)
    loads[1].wait()
    down = wd_s[...].T
    for load in loads[2:]:
        load.wait()
    key = k_s[...]
    hidden = []
    for start in range(0, 512, step):
        rows = slice(start, start + step)
        gate = dot(wg_s[rows, :], key, NT)
        up = dot(wu_s[rows, :], key, NT)
        back = dot(down[rows], scaled, NN)
        sigma = jax.nn.sigmoid(gate)
        active = gate * sigma
        hidden.append((active * up).astype(BF16))
        grad_gate = (back * up * sigma * (1.0 + gate * (1.0 - sigma))).astype(BF16)
        grad_up = (back * active).astype(BF16)
        put(dot(grad_gate, key, NN).astype(BF16), 0, start)
        put(dot(grad_up, key, NN).astype(BF16), 1, start)
    ship(0, 0, 64, 64)
    hidden = jnp.concatenate(hidden, axis=0)
    for start in range(0, 512, step):
        rows = slice(start, start + step)
        put(dot(scaled[rows], hidden, NT).astype(BF16), 2, start)
    ship(1, 64, 96, 104)
    for store in stores:
        store.wait()


def grads(spot, k, v, rate, flag, wg, wu, wd):
    sm = pl.BlockSpec(memory_space=pltpu.SMEM)
    vm = pl.BlockSpec(memory_space=pltpu.VMEM)
    hb = pl.BlockSpec(memory_space=pltpu.HBM)
    return pl.pallas_call(
        grads_kernel,
        out_shape=(jax.ShapeDtypeStruct((8, 4, 104, 128), BF16),)
        + (jax.ShapeDtypeStruct((8, 96, 128), BF16),) * 4,
        in_specs=[sm] + [hb] * 5 + [vm, vm],
        out_specs=(hb,) * 5,
        scratch_shapes=[pltpu.VMEM((512, 512), BF16)] * 5
        + [
            pltpu.VMEM((4, 8, 104, 128), BF16),
            pltpu.VMEM((4, 8, 96, 128), BF16),
            pltpu.SemaphoreType.DMA((5,)),
            pltpu.SemaphoreType.DMA((2, 4)),
            pltpu.SemaphoreType.DMA((2, 4)),
        ],
        name="grads",
    )(spot, k, v, wg, wu, wd, rate, flag)


def fold_kernel(spot_ref, left_ref, own, one, two, three, right_hbm, *refs):
    lefts, (in_s, left_s, right_s, sem_in, sem_out) = refs[:4], refs[4:]
    layer_z = lax.rem(lax.div(spot_ref[0], 8), 4)
    loads = [
        pltpu.make_async_copy(src, in_s.at[i], sem_in.at[i])
        for i, src in enumerate((own, one, two, three))
    ]
    for load in loads:
        load.start()
    for z in range(4):
        left_s[z, :96, :] = jnp.sum(left_ref[:, z, :96, :].astype(F32), axis=0).astype(BF16)
    tail = jnp.sum(left_ref[:, 0, 96:104, :].astype(F32), axis=0)
    total = jnp.broadcast_to(tail[0:1] + tail[1:2], (8, 128))
    high = total.astype(BF16).astype(F32)
    row = lax.broadcasted_iota(jnp.int32, (8, 128), 0)
    tail = jnp.where(row == 0, high, jnp.where(row == 1, total - high, 0.0)).astype(BF16)
    left_s[:, 96:104, :] = jnp.broadcast_to(tail[None], (4, 8, 128))
    stores = [
        pltpu.make_async_copy(left_s.at[lax.rem(layer_z + d, 4)], lefts[d], sem_out.at[d])
        for d in range(4)
    ]
    for store in stores:
        store.start()
    for load in loads:
        load.wait()
    right_s[...] = jnp.sum(in_s[...].astype(F32), axis=0).astype(BF16)
    stores.append(pltpu.make_async_copy(right_s, right_hbm, sem_out.at[4]))
    stores[4].start()
    for store in stores:
        store.wait()


def fold(spot, left, rights):
    sm = pl.BlockSpec(memory_space=pltpu.SMEM)
    vm = pl.BlockSpec(memory_space=pltpu.VMEM)
    hb = pl.BlockSpec(memory_space=pltpu.HBM)
    return pl.pallas_call(
        fold_kernel,
        out_shape=(jax.ShapeDtypeStruct((8, 96, 128), BF16),)
        + (jax.ShapeDtypeStruct((104, 128), BF16),) * 4,
        in_specs=[sm, vm] + [hb] * 4,
        out_specs=(hb,) * 5,
        scratch_shapes=[
            pltpu.VMEM((4, 8, 96, 128), BF16),
            pltpu.VMEM((4, 104, 128), BF16),
            pltpu.VMEM((8, 96, 128), BF16),
            pltpu.SemaphoreType.DMA((4,)),
            pltpu.SemaphoreType.DMA((5,)),
        ],
        compiler_params=pltpu.CompilerParams(vmem_limit_bytes=FOLD_VMEM),
        name="fold",
    )(spot, left, *rights)


def renorm_kernel(
    spot_ref, right_ref, own, one, two, three, wg, wu, wd, left_hbm, right_hbm,
    in_s, old_s, left_s, right_s, sem_in, sem_w, sem_left, sem_right, *, update_len,
):
    rows = pl.ds(pl.multiple_of(lax.rem(spot_ref[0], 32) * 16, 16), 16)
    loads = [
        pltpu.make_async_copy(ref.at[0, rows], old_s.at[i], sem_w.at[i])
        for i, ref in enumerate((wg, wu, wd))
    ] + [
        pltpu.make_async_copy(src, in_s.at[i], sem_in.at[i])
        for i, src in enumerate((own, one, two, three))
    ]
    for load in loads:
        load.start()
    right = jnp.sum(right_ref[...].astype(F32), axis=0)
    for load in loads:
        load.wait()
    left = jnp.sum(in_s[...].astype(F32), axis=0)
    total = left[96:97, 0:1] + left[97:98, 0:1]
    factor = 2.0 * update_len / (total * math.sqrt(update_len * 512))
    for which in range(3):
        row = which * 32
        summed = jnp.concatenate(
            [half[row + c * 16 : row + c * 16 + 16] for half in (left, right) for c in range(2)], axis=1
        )
        old = old_s[which].astype(F32)
        updated = old + summed * factor
        old_norm = jnp.sqrt(jnp.sum(old * old, axis=-1, keepdims=True))
        new_norm = jnp.sqrt(jnp.sum(updated * updated, axis=-1, keepdims=True) + 1e-6)
        fresh = (updated * (old_norm / new_norm)).astype(BF16)
        left_s[which] = fresh[:, :256]
        right_s[which] = fresh[:, 256:]
    stores = [pltpu.make_async_copy(right_s, right_hbm.at[d], sem_right.at[d]) for d in range(16)]
    stores.append(pltpu.make_async_copy(left_s, left_hbm, sem_left))
    for store in stores:
        store.start()
    for store in stores:
        store.wait()


def renorm(spot, right, lefts, wg, wu, wd, update_len):
    sm = pl.BlockSpec(memory_space=pltpu.SMEM)
    vm = pl.BlockSpec(memory_space=pltpu.VMEM)
    hb = pl.BlockSpec(memory_space=pltpu.HBM)
    return pl.pallas_call(
        functools.partial(renorm_kernel, update_len=update_len),
        out_shape=(
            jax.ShapeDtypeStruct((3, 16, 256), BF16),
            jax.ShapeDtypeStruct((16, 3, 16, 256), BF16),
        ),
        in_specs=[sm, vm] + [hb] * 7,
        out_specs=(hb, hb),
        scratch_shapes=[
            pltpu.VMEM((4, 104, 128), BF16),
            pltpu.VMEM((3, 16, 512), BF16),
            pltpu.VMEM((3, 16, 256), BF16),
            pltpu.VMEM((3, 16, 256), BF16),
            pltpu.SemaphoreType.DMA((4,)),
            pltpu.SemaphoreType.DMA((3,)),
            pltpu.SemaphoreType.DMA,
            pltpu.SemaphoreType.DMA((16,)),
        ],
        compiler_params=pltpu.CompilerParams(vmem_limit_bytes=RENORM_VMEM),
        name="renorm",
    )(spot, right, *lefts, wg, wu, wd)


def attend_kernel(
    pos_ref, doc_ref, q_hbm, k_hbm, v_hbm, pk_hbm, pv_hbm, out_hbm,
    q_ref, k_ref, v_ref, pk_ref, pv_ref, att_s, sem,
):
    base = pos_ref[0] * 512
    loads = [
        pltpu.make_async_copy(src.at[0], dst, sem.at[i])
        for i, (src, dst) in enumerate(
            (
                (q_hbm, q_ref),
                (k_hbm, k_ref),
                (v_hbm, v_ref),
                (pk_hbm, pk_ref),
                (pv_hbm, pv_ref),
            )
        )
    ]
    for load in loads:
        load.start()

    for load in loads:
        load.wait()
    step = 128
    scale = 1.0 / math.sqrt(512)
    doc = (jnp.broadcast_to(doc_ref[...], (8, 512)) - base).T[:, :1]
    for start in range(0, 512, step):
        rows = slice(start, start + step)
        q = q_ref[rows, :]
        keys = jnp.concatenate([pk_ref[start:, :], k_ref[: start + step, :]], axis=0)
        vals = jnp.concatenate([pv_ref[start:, :], v_ref[: start + step, :]], axis=0)
        width = 512 + step
        s = dot(q, keys, NT) * scale
        at = lax.broadcasted_iota(jnp.int32, (step, width), 0) + start
        to = lax.broadcasted_iota(jnp.int32, (step, width), 1) + (start - 512)
        ok = (to <= at) & (to > at - 512) & (to >= doc[rows])
        s = jnp.where(ok, s, -1e30)
        top = jnp.max(s, axis=-1, keepdims=True)
        e = jnp.exp(s - top)
        prob = (e / jnp.sum(e, axis=-1, keepdims=True)).astype(BF16)
        att_s[rows, :] = dot(prob, vals, NN)
    store = pltpu.make_async_copy(att_s, out_hbm.at[0], sem.at[5])
    store.start()
    store.wait()


def attend(pos, q, k, v, doc, pk, pv):
    vm = pl.BlockSpec(memory_space=pltpu.VMEM)
    hb = pl.BlockSpec(memory_space=pltpu.HBM)
    return pl.pallas_call(
        attend_kernel,
        out_shape=jax.ShapeDtypeStruct((2, 512, 512), F32),
        in_specs=[pl.BlockSpec(memory_space=pltpu.SMEM), vm] + [hb] * 5,
        out_specs=hb,
        scratch_shapes=[pltpu.VMEM((512, 512), BF16)] * 5
        + [
            pltpu.VMEM((512, 512), F32),
            pltpu.SemaphoreType.DMA((6,)),
        ],
        name="attend",
    )(pos, doc, q, k, v, pk, pv)


def relay_kernel(
    spot_ref, right, zero, one, two, three, wg, wu, wd, left_hbm, right_hbm,
    left_s, right_s, sem_in, sem_out, sem_right,
):
    first = spot_ref[0] < 32
    layer_z = lax.rem(lax.div(spot_ref[0], 8), 4)
    column = lax.rem(spot_ref[0], 8)

    def send(source):
        store = pltpu.make_async_copy(source, right_hbm, sem_right)
        store.start()
        copies = [pltpu.make_async_copy(left_s, left_hbm.at[d], sem_out.at[d]) for d in range(8)]
        for copy in copies:
            copy.start()
        for copy in copies:
            copy.wait()
        store.wait()

    @pl.when(first)
    def _():
        copies = []
        for i, ref in enumerate((wg, wu, wd)):
            copies.append(
                pltpu.make_async_copy(ref.at[:, column, :, pl.ds(0, 256)], left_s.at[:, i], sem_in.at[i])
            )
            copies.append(
                pltpu.make_async_copy(
                    ref.at[layer_z, :, :, pl.ds(256, 256)], right_s.at[:, i], sem_in.at[i + 3]
                )
            )
        for copy in copies:
            copy.start()
        for copy in copies:
            copy.wait()
        send(right_s)

    @pl.when(jnp.logical_not(first))
    def _():
        copies = [
            pltpu.make_async_copy(src, left_s.at[lax.rem(layer_z + 4 - d, 4)], sem_in.at[d])
            for d, src in enumerate((zero, one, two, three))
        ]
        for copy in copies:
            copy.start()
        for copy in copies:
            copy.wait()
        send(right.at[pl.ds(0, 8)])


def relay(spot, right, lefts, wg, wu, wd):
    sm = pl.BlockSpec(memory_space=pltpu.SMEM)
    vm = pl.BlockSpec(memory_space=pltpu.VMEM)
    hb = pl.BlockSpec(memory_space=pltpu.HBM)
    return pl.pallas_call(
        relay_kernel,
        out_shape=(
            jax.ShapeDtypeStruct((8, 4, 3, 16, 256), BF16),
            jax.ShapeDtypeStruct((8, 3, 16, 256), BF16),
        ),
        in_specs=[sm, vm] + [hb] * 7,
        out_specs=(hb, hb),
        scratch_shapes=[
            pltpu.VMEM((4, 3, 16, 256), BF16),
            pltpu.VMEM((8, 3, 16, 256), BF16),
            pltpu.SemaphoreType.DMA((6,)),
            pltpu.SemaphoreType.DMA((8,)),
            pltpu.SemaphoreType.DMA,
        ],
        compiler_params=pltpu.CompilerParams(vmem_limit_bytes=RELAY_VMEM),
        name="relay",
    )(spot, right, *lefts, *(x.reshape(4, 8, 16, 512) for x in (wg, wu, wd)))


def apply_kernel(
    spot_ref, left, own, one, two, three, q_hbm, att_hbm, wc_hbm, mixed_hbm, part_hbm,
    right, q_s, att_s, wc_s, mixed_s, part_s, sem_in, sem_right, sem_out,
):
    layer_z = lax.rem(lax.div(spot_ref[0], 8), 4)
    slabs = [
        pltpu.make_async_copy(src, right.at[lax.rem(layer_z + 4 - d, 4)], sem_right.at[d])
        for d, src in enumerate((own, one, two, three))
    ]
    for slab in slabs:
        slab.start()
    loads = [
        pltpu.make_async_copy(src, dst, sem_in.at[i])
        for i, (src, dst) in enumerate(((q_hbm.at[0], q_s), (att_hbm.at[0], att_s), (wc_hbm, wc_s)))
    ]
    for load in loads:
        load.start()

    def weight(i, low, count):
        spots = [(z, y) for z in range(low // 128, (low + count) // 128) for y in range(8)]
        return jnp.concatenate(
            [
                jnp.concatenate([left[y, z, i] for z, y in spots], axis=0),
                jnp.concatenate([right[z, y, i] for z, y in spots], axis=0),
            ],
            axis=1,
        )

    step = APPLY_STEP
    loads[0].wait()
    for slab in slabs:
        slab.wait()
    q = q_s[...]
    hidden = []
    for start in range(0, 512, step):
        gate = dot(q, weight(0, start, step), NT)
        up = dot(q, weight(1, start, step), NT)
        hidden.append((gate * jax.nn.sigmoid(gate) * up).astype(BF16))
    hidden = jnp.concatenate(hidden, axis=1)
    loads[1].wait()
    for start in range(0, 512, step):
        cols = slice(start, start + step)
        mixed_s[:, cols] = (att_s[:, cols] + dot(hidden, weight(2, start, step), NT)).astype(BF16)
    stores = [pltpu.make_async_copy(mixed_s, mixed_hbm.at[0], sem_out.at[0])]
    stores[0].start()
    loads[2].wait()
    mixed = mixed_s[...]
    for start in range(0, 512, step):
        cols = slice(start, start + step)
        part_s[:, cols] = dot(mixed, wc_s[:, cols], NN).astype(BF16)
    stores.append(pltpu.make_async_copy(part_s, part_hbm, sem_out.at[1]))
    stores[1].start()
    for store in stores:
        store.wait()


def fast_apply(spot, left, rights, q, att, wc):
    vm = pl.BlockSpec(memory_space=pltpu.VMEM)
    hb = pl.BlockSpec(memory_space=pltpu.HBM)
    return pl.pallas_call(
        apply_kernel,
        out_shape=(
            jax.ShapeDtypeStruct((1, 512, 512), BF16),
            jax.ShapeDtypeStruct((512, 512), BF16),
        ),
        in_specs=[pl.BlockSpec(memory_space=pltpu.SMEM), vm] + [hb] * 7,
        out_specs=(hb, hb),
        scratch_shapes=[
            pltpu.VMEM((4, 8, 3, 16, 256), BF16),
            pltpu.VMEM((512, 512), BF16),
            pltpu.VMEM((512, 512), F32),
            pltpu.VMEM((512, 512), BF16),
            pltpu.VMEM((512, 512), BF16),
            pltpu.VMEM((512, 512), BF16),
            pltpu.SemaphoreType.DMA((3,)),
            pltpu.SemaphoreType.DMA((4,)),
            pltpu.SemaphoreType.DMA((2,)),
        ],
        compiler_params=pltpu.CompilerParams(vmem_limit_bytes=APPLY_VMEM),
        name="fast_apply",
    )(spot, left, *rights, q, att, wc)


def combine_kernel(recv_ref, flag_ref, out_ref):
    summed = jnp.sum(recv_ref[...].astype(F32), axis=0)
    flag = jnp.broadcast_to(flag_ref[...].astype(F32), (8, 64)).T[:, :1]
    out_ref[0] = (summed * flag).astype(BF16)


def combine(recv, flag):
    vm = pl.BlockSpec(memory_space=pltpu.VMEM)
    return pl.pallas_call(
        combine_kernel,
        out_shape=jax.ShapeDtypeStruct((1, 64, 512), BF16),
        in_specs=[vm, vm],
        out_specs=vm,
        compiler_params=pltpu.CompilerParams(vmem_limit_bytes=4 << 20),
        name="combine",
    )(recv, flag)


def layer(q, k, v, rate, doc_start, flag, wg, wu, wd, wc):
    seq_count = lax.axis_size("seq")
    half = seq_count // 2
    index = lax.axis_index("seq").astype(jnp.int32)
    place = lambda z, y: z * 8 + y
    slabs = [[place(z + lift, y) for lift in (0, 4) for y in range(8)] for z in range(4)]
    rows = [[place(z, y) for y in range(8)] for z in range(8)]
    route = [(i - 1, i) for i in range(1, seq_count)]

    def turn(block, d):
        pairs = [
            (place(z + lift, y), place((z + d) % 4 + lift, y))
            for lift in (0, 4)
            for z in range(4)
            for y in range(8)
        ]
        return lax.ppermute(block, "seq", pairs)

    def lift_up(block, d):
        pairs = [(place(z, y), place((z + d) % 4 + 4, y)) for z in range(4) for y in range(8)]
        return lax.ppermute(block, "seq", pairs)

    spot = index[None]
    pk = lax.ppermute(k, "seq", route)
    pv = lax.ppermute(v, "seq", route)
    left, *rights = grads(spot, k, v, rate, flag[None], wg, wu, wd)
    left = lax.all_to_all(left, "seq", 0, 0, axis_index_groups=rows)
    rights = [rights[0]] + [turn(rights[d], d) for d in range(1, 4)]
    right, *lefts = fold(spot, left, rights)
    right = lax.all_to_all(right, "seq", 0, 0, axis_index_groups=rows)
    lefts = [lefts[0]] + [turn(lefts[d], d) for d in range(1, 4)]
    left, right = renorm(spot, right, lefts, wg, wu, wd, 512 * half)
    right = lax.all_to_all(right, "seq", 0, 0, axis_index_groups=slabs)
    lefts = [lift_up(left, d) for d in range(4)]
    left, right = relay(spot, right, lefts, wg, wu, wd)
    left = lax.all_to_all(left, "seq", 0, 0, axis_index_groups=rows)
    rights = [right] + [turn(right, d) for d in range(1, 4)]
    att = attend(spot, q, k, v, doc_start[None], pk, pv)
    mixed, part = fast_apply(spot, left, rights, q, att, wc)
    flags = lax.dynamic_slice_in_dim(flag, lax.axis_index("head") * 64, 64, 0)[None]
    got = lax.all_to_all(part.reshape(8, 64, 512), "head", 0, 0)
    return mixed, combine(got, flags)


def solution(mesh):
    placed = (
        P("head", "seq", None),
        P("head", "seq", None),
        P("head", "seq", None),
        P("head", "seq"),
        P("seq"),
        P("seq"),
        P("head", None, None),
        P("head", None, None),
        P("head", None, None),
        P("head", None),
    )
    return jax.shard_map(
        layer,
        mesh=mesh,
        in_specs=placed,
        out_specs=(P("head", "seq", None), P("seq", "head", None)),
        check_vma=False,
    )
```

time: 177 us -> 164 us (0.927)
  the two profiles are of different devices: /device:TPU:1 before, /device:TPU:128 now
where the time goes in v6:
time: 164 us; the launch traced here: 163 us
  starting transfers between devices  82.3 us (50%)
  waiting for transfers between devices  55.3 us (34%)
  Pallas kernels  21.9 us (13%)
  local copies, waits for them, and re-layouts  2.5 us (2%)
    ppermute x9, starting transfers between devices, turn(): return lax.ppermute(block, 'seq', pairs)  28.7 us
    ppermute x9, waiting for transfers between devices, turn(): return lax.ppermute(block, 'seq', pairs)  16.6 us
    ppermute x1, waiting for transfers between devices, layer(): pk = lax.ppermute(k, 'seq', route)  13.7 us
    all_to_all x1, starting transfers between devices, layer(): right = lax.all_to_all(right, 'seq', 0, 0, axis_index_groups=slabs)  13.4 us
    all_to_all x2, starting transfers between devices, layer(): left = lax.all_to_all(left, 'seq', 0, 0, axis_index_groups=rows)  12.9 us
    ppermute x4, starting transfers between devices, lift_up(): return lax.ppermute(block, 'seq', pairs)  12.3 us
    all_to_all x1, waiting for transfers between devices, layer(): got = lax.all_to_all(part.reshape(8, 64, 512), 'head', 0, 0)  9.56 us
    ppermute x1, waiting for transfers between devices, layer(): pv = lax.ppermute(v, 'seq', route)  9.29 us
  transfers between devices with their start and end apart: 20, of which 12 were waited for; matrix products, arithmetic and copies ran while one was open for 0% of the time, Pallas kernels for 4%

profile of v6, /device:TPU:128, one launch (start us, length us, event | category | flops | bytes accessed | tf_op | source)
XLA Modules:
  0.0 162.9 jit_solution(7154099226077150054)
XLA Ops:
  0.6 5.6 %grads.1 = (bf16[8,4,104,128]{3,2,1,0:T(8,128)(2,1)}, bf16[8,96,128]{2,1,0:T(8,128)(2,1)}, bf16[8,96,128]{2,1,0:T(8,128)(2,1)}, bf16[8,96,128]{2,1,0:T(8,128)(2,1)}, bf16[8,96,128]{2,1,0:T(8,128)(2,1)}) custom-call(s32[1]{0:T(128)} %bitcast.spot_ref.pos_ref, bf16[1,512,512]{2,1,0:T(8,128)(2,1)} %k_hbm.3, bf16[1,512,512]{2,1,0:T(8,128)(2,1)} %v_hbm.3, ...), custom_call_target="tpu_custom_call" | custom-call | tf_op jit(solution)/shard_map/grads/pallas_call | solution.py:109
  6.3 7.2 %all-to-all-start = ((bf16[8,4,104,128]{3,2,1,0:T(8,128)(2,1)}), bf16[8,4,104,128]{3,2,1,0:T(8,128)(2,1)S(1)}, u32[]{:S(2)}, u32[]{:S(2)}) async-start(bf16[8,4,104,128]{3,2,1,0:T(8,128)(2,1)} %get-tuple-element.18), calls=%async_computation | async-start | bytes 1703936 | tf_op jit(solution)/shard_map/all_to_all | solution.py:510
  13.5 4.3 %collective-permute-start = (bf16[8,96,128]{2,1,0:T(8,128)(2,1)}, bf16[8,96,128]{2,1,0:T(8,128)(2,1)S(1)}, u32[]{:S(2)}, u32[]{:S(2)}) collective-permute-start(bf16[8,96,128]{2,1,0:T(8,128)(2,1)} %get-tuple-element.20), channel_id=1, source_target_pairs={{0,8},{1,9},{2,10},{3,11},{4,12},{5,13},{6,14},{7,15},{8,16},{9,17... | collective-permute-start | bytes 589832 | tf_op jit(solution)/shard_map/ppermute | solution.py:500
  17.8 1.9 %collective-permute-start.1 = (bf16[8,96,128]{2,1,0:T(8,128)(2,1)}, bf16[8,96,128]{2,1,0:T(8,128)(2,1)S(1)}, u32[]{:S(2)}, u32[]{:S(2)}) collective-permute-start(bf16[8,96,128]{2,1,0:T(8,128)(2,1)} %get-tuple-element.21), channel_id=1, source_target_pairs={{0,16},{1,17},{2,18},{3,19},{4,20},{5,21},{6,22},{7,23},{8,24},{9,... | collective-permute-start | bytes 589832 | tf_op jit(solution)/shard_map/ppermute | solution.py:500
  19.7 3.4 %collective-permute-start.2 = (bf16[8,96,128]{2,1,0:T(8,128)(2,1)}, bf16[8,96,128]{2,1,0:T(8,128)(2,1)S(1)}, u32[]{:S(2)}, u32[]{:S(2)}) collective-permute-start(bf16[8,96,128]{2,1,0:T(8,128)(2,1)} %get-tuple-element.22), channel_id=1, source_target_pairs={{0,24},{1,25},{2,26},{3,27},{4,28},{5,29},{6,30},{7,31},{8,0},{9,1... | collective-permute-start | bytes 589832 | tf_op jit(solution)/shard_map/ppermute | solution.py:500
  23.1 7.2 %collective-permute-done.1.two = bf16[8,96,128]{2,1,0:T(8,128)(2,1)S(1)} collective-permute-done((bf16[8,96,128]{2,1,0:T(8,128)(2,1)}, bf16[8,96,128]{2,1,0:T(8,128)(2,1)S(1)}, u32[]{:S(2)}, u32[]{:S(2)}) %collective-permute-start.1) | collective-permute-done | bytes 196640 | tf_op jit(solution)/shard_map/ppermute | solution.py:500
  30.3 4.1 %collective-permute-done.2.three = bf16[8,96,128]{2,1,0:T(8,128)(2,1)S(1)} collective-permute-done((bf16[8,96,128]{2,1,0:T(8,128)(2,1)}, bf16[8,96,128]{2,1,0:T(8,128)(2,1)S(1)}, u32[]{:S(2)}, u32[]{:S(2)}) %collective-permute-start.2) | collective-permute-done | bytes 196640 | tf_op jit(solution)/shard_map/ppermute | solution.py:500
  34.4 3.6 %all-to-all-done.left_ref = bf16[8,4,104,128]{3,2,1,0:T(8,128)(2,1)S(1)} async-done(((bf16[8,4,104,128]{3,2,1,0:T(8,128)(2,1)}), bf16[8,4,104,128]{3,2,1,0:T(8,128)(2,1)S(1)}, u32[]{:S(2)}, u32[]{:S(2)}) %all-to-all-start) | async-done | bytes 852000 | tf_op jit(solution)/shard_map/all_to_all | solution.py:510
  39.0 2.1 %fold.1 = (bf16[8,96,128]{2,1,0:T(8,128)(2,1)}, bf16[104,128]{1,0:T(8,128)(2,1)S(1)}, bf16[104,128]{1,0:T(8,128)(2,1)S(1)}, bf16[104,128]{1,0:T(8,128)(2,1)S(1)}, bf16[104,128]{1,0:T(8,128)(2,1)S(1)}) custom-call(s32[1]{0:T(128)} %bitcast.spot_ref.pos_ref, bf16[8,4,104,128]{3,2,1,0:T(8,128)(2,1)S(1)} %all-to-all-done.left_ref, ...), custom_call_target="tpu_custom_call" | custom-call | tf_op jit(solution)/shard_map/fold/pallas_call | solution.py:163
  41.1 3.4 %all-to-all-start.1 = ((bf16[8,96,128]{2,1,0:T(8,128)(2,1)}), bf16[8,96,128]{2,1,0:T(8,128)(2,1)S(1)}, u32[]{:S(2)}, u32[]{:S(2)}) async-start(bf16[8,96,128]{2,1,0:T(8,128)(2,1)} %get-tuple-element.23), calls=%async_computation.1 | async-start | bytes 393216 | tf_op jit(solution)/shard_map/all_to_all | solution.py:513
  44.5 4.3 %collective-permute-start.3 = (bf16[104,128]{1,0:T(8,128)(2,1)S(1)}, bf16[104,128]{1,0:T(8,128)(2,1)S(1)}, u32[]{:S(2)}, u32[]{:S(2)}) collective-permute-start(bf16[104,128]{1,0:T(8,128)(2,1)S(1)} %get-tuple-element.25), channel_id=1, source_target_pairs={{0,8},{1,9},{2,10},{3,11},{4,12},{5,13},{6,14},{7,15},{8,16},{9,17... | collective-permute-start | bytes 79880 | tf_op jit(solution)/shard_map/ppermute | solution.py:500
  48.8 3.2 %collective-permute-start.4 = (bf16[104,128]{1,0:T(8,128)(2,1)S(1)}, bf16[104,128]{1,0:T(8,128)(2,1)S(1)}, u32[]{:S(2)}, u32[]{:S(2)}) collective-permute-start(bf16[104,128]{1,0:T(8,128)(2,1)S(1)} %get-tuple-element.26), channel_id=1, source_target_pairs={{0,16},{1,17},{2,18},{3,19},{4,20},{5,21},{6,22},{7,23},{8,24},{9,... | collective-permute-start | bytes 79880 | tf_op jit(solution)/shard_map/ppermute | solution.py:500
  52.0 2.1 %collective-permute-start.5 = (bf16[104,128]{1,0:T(8,128)(2,1)S(1)}, bf16[104,128]{1,0:T(8,128)(2,1)S(1)}, u32[]{:S(2)}, u32[]{:S(2)}) collective-permute-start(bf16[104,128]{1,0:T(8,128)(2,1)S(1)} %get-tuple-element.27), channel_id=1, source_target_pairs={{0,24},{1,25},{2,26},{3,27},{4,28},{5,29},{6,30},{7,31},{8,0},{9,1... | collective-permute-start | bytes 79880 | tf_op jit(solution)/shard_map/ppermute | solution.py:500
  55.4 2.3 %collective-permute-done.5.three = bf16[104,128]{1,0:T(8,128)(2,1)S(1)} collective-permute-done((bf16[104,128]{1,0:T(8,128)(2,1)S(1)}, bf16[104,128]{1,0:T(8,128)(2,1)S(1)}, u32[]{:S(2)}, u32[]{:S(2)}) %collective-permute-start.5) | collective-permute-done | bytes 26656 | tf_op jit(solution)/shard_map/ppermute | solution.py:500
  57.8 1.9 %renorm.1 = (bf16[3,16,256]{2,1,0:T(8,128)(2,1)S(1)}, bf16[16,3,16,256]{3,2,1,0:T(8,128)(2,1)}) custom-call(s32[1]{0:T(128)} %bitcast.spot_ref.pos_ref, bf16[8,96,128]{2,1,0:T(8,128)(2,1)S(1)} %all-to-all-done.1.right_ref, bf16[104,128]{1,0:T(8,128)(2,1)S(1)} %get-tuple-element.24.own, bf16[104,128]{1,0:T(8,128)(2,1)S(1)} %collective-permute-done.3.one, ...), custom_call_target="tpu_custom_call" | custom-call | tf_op jit(solution)/shard_map/renorm/pallas_call | solution.py:225
  59.7 13.4 %all-to-all-start.2 = ((bf16[16,3,16,256]{3,2,1,0:T(8,128)(2,1)}), bf16[16,3,16,256]{3,2,1,0:T(8,128)(2,1)S(1)}, u32[]{:S(2)}, u32[]{:S(2)}) async-start(bf16[16,3,16,256]{3,2,1,0:T(8,128)(2,1)} %get-tuple-element.28), calls=%async_computation.2 | async-start | bytes 786432 | tf_op jit(solution)/shard_map/all_to_all | solution.py:516
  73.1 6.6 %collective-permute-start.9 = (bf16[3,16,256]{2,1,0:T(8,128)(2,1)S(1)}, bf16[3,16,256]{2,1,0:T(8,128)(2,1)S(1)}, u32[]{:S(2)}, u32[]{:S(2)}) collective-permute-start(bf16[3,16,256]{2,1,0:T(8,128)(2,1)S(1)} %get-tuple-element.29), channel_id=1, source_target_pairs={{0,56},{1,57},{2,58},{3,59},{4,60},{5,61},{6,62},{7,63},{8,32},{9,... | collective-permute-start | bytes 73736 | tf_op jit(solution)/shard_map/ppermute | solution.py:504
  79.7 1.5 collective-permute-start.8
  81.2 2.9 %collective-permute-start.7 = (bf16[3,16,256]{2,1,0:T(8,128)(2,1)S(1)}, bf16[3,16,256]{2,1,0:T(8,128)(2,1)S(1)}, u32[]{:S(2)}, u32[]{:S(2)}) collective-permute-start(bf16[3,16,256]{2,1,0:T(8,128)(2,1)S(1)} %get-tuple-element.29), channel_id=1, source_target_pairs={{0,40},{1,41},{2,42},{3,43},{4,44},{5,45},{6,46},{7,47},{8,48},{9,... | collective-permute-start | bytes 73736 | tf_op jit(solution)/shard_map/ppermute | solution.py:504
  89.3 5.6 %all-to-all-start.3 = ((bf16[8,4,3,16,256]{4,3,2,1,0:T(8,128)(2,1)}), bf16[8,4,3,16,256]{4,3,2,1,0:T(8,128)(2,1)S(1)}, u32[]{:S(2)}, u32[]{:S(2)}) async-start(bf16[8,4,3,16,256]{4,3,2,1,0:T(8,128)(2,1)} %get-tuple-element.30), calls=%async_computation.3 | async-start | bytes 1572864 | tf_op jit(solution)/shard_map/all_to_all | solution.py:519
  94.9 3.9 %collective-permute-start.13 = (bf16[1,512,512]{2,1,0:T(8,128)(2,1)S(1)}, bf16[1,512,512]{2,1,0:T(8,128)(2,1)S(1)}, u32[]{:S(2)}, u32[]{:S(2)}) collective-permute-start(bf16[1,512,512]{2,1,0:T(8,128)(2,1)S(1)} %copy-done.6), channel_id=1, source_target_pairs={{0,1},{1,2},{2,3},{3,4},{4,5},{5,6},{6,7},{7,8},{8,9},{9,10},{10,1... | collective-permute-start | bytes 1572872 | tf_op jit(solution)/shard_map/ppermute | solution.py:507
  98.9 3.4 %collective-permute-start.14 = (bf16[1,512,512]{2,1,0:T(8,128)(2,1)S(1)}, bf16[1,512,512]{2,1,0:T(8,128)(2,1)S(1)}, u32[]{:S(2)}, u32[]{:S(2)}) collective-permute-start(bf16[1,512,512]{2,1,0:T(8,128)(2,1)S(1)} %copy-done.7), channel_id=1, source_target_pairs={{0,1},{1,2},{2,3},{3,4},{4,5},{5,6},{6,7},{7,8},{8,9},{9,10},{10,1... | collective-permute-start | bytes 1572872 | tf_op jit(solution)/shard_map/ppermute | solution.py:508
  102.3 2.5 %collective-permute-start.12 = (bf16[8,3,16,256]{3,2,1,0:T(8,128)(2,1)S(1)}, bf16[8,3,16,256]{3,2,1,0:T(8,128)(2,1)S(1)}, u32[]{:S(2)}, u32[]{:S(2)}) collective-permute-start(bf16[8,3,16,256]{3,2,1,0:T(8,128)(2,1)S(1)} %get-tuple-element.31.own), channel_id=1, source_target_pairs={{0,24},{1,25},{2,26},{3,27},{4,28},{5,29},{6,30},{7,31},{8,0},{9,1... | collective-permute-start | bytes 589832 | tf_op jit(solution)/shard_map/ppermute | solution.py:500
  104.7 5.2 %collective-permute-start.11 = (bf16[8,3,16,256]{3,2,1,0:T(8,128)(2,1)S(1)}, bf16[8,3,16,256]{3,2,1,0:T(8,128)(2,1)S(1)}, u32[]{:S(2)}, u32[]{:S(2)}) collective-permute-start(bf16[8,3,16,256]{3,2,1,0:T(8,128)(2,1)S(1)} %get-tuple-element.31.own), channel_id=1, source_target_pairs={{0,16},{1,17},{2,18},{3,19},{4,20},{5,21},{6,22},{7,23},{8,24},{9,... | collective-permute-start | bytes 589832 | tf_op jit(solution)/shard_map/ppermute | solution.py:500
  109.9 1.9 %collective-permute-start.10 = (bf16[8,3,16,256]{3,2,1,0:T(8,128)(2,1)S(1)}, bf16[8,3,16,256]{3,2,1,0:T(8,128)(2,1)S(1)}, u32[]{:S(2)}, u32[]{:S(2)}) collective-permute-start(bf16[8,3,16,256]{3,2,1,0:T(8,128)(2,1)S(1)} %get-tuple-element.31.own), channel_id=1, source_target_pairs={{0,8},{1,9},{2,10},{3,11},{4,12},{5,13},{6,14},{7,15},{8,16},{9,17... | collective-permute-start | bytes 589832 | tf_op jit(solution)/shard_map/ppermute | solution.py:500
  111.8 13.7 %collective-permute-done.13.pk_hbm = bf16[1,512,512]{2,1,0:T(8,128)(2,1)S(1)} collective-permute-done((bf16[1,512,512]{2,1,0:T(8,128)(2,1)S(1)}, bf16[1,512,512]{2,1,0:T(8,128)(2,1)S(1)}, u32[]{:S(2)}, u32[]{:S(2)}) %collective-permute-start.13) | collective-permute-done | bytes 524320 | tf_op jit(solution)/shard_map/ppermute | solution.py:507
  125.5 9.3 %collective-permute-done.14.pv_hbm = bf16[1,512,512]{2,1,0:T(8,128)(2,1)S(1)} collective-permute-done((bf16[1,512,512]{2,1,0:T(8,128)(2,1)S(1)}, bf16[1,512,512]{2,1,0:T(8,128)(2,1)S(1)}, u32[]{:S(2)}, u32[]{:S(2)}) %collective-permute-start.14) | collective-permute-done | bytes 524320 | tf_op jit(solution)/shard_map/ppermute | solution.py:508
  135.6 6.1 %attend.1.att_hbm = f32[2,512,512]{2,1,0:T(8,128)} custom-call(s32[1]{0:T(128)} %bitcast.spot_ref.pos_ref, s32[1,512]{1,0:T(1,128)} %bitcast.12, bf16[1,512,512]{2,1,0:T(8,128)(2,1)} %q_hbm.3, bf16[1,512,512]{2,1,0:T(8,128)(2,1)} %k_hbm.3, bf16[1,512,512]{2,1,0:T(8,128)(2,1)} %v_hbm.3, bf16[1,512,512]{2,1,0:T(8,128)(2,1)} %copy-done.8, ...), custom_call_target="tpu_custom_call" | custom-call | tf_op jit(solution)/shard_map/attend/pallas_call | solution.py:296
  141.8 1.6 collective-permute-done.10.one
  143.4 4.1 %fast_apply.1 = (bf16[1,512,512]{2,1,0:T(8,128)(2,1)}, bf16[512,512]{1,0:T(8,128)(2,1)}) custom-call(s32[1]{0:T(128)} %bitcast.spot_ref.pos_ref, bf16[8,4,3,16,256]{4,3,2,1,0:T(8,128)(2,1)S(1)} %all-to-all-done.3.left, bf16[8,3,16,256]{3,2,1,0:T(8,128)(2,1)S(1)} %get-tuple-element.31.own, bf16[8,3,16,256]{3,2,1,0:T(8,128)(2,1)S(1)} %collective-permute-done.10.one, ...), custom_call_target="tpu_custom_call" | custom-call | tf_op jit(solution)/shard_map/fast_apply/pallas_call | solution.py:442
  147.5 4.3 %all-to-all-start.4 = ((bf16[8,64,512]{2,1,0:T(8,128)(2,1)}), bf16[8,64,512]{2,1,0:T(8,128)(2,1)S(1)}, u32[]{:S(2)}, u32[]{:S(2)}) async-start(bf16[8,64,512]{2,1,0:T(8,128)(2,1)} %bitcast.6), calls=%async_computation.4 | async-start | bytes 1048576 | tf_op jit(solution)/shard_map/all_to_all | solution.py:524
  152.6 9.6 %all-to-all-done.4.recv_ref = bf16[8,64,512]{2,1,0:T(8,128)(2,1)S(1)} async-done(((bf16[8,64,512]{2,1,0:T(8,128)(2,1)}), bf16[8,64,512]{2,1,0:T(8,128)(2,1)S(1)}, u32[]{:S(2)}, u32[]{:S(2)}) %all-to-all-start.4) | async-done | bytes 524320 | tf_op jit(solution)/shard_map/all_to_all | solution.py:524
  (36 shorter events, 9.7 us)
Async XLA Ops:
  6.3 51.5 %copy-start = (bf16[1,512,512]{2,1,0:T(8,128)(2,1)S(1)}, bf16[1,512,512]{2,1,0:T(8,128)(2,1)}, u32[]{:S(2)}) copy-start(bf16[1,512,512]{2,1,0:T(8,128)(2,1)} %wg.1) | copy-start | bytes 1572868
  6.3 51.5 %copy-start.1 = (bf16[1,512,512]{2,1,0:T(8,128)(2,1)S(1)}, bf16[1,512,512]{2,1,0:T(8,128)(2,1)}, u32[]{:S(2)}) copy-start(bf16[1,512,512]{2,1,0:T(8,128)(2,1)} %wu.1) | copy-start | bytes 1572868
  6.3 31.8 %all-to-all-start = ((bf16[8,4,104,128]{3,2,1,0:T(8,128)(2,1)}), bf16[8,4,104,128]{3,2,1,0:T(8,128)(2,1)S(1)}, u32[]{:S(2)}, u32[]{:S(2)}) async-start(bf16[8,4,104,128]{3,2,1,0:T(8,128)(2,1)} %get-tuple-element.18), calls=%async_computation | async-start | bytes 1703936 | tf_op jit(solution)/shard_map/all_to_all | solution.py:510
  13.5 9.6 %collective-permute-start = (bf16[8,96,128]{2,1,0:T(8,128)(2,1)}, bf16[8,96,128]{2,1,0:T(8,128)(2,1)S(1)}, u32[]{:S(2)}, u32[]{:S(2)}) collective-permute-start(bf16[8,96,128]{2,1,0:T(8,128)(2,1)} %get-tuple-element.20), channel_id=1, source_target_pairs={{0,8},{1,9},{2,10},{3,11},{4,12},{5,13},{6,14},{7,15},{8,16},{9,17... | collective-permute-start | bytes 589832 | tf_op jit(solution)/shard_map/ppermute | solution.py:500
  17.8 12.5 %collective-permute-start.1 = (bf16[8,96,128]{2,1,0:T(8,128)(2,1)}, bf16[8,96,128]{2,1,0:T(8,128)(2,1)S(1)}, u32[]{:S(2)}, u32[]{:S(2)}) collective-permute-start(bf16[8,96,128]{2,1,0:T(8,128)(2,1)} %get-tuple-element.21), channel_id=1, source_target_pairs={{0,16},{1,17},{2,18},{3,19},{4,20},{5,21},{6,22},{7,23},{8,24},{9,... | collective-permute-start | bytes 589832 | tf_op jit(solution)/shard_map/ppermute | solution.py:500
  19.7 14.7 %collective-permute-start.2 = (bf16[8,96,128]{2,1,0:T(8,128)(2,1)}, bf16[8,96,128]{2,1,0:T(8,128)(2,1)S(1)}, u32[]{:S(2)}, u32[]{:S(2)}) collective-permute-start(bf16[8,96,128]{2,1,0:T(8,128)(2,1)} %get-tuple-element.22), channel_id=1, source_target_pairs={{0,24},{1,25},{2,26},{3,27},{4,28},{5,29},{6,30},{7,31},{8,0},{9,1... | collective-permute-start | bytes 589832 | tf_op jit(solution)/shard_map/ppermute | solution.py:500
  38.0 0.9 copy-start.5
  39.0 49.0 %copy-start.2 = (bf16[1,512,512]{2,1,0:T(8,128)(2,1)S(1)}, bf16[1,512,512]{2,1,0:T(8,128)(2,1)}, u32[]{:S(2)}) copy-start(bf16[1,512,512]{2,1,0:T(8,128)(2,1)} %wd.1) | copy-start | bytes 1572868
  41.1 16.7 %all-to-all-start.1 = ((bf16[8,96,128]{2,1,0:T(8,128)(2,1)}), bf16[8,96,128]{2,1,0:T(8,128)(2,1)S(1)}, u32[]{:S(2)}, u32[]{:S(2)}) async-start(bf16[8,96,128]{2,1,0:T(8,128)(2,1)} %get-tuple-element.23), calls=%async_computation.1 | async-start | bytes 393216 | tf_op jit(solution)/shard_map/all_to_all | solution.py:513
  44.5 9.6 %collective-permute-start.3 = (bf16[104,128]{1,0:T(8,128)(2,1)S(1)}, bf16[104,128]{1,0:T(8,128)(2,1)S(1)}, u32[]{:S(2)}, u32[]{:S(2)}) collective-permute-start(bf16[104,128]{1,0:T(8,128)(2,1)S(1)} %get-tuple-element.25), channel_id=1, source_target_pairs={{0,8},{1,9},{2,10},{3,11},{4,12},{5,13},{6,14},{7,15},{8,16},{9,17... | collective-permute-start | bytes 79880 | tf_op jit(solution)/shard_map/ppermute | solution.py:500
  48.8 6.6 %collective-permute-start.4 = (bf16[104,128]{1,0:T(8,128)(2,1)S(1)}, bf16[104,128]{1,0:T(8,128)(2,1)S(1)}, u32[]{:S(2)}, u32[]{:S(2)}) collective-permute-start(bf16[104,128]{1,0:T(8,128)(2,1)S(1)} %get-tuple-element.26), channel_id=1, source_target_pairs={{0,16},{1,17},{2,18},{3,19},{4,20},{5,21},{6,22},{7,23},{8,24},{9,... | collective-permute-start | bytes 79880 | tf_op jit(solution)/shard_map/ppermute | solution.py:500
  52.0 5.7 %collective-permute-start.5 = (bf16[104,128]{1,0:T(8,128)(2,1)S(1)}, bf16[104,128]{1,0:T(8,128)(2,1)S(1)}, u32[]{:S(2)}, u32[]{:S(2)}) collective-permute-start(bf16[104,128]{1,0:T(8,128)(2,1)S(1)} %get-tuple-element.27), channel_id=1, source_target_pairs={{0,24},{1,25},{2,26},{3,27},{4,28},{5,29},{6,30},{7,31},{8,0},{9,1... | collective-permute-start | bytes 79880 | tf_op jit(solution)/shard_map/ppermute | solution.py:500
  59.7 35.3 %copy-start.6 = (bf16[1,512,512]{2,1,0:T(8,128)(2,1)S(1)}, bf16[1,512,512]{2,1,0:T(8,128)(2,1)}, u32[]{:S(2)}) copy-start(bf16[1,512,512]{2,1,0:T(8,128)(2,1)} %k_hbm.3) | copy-start | bytes 1572868
  59.7 39.2 %copy-start.7 = (bf16[1,512,512]{2,1,0:T(8,128)(2,1)S(1)}, bf16[1,512,512]{2,1,0:T(8,128)(2,1)}, u32[]{:S(2)}) copy-start(bf16[1,512,512]{2,1,0:T(8,128)(2,1)} %v_hbm.3) | copy-start | bytes 1572868
  59.7 28.3 %all-to-all-start.2 = ((bf16[16,3,16,256]{3,2,1,0:T(8,128)(2,1)}), bf16[16,3,16,256]{3,2,1,0:T(8,128)(2,1)S(1)}, u32[]{:S(2)}, u32[]{:S(2)}) async-start(bf16[16,3,16,256]{3,2,1,0:T(8,128)(2,1)} %get-tuple-element.28), calls=%async_computation.2 | async-start | bytes 786432 | tf_op jit(solution)/shard_map/all_to_all | solution.py:516
  73.1 12.3 %collective-permute-start.9 = (bf16[3,16,256]{2,1,0:T(8,128)(2,1)S(1)}, bf16[3,16,256]{2,1,0:T(8,128)(2,1)S(1)}, u32[]{:S(2)}, u32[]{:S(2)}) collective-permute-start(bf16[3,16,256]{2,1,0:T(8,128)(2,1)S(1)} %get-tuple-element.29), channel_id=1, source_target_pairs={{0,56},{1,57},{2,58},{3,59},{4,60},{5,61},{6,62},{7,63},{8,32},{9,... | collective-permute-start | bytes 73736 | tf_op jit(solution)/shard_map/ppermute | solution.py:504
  79.7 5.7 %collective-permute-start.8 = (bf16[3,16,256]{2,1,0:T(8,128)(2,1)S(1)}, bf16[3,16,256]{2,1,0:T(8,128)(2,1)S(1)}, u32[]{:S(2)}, u32[]{:S(2)}) collective-permute-start(bf16[3,16,256]{2,1,0:T(8,128)(2,1)S(1)} %get-tuple-element.29), channel_id=1, source_target_pairs={{0,48},{1,49},{2,50},{3,51},{4,52},{5,53},{6,54},{7,55},{8,56},{9,... | collective-permute-start | bytes 73736 | tf_op jit(solution)/shard_map/ppermute | solution.py:504
  81.2 4.4 %collective-permute-start.7 = (bf16[3,16,256]{2,1,0:T(8,128)(2,1)S(1)}, bf16[3,16,256]{2,1,0:T(8,128)(2,1)S(1)}, u32[]{:S(2)}, u32[]{:S(2)}) collective-permute-start(bf16[3,16,256]{2,1,0:T(8,128)(2,1)S(1)} %get-tuple-element.29), channel_id=1, source_target_pairs={{0,40},{1,41},{2,42},{3,43},{4,44},{5,45},{6,46},{7,47},{8,48},{9,... | collective-permute-start | bytes 73736 | tf_op jit(solution)/shard_map/ppermute | solution.py:504
  84.2 2.8 %collective-permute-start.6 = (bf16[3,16,256]{2,1,0:T(8,128)(2,1)S(1)}, bf16[3,16,256]{2,1,0:T(8,128)(2,1)S(1)}, u32[]{:S(2)}, u32[]{:S(2)}) collective-permute-start(bf16[3,16,256]{2,1,0:T(8,128)(2,1)S(1)} %get-tuple-element.29), channel_id=1, source_target_pairs={{0,32},{1,33},{2,34},{3,35},{4,36},{5,37},{6,38},{7,39},{8,40},{9,... | collective-permute-start | bytes 73736 | tf_op jit(solution)/shard_map/ppermute | solution.py:504
  89.3 54.1 %all-to-all-start.3 = ((bf16[8,4,3,16,256]{4,3,2,1,0:T(8,128)(2,1)}), bf16[8,4,3,16,256]{4,3,2,1,0:T(8,128)(2,1)S(1)}, u32[]{:S(2)}, u32[]{:S(2)}) async-start(bf16[8,4,3,16,256]{4,3,2,1,0:T(8,128)(2,1)} %get-tuple-element.30), calls=%async_computation.3 | async-start | bytes 1572864 | tf_op jit(solution)/shard_map/all_to_all | solution.py:519
  94.9 30.6 %collective-permute-start.13 = (bf16[1,512,512]{2,1,0:T(8,128)(2,1)S(1)}, bf16[1,512,512]{2,1,0:T(8,128)(2,1)S(1)}, u32[]{:S(2)}, u32[]{:S(2)}) collective-permute-start(bf16[1,512,512]{2,1,0:T(8,128)(2,1)S(1)} %copy-done.6), channel_id=1, source_target_pairs={{0,1},{1,2},{2,3},{3,4},{4,5},{5,6},{6,7},{7,8},{8,9},{9,10},{10,1... | collective-permute-start | bytes 1572872 | tf_op jit(solution)/shard_map/ppermute | solution.py:507
  98.9 36.0 %collective-permute-start.14 = (bf16[1,512,512]{2,1,0:T(8,128)(2,1)S(1)}, bf16[1,512,512]{2,1,0:T(8,128)(2,1)S(1)}, u32[]{:S(2)}, u32[]{:S(2)}) collective-permute-start(bf16[1,512,512]{2,1,0:T(8,128)(2,1)S(1)} %copy-done.7), channel_id=1, source_target_pairs={{0,1},{1,2},{2,3},{3,4},{4,5},{5,6},{6,7},{7,8},{8,9},{9,10},{10,1... | collective-permute-start | bytes 1572872 | tf_op jit(solution)/shard_map/ppermute | solution.py:508
  102.3 39.5 %collective-permute-start.12 = (bf16[8,3,16,256]{3,2,1,0:T(8,128)(2,1)S(1)}, bf16[8,3,16,256]{3,2,1,0:T(8,128)(2,1)S(1)}, u32[]{:S(2)}, u32[]{:S(2)}) collective-permute-start(bf16[8,3,16,256]{3,2,1,0:T(8,128)(2,1)S(1)} %get-tuple-element.31.own), channel_id=1, source_target_pairs={{0,24},{1,25},{2,26},{3,27},{4,28},{5,29},{6,30},{7,31},{8,0},{9,1... | collective-permute-start | bytes 589832 | tf_op jit(solution)/shard_map/ppermute | solution.py:500
  104.7 37.0 %collective-permute-start.11 = (bf16[8,3,16,256]{3,2,1,0:T(8,128)(2,1)S(1)}, bf16[8,3,16,256]{3,2,1,0:T(8,128)(2,1)S(1)}, u32[]{:S(2)}, u32[]{:S(2)}) collective-permute-start(bf16[8,3,16,256]{3,2,1,0:T(8,128)(2,1)S(1)} %get-tuple-element.31.own), channel_id=1, source_target_pairs={{0,16},{1,17},{2,18},{3,19},{4,20},{5,21},{6,22},{7,23},{8,24},{9,... | collective-permute-start | bytes 589832 | tf_op jit(solution)/shard_map/ppermute | solution.py:500
  109.9 33.5 %collective-permute-start.10 = (bf16[8,3,16,256]{3,2,1,0:T(8,128)(2,1)S(1)}, bf16[8,3,16,256]{3,2,1,0:T(8,128)(2,1)S(1)}, u32[]{:S(2)}, u32[]{:S(2)}) collective-permute-start(bf16[8,3,16,256]{3,2,1,0:T(8,128)(2,1)S(1)} %get-tuple-element.31.own), channel_id=1, source_target_pairs={{0,8},{1,9},{2,10},{3,11},{4,12},{5,13},{6,14},{7,15},{8,16},{9,17... | collective-permute-start | bytes 589832 | tf_op jit(solution)/shard_map/ppermute | solution.py:500
  125.5 10.1 %copy-start.8 = (bf16[1,512,512]{2,1,0:T(8,128)(2,1)}, bf16[1,512,512]{2,1,0:T(8,128)(2,1)S(1)}, u32[]{:S(2)}) copy-start(bf16[1,512,512]{2,1,0:T(8,128)(2,1)S(1)} %collective-permute-done.13.pk_hbm) | copy-start | bytes 1572868
  134.8 0.8 copy-start.9
  135.6 7.8 %copy-start.3 = (bf16[1,512,512]{2,1,0:T(8,128)(2,1)S(1)}, bf16[1,512,512]{2,1,0:T(8,128)(2,1)}, u32[]{:S(2)}) copy-start(bf16[1,512,512]{2,1,0:T(8,128)(2,1)} %q_hbm.3) | copy-start | bytes 1572868
  135.6 7.8 %copy-start.4 = (bf16[512,512]{1,0:T(8,128)(2,1)S(1)}, bf16[512,512]{1,0:T(8,128)(2,1)}, u32[]{:S(2)}) copy-start(bf16[512,512]{1,0:T(8,128)(2,1)} %wc_hbm.1) | copy-start | bytes 1572868
  147.5 14.6 %all-to-all-start.4 = ((bf16[8,64,512]{2,1,0:T(8,128)(2,1)}), bf16[8,64,512]{2,1,0:T(8,128)(2,1)S(1)}, u32[]{:S(2)}, u32[]{:S(2)}) async-start(bf16[8,64,512]{2,1,0:T(8,128)(2,1)} %bitcast.6), calls=%async_computation.4 | async-start | bytes 1048576 | tf_op jit(solution)/shard_map/all_to_all | solution.py:524

commit v7 on v6

--- a/solution.py
+++ b/solution.py
@@ -25,9 +25,10 @@
 
 
 def grads_kernel(
-    spot_ref, k_hbm, v_hbm, wg_hbm, wu_hbm, wd_hbm, rate_ref, flag_ref, left_hbm, *refs
+    spot_ref, k_hbm, v_hbm, wg_hbm, wu_hbm, wd_hbm, rate_ref, flag_ref, left_hbm, kv_hbm, *refs
 ):
-    rights, (k_s, v_s, wg_s, wu_s, wd_s, left_s, right_s, sem_in, sem_left, sem_right) = refs[:4], refs[4:]
+    rights, (k_s, v_s, wg_s, wu_s, wd_s, left_s, right_s, *sems) = refs[:4], refs[4:]
+    sem_in, sem_left, sem_right, sem_kv = sems
     layer_z = lax.rem(lax.div(spot_ref[0], 8), 4)
     loads = [
         pltpu.make_async_copy(src.at[0], dst, sem_in.at[i])
@@ -78,6 +79,9 @@
     down = wd_s[...].T
     for load in loads[2:]:
         load.wait()
+    for i, src in enumerate((k_s, v_s)):
+        stores.append(pltpu.make_async_copy(src, kv_hbm.at[i], sem_kv.at[i]))
+        stores[i].start()
     key = k_s[...]
     hidden = []
     for start in range(0, 512, step):
@@ -108,10 +112,13 @@
     hb = pl.BlockSpec(memory_space=pltpu.HBM)
     return pl.pallas_call(
         grads_kernel,
-        out_shape=(jax.ShapeDtypeStruct((8, 4, 104, 128), BF16),)
+        out_shape=(
+            jax.ShapeDtypeStruct((8, 4, 104, 128), BF16),
+            jax.ShapeDtypeStruct((2, 512, 512), BF16),
+        )
         + (jax.ShapeDtypeStruct((8, 96, 128), BF16),) * 4,
         in_specs=[sm] + [hb] * 5 + [vm, vm],
-        out_specs=(hb,) * 5,
+        out_specs=(hb,) * 6,
         scratch_shapes=[pltpu.VMEM((512, 512), BF16)] * 5
         + [
             pltpu.VMEM((4, 8, 104, 128), BF16),
@@ -119,6 +126,7 @@
             pltpu.SemaphoreType.DMA((5,)),
             pltpu.SemaphoreType.DMA((2, 4)),
             pltpu.SemaphoreType.DMA((2, 4)),
+            pltpu.SemaphoreType.DMA((2,)),
         ],
         name="grads",
     )(spot, k, v, wg, wu, wd, rate, flag)
@@ -246,19 +254,19 @@
 
 
 def attend_kernel(
-    pos_ref, doc_ref, q_hbm, k_hbm, v_hbm, pk_hbm, pv_hbm, out_hbm,
+    pos_ref, doc_ref, q_hbm, k_hbm, v_hbm, prev_hbm, out_hbm,
     q_ref, k_ref, v_ref, pk_ref, pv_ref, att_s, sem,
 ):
     base = pos_ref[0] * 512
     loads = [
-        pltpu.make_async_copy(src.at[0], dst, sem.at[i])
-        for i, (src, dst) in enumerate(
+        pltpu.make_async_copy(src.at[n], dst, sem.at[i])
+        for i, (src, dst, n) in enumerate(
             (
-                (q_hbm, q_ref),
-                (k_hbm, k_ref),
-                (v_hbm, v_ref),
-                (pk_hbm, pk_ref),
-                (pv_hbm, pv_ref),
+                (q_hbm, q_ref, 0),
+                (k_hbm, k_ref, 0),
+                (v_hbm, v_ref, 0),
+                (prev_hbm, pk_ref, 0),
+                (prev_hbm, pv_ref, 1),
             )
         )
     ]
@@ -290,13 +298,13 @@
     store.wait()
 
 
-def attend(pos, q, k, v, doc, pk, pv):
+def attend(pos, q, k, v, doc, prev):
     vm = pl.BlockSpec(memory_space=pltpu.VMEM)
     hb = pl.BlockSpec(memory_space=pltpu.HBM)
     return pl.pallas_call(
         attend_kernel,
         out_shape=jax.ShapeDtypeStruct((2, 512, 512), F32),
-        in_specs=[pl.BlockSpec(memory_space=pltpu.SMEM), vm] + [hb] * 5,
+        in_specs=[pl.BlockSpec(memory_space=pltpu.SMEM), vm] + [hb] * 4,
         out_specs=hb,
         scratch_shapes=[pltpu.VMEM((512, 512), BF16)] * 5
         + [
@@ -304,7 +312,7 @@
             pltpu.SemaphoreType.DMA((6,)),
         ],
         name="attend",
-    )(pos, doc, q, k, v, pk, pv)
+    )(pos, doc, q, k, v, prev)
 
 
 def relay_kernel(
@@ -504,21 +512,20 @@
         return lax.ppermute(block, "seq", pairs)
 
     spot = index[None]
-    pk = lax.ppermute(k, "seq", route)
-    pv = lax.ppermute(v, "seq", route)
-    left, *rights = grads(spot, k, v, rate, flag[None], wg, wu, wd)
+    left, kv, *rights = grads(spot, k, v, rate, flag[None], wg, wu, wd)
     left = lax.all_to_all(left, "seq", 0, 0, axis_index_groups=rows)
     rights = [rights[0]] + [turn(rights[d], d) for d in range(1, 4)]
     right, *lefts = fold(spot, left, rights)
     right = lax.all_to_all(right, "seq", 0, 0, axis_index_groups=rows)
     lefts = [lefts[0]] + [turn(lefts[d], d) for d in range(1, 4)]
+    prev = lax.ppermute(kv, "seq", route)
     left, right = renorm(spot, right, lefts, wg, wu, wd, 512 * half)
     right = lax.all_to_all(right, "seq", 0, 0, axis_index_groups=slabs)
     lefts = [lift_up(left, d) for d in range(4)]
     left, right = relay(spot, right, lefts, wg, wu, wd)
     left = lax.all_to_all(left, "seq", 0, 0, axis_index_groups=rows)
     rights = [right] + [turn(right, d) for d in range(1, 4)]
-    att = attend(spot, q, k, v, doc_start[None], pk, pv)
+    att = attend(spot, q, k, v, doc_start[None], prev)
     mixed, part = fast_apply(spot, left, rights, q, att, wc)
     flags = lax.dynamic_slice_in_dim(flag, lax.axis_index("head") * 64, 64, 0)[None]
     got = lax.all_to_all(part.reshape(8, 64, 512), "head", 0, 0)

time: 164 us -> 164 us (level)
  the two profiles are of different devices: /device:TPU:128 before, /device:TPU:1 now
where the time goes in v7:
time: 164 us; the launch traced here: 161 us
  starting transfers between devices  84.6 us (52%)
  waiting for transfers between devices  50.6 us (31%)
  Pallas kernels  21.9 us (13%)
  local copies, waits for them, and re-layouts  2.69 us (2%)
    ppermute x9, starting transfers between devices, turn(): return lax.ppermute(block, 'seq', pairs)  32.9 us
    ppermute x1, waiting for transfers between devices, layer(): prev = lax.ppermute(kv, 'seq', route)  25.5 us
    all_to_all x1, starting transfers between devices, layer(): right = lax.all_to_all(right, 'seq', 0, 0, axis_index_groups=slabs)  12.5 us
    all_to_all x2, starting transfers between devices, layer(): left = lax.all_to_all(left, 'seq', 0, 0, axis_index_groups=rows)  12.1 us
    ppermute x9, waiting for transfers between devices, turn(): return lax.ppermute(block, 'seq', pairs)  11.8 us
    ppermute x4, starting transfers between devices, lift_up(): return lax.ppermute(block, 'seq', pairs)  11 us
    all_to_all x1, waiting for transfers between devices, layer(): got = lax.all_to_all(part.reshape(8, 64, 512), 'head', 0, 0)  8.6 us
    all_to_all x1, starting transfers between devices, layer(): got = lax.all_to_all(part.reshape(8, 64, 512), 'head', 0, 0)  7.16 us
  transfers between devices with their start and end apart: 19, of which 8 were waited for; matrix products, arithmetic and copies ran while one was open for 0% of the time, Pallas kernels for 4%

profile of v7, /device:TPU:1, one launch (start us, length us, event | category | flops | bytes accessed | tf_op | source)
XLA Modules:
  0.0 160.8 jit_solution(14282324651497938056)
XLA Ops:
  0.6 5.6 %grads.1 = (bf16[8,4,104,128]{3,2,1,0:T(8,128)(2,1)}, bf16[2,512,512]{2,1,0:T(8,128)(2,1)}, bf16[8,96,128]{2,1,0:T(8,128)(2,1)}, bf16[8,96,128]{2,1,0:T(8,128)(2...) custom-call(s32[1]{0:T(128)} %bitcast.spot_ref.pos_ref, bf16[1,512,512]{2,1,0:T(8,128)(2,1)} %k_hbm.3, ...), custom_call_target="tpu_custom_call" | custom-call | tf_op jit(solution)/shard_map/grads/pallas_call | solution.py:113
  6.3 7.8 %all-to-all-start = ((bf16[8,4,104,128]{3,2,1,0:T(8,128)(2,1)}), bf16[8,4,104,128]{3,2,1,0:T(8,128)(2,1)S(1)}, u32[]{:S(2)}, u32[]{:S(2)}) async-start(bf16[8,4,104,128]{3,2,1,0:T(8,128)(2,1)} %get-tuple-element.19), calls=%async_computation | async-start | bytes 1703936 | tf_op jit(solution)/shard_map/all_to_all | solution.py:516
  14.1 4.0 %collective-permute-start = (bf16[8,96,128]{2,1,0:T(8,128)(2,1)}, bf16[8,96,128]{2,1,0:T(8,128)(2,1)S(1)}, u32[]{:S(2)}, u32[]{:S(2)}) collective-permute-start(bf16[8,96,128]{2,1,0:T(8,128)(2,1)} %get-tuple-element.21), channel_id=1, source_target_pairs={{0,8},{1,9},{2,10},{3,11},{4,12},{5,13},{6,14},{7,15},{8,16},{9,17... | collective-permute-start | bytes 589832 | tf_op jit(solution)/shard_map/ppermute | solution.py:508
  18.1 5.8 %collective-permute-start.1 = (bf16[8,96,128]{2,1,0:T(8,128)(2,1)}, bf16[8,96,128]{2,1,0:T(8,128)(2,1)S(1)}, u32[]{:S(2)}, u32[]{:S(2)}) collective-permute-start(bf16[8,96,128]{2,1,0:T(8,128)(2,1)} %get-tuple-element.22), channel_id=1, source_target_pairs={{0,16},{1,17},{2,18},{3,19},{4,20},{5,21},{6,22},{7,23},{8,24},{9,... | collective-permute-start | bytes 589832 | tf_op jit(solution)/shard_map/ppermute | solution.py:508
  23.9 2.2 %collective-permute-start.2 = (bf16[8,96,128]{2,1,0:T(8,128)(2,1)}, bf16[8,96,128]{2,1,0:T(8,128)(2,1)S(1)}, u32[]{:S(2)}, u32[]{:S(2)}) collective-permute-start(bf16[8,96,128]{2,1,0:T(8,128)(2,1)} %get-tuple-element.23), channel_id=1, source_target_pairs={{0,24},{1,25},{2,26},{3,27},{4,28},{5,29},{6,30},{7,31},{8,0},{9,1... | collective-permute-start | bytes 589832 | tf_op jit(solution)/shard_map/ppermute | solution.py:508
  26.2 9.5 %collective-permute-done.1.two = bf16[8,96,128]{2,1,0:T(8,128)(2,1)S(1)} collective-permute-done((bf16[8,96,128]{2,1,0:T(8,128)(2,1)}, bf16[8,96,128]{2,1,0:T(8,128)(2,1)S(1)}, u32[]{:S(2)}, u32[]{:S(2)}) %collective-permute-start.1) | collective-permute-done | bytes 196640 | tf_op jit(solution)/shard_map/ppermute | solution.py:508
  35.7 1.3 all-to-all-done.left_ref
  37.9 2.1 %fold.1 = (bf16[8,96,128]{2,1,0:T(8,128)(2,1)}, bf16[104,128]{1,0:T(8,128)(2,1)S(1)}, bf16[104,128]{1,0:T(8,128)(2,1)S(1)}, bf16[104,128]{1,0:T(8,128)(2,1)S(1)}, bf16[104,128]{1,0:T(8,128)(2,1)S(1)}) custom-call(s32[1]{0:T(128)} %bitcast.spot_ref.pos_ref, bf16[8,4,104,128]{3,2,1,0:T(8,128)(2,1)S(1)} %all-to-all-done.left_ref, ...), custom_call_target="tpu_custom_call" | custom-call | tf_op jit(solution)/shard_map/fold/pallas_call | solution.py:171
  40.0 5.4 %all-to-all-start.1 = ((bf16[8,96,128]{2,1,0:T(8,128)(2,1)}), bf16[8,96,128]{2,1,0:T(8,128)(2,1)S(1)}, u32[]{:S(2)}, u32[]{:S(2)}) async-start(bf16[8,96,128]{2,1,0:T(8,128)(2,1)} %get-tuple-element.24), calls=%async_computation.1 | async-start | bytes 393216 | tf_op jit(solution)/shard_map/all_to_all | solution.py:519
  45.4 6.4 %collective-permute-start.3 = (bf16[104,128]{1,0:T(8,128)(2,1)S(1)}, bf16[104,128]{1,0:T(8,128)(2,1)S(1)}, u32[]{:S(2)}, u32[]{:S(2)}) collective-permute-start(bf16[104,128]{1,0:T(8,128)(2,1)S(1)} %get-tuple-element.26), channel_id=1, source_target_pairs={{0,8},{1,9},{2,10},{3,11},{4,12},{5,13},{6,14},{7,15},{8,16},{9,17... | collective-permute-start | bytes 79880 | tf_op jit(solution)/shard_map/ppermute | solution.py:508
  51.8 3.5 %collective-permute-start.4 = (bf16[104,128]{1,0:T(8,128)(2,1)S(1)}, bf16[104,128]{1,0:T(8,128)(2,1)S(1)}, u32[]{:S(2)}, u32[]{:S(2)}) collective-permute-start(bf16[104,128]{1,0:T(8,128)(2,1)S(1)} %get-tuple-element.27), channel_id=1, source_target_pairs={{0,16},{1,17},{2,18},{3,19},{4,20},{5,21},{6,22},{7,23},{8,24},{9,... | collective-permute-start | bytes 79880 | tf_op jit(solution)/shard_map/ppermute | solution.py:508
  55.3 2.4 %collective-permute-start.5 = (bf16[104,128]{1,0:T(8,128)(2,1)S(1)}, bf16[104,128]{1,0:T(8,128)(2,1)S(1)}, u32[]{:S(2)}, u32[]{:S(2)}) collective-permute-start(bf16[104,128]{1,0:T(8,128)(2,1)S(1)} %get-tuple-element.28), channel_id=1, source_target_pairs={{0,24},{1,25},{2,26},{3,27},{4,28},{5,29},{6,30},{7,31},{8,0},{9,1... | collective-permute-start | bytes 79880 | tf_op jit(solution)/shard_map/ppermute | solution.py:508
  57.8 2.2 %collective-permute-done.5.three = bf16[104,128]{1,0:T(8,128)(2,1)S(1)} collective-permute-done((bf16[104,128]{1,0:T(8,128)(2,1)S(1)}, bf16[104,128]{1,0:T(8,128)(2,1)S(1)}, u32[]{:S(2)}, u32[]{:S(2)}) %collective-permute-start.5) | collective-permute-done | bytes 26656 | tf_op jit(solution)/shard_map/ppermute | solution.py:508
  59.9 1.9 %renorm.1 = (bf16[3,16,256]{2,1,0:T(8,128)(2,1)S(1)}, bf16[16,3,16,256]{3,2,1,0:T(8,128)(2,1)}) custom-call(s32[1]{0:T(128)} %bitcast.spot_ref.pos_ref, bf16[8,96,128]{2,1,0:T(8,128)(2,1)S(1)} %all-to-all-done.1.right_ref, bf16[104,128]{1,0:T(8,128)(2,1)S(1)} %get-tuple-element.25.own, bf16[104,128]{1,0:T(8,128)(2,1)S(1)} %collective-permute-done.3.one, ...), custom_call_target="tpu_custom_call" | custom-call | tf_op jit(solution)/shard_map/renorm/pallas_call | solution.py:233
  61.8 12.5 %all-to-all-start.2 = ((bf16[16,3,16,256]{3,2,1,0:T(8,128)(2,1)}), bf16[16,3,16,256]{3,2,1,0:T(8,128)(2,1)S(1)}, u32[]{:S(2)}, u32[]{:S(2)}) async-start(bf16[16,3,16,256]{3,2,1,0:T(8,128)(2,1)} %get-tuple-element.29), calls=%async_computation.2 | async-start | bytes 786432 | tf_op jit(solution)/shard_map/all_to_all | solution.py:523
  74.4 7.2 %collective-permute-start.9 = (bf16[3,16,256]{2,1,0:T(8,128)(2,1)S(1)}, bf16[3,16,256]{2,1,0:T(8,128)(2,1)S(1)}, u32[]{:S(2)}, u32[]{:S(2)}) collective-permute-start(bf16[3,16,256]{2,1,0:T(8,128)(2,1)S(1)} %get-tuple-element.30), channel_id=1, source_target_pairs={{0,56},{1,57},{2,58},{3,59},{4,60},{5,61},{6,62},{7,63},{8,32},{9,... | collective-permute-start | bytes 73736 | tf_op jit(solution)/shard_map/ppermute | solution.py:512
  81.6 1.3 collective-permute-start.8
  82.8 1.3 collective-permute-start.7
  84.1 1.3 collective-permute-start.6
  85.5 2.4 %collective-permute-done.8.two = bf16[3,16,256]{2,1,0:T(8,128)(2,1)S(1)} collective-permute-done((bf16[3,16,256]{2,1,0:T(8,128)(2,1)S(1)}, bf16[3,16,256]{2,1,0:T(8,128)(2,1)S(1)}, u32[]{:S(2)}, u32[]{:S(2)}) %collective-permute-start.8) | collective-permute-done | bytes 24608 | tf_op jit(solution)/shard_map/ppermute | solution.py:512
  87.9 1.1 collective-permute-done.7.one
  89.0 1.3 relay.1
  90.3 4.3 %all-to-all-start.3 = ((bf16[8,4,3,16,256]{4,3,2,1,0:T(8,128)(2,1)}), bf16[8,4,3,16,256]{4,3,2,1,0:T(8,128)(2,1)S(1)}, u32[]{:S(2)}, u32[]{:S(2)}) async-start(bf16[8,4,3,16,256]{4,3,2,1,0:T(8,128)(2,1)} %get-tuple-element.31), calls=%async_computation.3 | async-start | bytes 1572864 | tf_op jit(solution)/shard_map/all_to_all | solution.py:526
  94.6 3.4 %collective-permute-start.13 = (bf16[2,512,512]{2,1,0:T(8,128)(2,1)S(1)}, bf16[2,512,512]{2,1,0:T(8,128)(2,1)S(1)}, u32[]{:S(2)}, u32[]{:S(2)}) collective-permute-start(bf16[2,512,512]{2,1,0:T(8,128)(2,1)S(1)} %copy-done.7), channel_id=1, source_target_pairs={{0,1},{1,2},{2,3},{3,4},{4,5},{5,6},{6,7},{7,8},{8,9},{9,10},{10,1... | collective-permute-start | bytes 3145736 | tf_op jit(solution)/shard_map/ppermute | solution.py:521
  98.0 4.3 %collective-permute-start.12 = (bf16[8,3,16,256]{3,2,1,0:T(8,128)(2,1)S(1)}, bf16[8,3,16,256]{3,2,1,0:T(8,128)(2,1)S(1)}, u32[]{:S(2)}, u32[]{:S(2)}) collective-permute-start(bf16[8,3,16,256]{3,2,1,0:T(8,128)(2,1)S(1)} %get-tuple-element.32.own), channel_id=1, source_target_pairs={{0,24},{1,25},{2,26},{3,27},{4,28},{5,29},{6,30},{7,31},{8,0},{9,1... | collective-permute-start | bytes 589832 | tf_op jit(solution)/shard_map/ppermute | solution.py:508
  102.3 1.9 %collective-permute-start.11 = (bf16[8,3,16,256]{3,2,1,0:T(8,128)(2,1)S(1)}, bf16[8,3,16,256]{3,2,1,0:T(8,128)(2,1)S(1)}, u32[]{:S(2)}, u32[]{:S(2)}) collective-permute-start(bf16[8,3,16,256]{3,2,1,0:T(8,128)(2,1)S(1)} %get-tuple-element.32.own), channel_id=1, source_target_pairs={{0,16},{1,17},{2,18},{3,19},{4,20},{5,21},{6,22},{7,23},{8,24},{9,... | collective-permute-start | bytes 589832 | tf_op jit(solution)/shard_map/ppermute | solution.py:508
  104.3 2.5 %collective-permute-start.10 = (bf16[8,3,16,256]{3,2,1,0:T(8,128)(2,1)S(1)}, bf16[8,3,16,256]{3,2,1,0:T(8,128)(2,1)S(1)}, u32[]{:S(2)}, u32[]{:S(2)}) collective-permute-start(bf16[8,3,16,256]{3,2,1,0:T(8,128)(2,1)S(1)} %get-tuple-element.32.own), channel_id=1, source_target_pairs={{0,8},{1,9},{2,10},{3,11},{4,12},{5,13},{6,14},{7,15},{8,16},{9,17... | collective-permute-start | bytes 589832 | tf_op jit(solution)/shard_map/ppermute | solution.py:508
  106.7 25.5 %collective-permute-done.13.prev_hbm = bf16[2,512,512]{2,1,0:T(8,128)(2,1)S(1)} collective-permute-done((bf16[2,512,512]{2,1,0:T(8,128)(2,1)S(1)}, bf16[2,512,512]{2,1,0:T(8,128)(2,1)S(1)}, u32[]{:S(2)}, u32[]{:S(2)}) %collective-permute-start.13) | collective-permute-done | bytes 1048608 | tf_op jit(solution)/shard_map/ppermute | solution.py:521
  133.2 6.1 %attend.1.att_hbm = f32[2,512,512]{2,1,0:T(8,128)} custom-call(s32[1]{0:T(128)} %bitcast.spot_ref.pos_ref, s32[1,512]{1,0:T(1,128)} %bitcast.12, bf16[1,512,512]{2,1,0:T(8,128)(2,1)} %q_hbm.3, bf16[1,512,512]{2,1,0:T(8,128)(2,1)} %k_hbm.3, bf16[1,512,512]{2,1,0:T(8,128)(2,1)} %v_hbm.3, bf16[2,512,512]{2,1,0:T(8,128)(2,1)} %copy-done.6), custom_call_target="tpu_custom_call" | custom-call | tf_op jit(solution)/shard_map/attend/pallas_call | solution.py:304
  139.4 4.1 %fast_apply.1 = (bf16[1,512,512]{2,1,0:T(8,128)(2,1)}, bf16[512,512]{1,0:T(8,128)(2,1)}) custom-call(s32[1]{0:T(128)} %bitcast.spot_ref.pos_ref, bf16[8,4,3,16,256]{4,3,2,1,0:T(8,128)(2,1)S(1)} %all-to-all-done.3.left, bf16[8,3,16,256]{3,2,1,0:T(8,128)(2,1)S(1)} %get-tuple-element.32.own, bf16[8,3,16,256]{3,2,1,0:T(8,128)(2,1)S(1)} %collective-permute-done.10.one, ...), custom_call_target="tpu_custom_call" | custom-call | tf_op jit(solution)/shard_map/fast_apply/pallas_call | solution.py:450
  143.5 7.2 %all-to-all-start.4 = ((bf16[8,64,512]{2,1,0:T(8,128)(2,1)}), bf16[8,64,512]{2,1,0:T(8,128)(2,1)S(1)}, u32[]{:S(2)}, u32[]{:S(2)}) async-start(bf16[8,64,512]{2,1,0:T(8,128)(2,1)} %bitcast.6), calls=%async_computation.4 | async-start | bytes 1048576 | tf_op jit(solution)/shard_map/all_to_all | solution.py:531
  151.4 8.6 %all-to-all-done.4.recv_ref = bf16[8,64,512]{2,1,0:T(8,128)(2,1)S(1)} async-done(((bf16[8,64,512]{2,1,0:T(8,128)(2,1)}), bf16[8,64,512]{2,1,0:T(8,128)(2,1)S(1)}, u32[]{:S(2)}, u32[]{:S(2)}) %all-to-all-start.4) | async-done | bytes 524320 | tf_op jit(solution)/shard_map/all_to_all | solution.py:531
  (30 shorter events, 3.6 us)
Async XLA Ops:
  6.3 53.6 %copy-start = (bf16[1,512,512]{2,1,0:T(8,128)(2,1)S(1)}, bf16[1,512,512]{2,1,0:T(8,128)(2,1)}, u32[]{:S(2)}) copy-start(bf16[1,512,512]{2,1,0:T(8,128)(2,1)} %wg.1) | copy-start | bytes 1572868
  6.3 53.6 %copy-start.1 = (bf16[1,512,512]{2,1,0:T(8,128)(2,1)S(1)}, bf16[1,512,512]{2,1,0:T(8,128)(2,1)}, u32[]{:S(2)}) copy-start(bf16[1,512,512]{2,1,0:T(8,128)(2,1)} %wu.1) | copy-start | bytes 1572868
  6.3 30.7 %all-to-all-start = ((bf16[8,4,104,128]{3,2,1,0:T(8,128)(2,1)}), bf16[8,4,104,128]{3,2,1,0:T(8,128)(2,1)S(1)}, u32[]{:S(2)}, u32[]{:S(2)}) async-start(bf16[8,4,104,128]{3,2,1,0:T(8,128)(2,1)} %get-tuple-element.19), calls=%async_computation | async-start | bytes 1703936 | tf_op jit(solution)/shard_map/all_to_all | solution.py:516
  14.1 12.1 %collective-permute-start = (bf16[8,96,128]{2,1,0:T(8,128)(2,1)}, bf16[8,96,128]{2,1,0:T(8,128)(2,1)S(1)}, u32[]{:S(2)}, u32[]{:S(2)}) collective-permute-start(bf16[8,96,128]{2,1,0:T(8,128)(2,1)} %get-tuple-element.21), channel_id=1, source_target_pairs={{0,8},{1,9},{2,10},{3,11},{4,12},{5,13},{6,14},{7,15},{8,16},{9,17... | collective-permute-start | bytes 589832 | tf_op jit(solution)/shard_map/ppermute | solution.py:508
  18.1 17.6 %collective-permute-start.1 = (bf16[8,96,128]{2,1,0:T(8,128)(2,1)}, bf16[8,96,128]{2,1,0:T(8,128)(2,1)S(1)}, u32[]{:S(2)}, u32[]{:S(2)}) collective-permute-start(bf16[8,96,128]{2,1,0:T(8,128)(2,1)} %get-tuple-element.22), channel_id=1, source_target_pairs={{0,16},{1,17},{2,18},{3,19},{4,20},{5,21},{6,22},{7,23},{8,24},{9,... | collective-permute-start | bytes 589832 | tf_op jit(solution)/shard_map/ppermute | solution.py:508
  23.9 11.8 %collective-permute-start.2 = (bf16[8,96,128]{2,1,0:T(8,128)(2,1)}, bf16[8,96,128]{2,1,0:T(8,128)(2,1)S(1)}, u32[]{:S(2)}, u32[]{:S(2)}) collective-permute-start(bf16[8,96,128]{2,1,0:T(8,128)(2,1)} %get-tuple-element.23), channel_id=1, source_target_pairs={{0,24},{1,25},{2,26},{3,27},{4,28},{5,29},{6,30},{7,31},{8,0},{9,1... | collective-permute-start | bytes 589832 | tf_op jit(solution)/shard_map/ppermute | solution.py:508
  37.0 0.9 copy-start.5
  37.9 51.0 %copy-start.2 = (bf16[1,512,512]{2,1,0:T(8,128)(2,1)S(1)}, bf16[1,512,512]{2,1,0:T(8,128)(2,1)}, u32[]{:S(2)}) copy-start(bf16[1,512,512]{2,1,0:T(8,128)(2,1)} %wd.1) | copy-start | bytes 1572868
  40.0 19.9 %all-to-all-start.1 = ((bf16[8,96,128]{2,1,0:T(8,128)(2,1)}), bf16[8,96,128]{2,1,0:T(8,128)(2,1)S(1)}, u32[]{:S(2)}, u32[]{:S(2)}) async-start(bf16[8,96,128]{2,1,0:T(8,128)(2,1)} %get-tuple-element.24), calls=%async_computation.1 | async-start | bytes 393216 | tf_op jit(solution)/shard_map/all_to_all | solution.py:519
  45.4 12.3 %collective-permute-start.3 = (bf16[104,128]{1,0:T(8,128)(2,1)S(1)}, bf16[104,128]{1,0:T(8,128)(2,1)S(1)}, u32[]{:S(2)}, u32[]{:S(2)}) collective-permute-start(bf16[104,128]{1,0:T(8,128)(2,1)S(1)} %get-tuple-element.26), channel_id=1, source_target_pairs={{0,8},{1,9},{2,10},{3,11},{4,12},{5,13},{6,14},{7,15},{8,16},{9,17... | collective-permute-start | bytes 79880 | tf_op jit(solution)/shard_map/ppermute | solution.py:508
  51.8 5.9 %collective-permute-start.4 = (bf16[104,128]{1,0:T(8,128)(2,1)S(1)}, bf16[104,128]{1,0:T(8,128)(2,1)S(1)}, u32[]{:S(2)}, u32[]{:S(2)}) collective-permute-start(bf16[104,128]{1,0:T(8,128)(2,1)S(1)} %get-tuple-element.27), channel_id=1, source_target_pairs={{0,16},{1,17},{2,18},{3,19},{4,20},{5,21},{6,22},{7,23},{8,24},{9,... | collective-permute-start | bytes 79880 | tf_op jit(solution)/shard_map/ppermute | solution.py:508
  55.3 4.6 %collective-permute-start.5 = (bf16[104,128]{1,0:T(8,128)(2,1)S(1)}, bf16[104,128]{1,0:T(8,128)(2,1)S(1)}, u32[]{:S(2)}, u32[]{:S(2)}) collective-permute-start(bf16[104,128]{1,0:T(8,128)(2,1)S(1)} %get-tuple-element.28), channel_id=1, source_target_pairs={{0,24},{1,25},{2,26},{3,27},{4,28},{5,29},{6,30},{7,31},{8,0},{9,1... | collective-permute-start | bytes 79880 | tf_op jit(solution)/shard_map/ppermute | solution.py:508
  61.8 32.8 %copy-start.7 = (bf16[2,512,512]{2,1,0:T(8,128)(2,1)S(1)}, bf16[2,512,512]{2,1,0:T(8,128)(2,1)}, u32[]{:S(2)}) copy-start(bf16[2,512,512]{2,1,0:T(8,128)(2,1)} %get-tuple-element.33) | copy-start | bytes 3145732
  61.8 27.1 %all-to-all-start.2 = ((bf16[16,3,16,256]{3,2,1,0:T(8,128)(2,1)}), bf16[16,3,16,256]{3,2,1,0:T(8,128)(2,1)S(1)}, u32[]{:S(2)}, u32[]{:S(2)}) async-start(bf16[16,3,16,256]{3,2,1,0:T(8,128)(2,1)} %get-tuple-element.29), calls=%async_computation.2 | async-start | bytes 786432 | tf_op jit(solution)/shard_map/all_to_all | solution.py:523
  74.4 11.1 %collective-permute-start.9 = (bf16[3,16,256]{2,1,0:T(8,128)(2,1)S(1)}, bf16[3,16,256]{2,1,0:T(8,128)(2,1)S(1)}, u32[]{:S(2)}, u32[]{:S(2)}) collective-permute-start(bf16[3,16,256]{2,1,0:T(8,128)(2,1)S(1)} %get-tuple-element.30), channel_id=1, source_target_pairs={{0,56},{1,57},{2,58},{3,59},{4,60},{5,61},{6,62},{7,63},{8,32},{9,... | collective-permute-start | bytes 73736 | tf_op jit(solution)/shard_map/ppermute | solution.py:512
  81.6 6.3 %collective-permute-start.8 = (bf16[3,16,256]{2,1,0:T(8,128)(2,1)S(1)}, bf16[3,16,256]{2,1,0:T(8,128)(2,1)S(1)}, u32[]{:S(2)}, u32[]{:S(2)}) collective-permute-start(bf16[3,16,256]{2,1,0:T(8,128)(2,1)S(1)} %get-tuple-element.30), channel_id=1, source_target_pairs={{0,48},{1,49},{2,50},{3,51},{4,52},{5,53},{6,54},{7,55},{8,56},{9,... | collective-permute-start | bytes 73736 | tf_op jit(solution)/shard_map/ppermute | solution.py:512
  82.8 6.1 %collective-permute-start.7 = (bf16[3,16,256]{2,1,0:T(8,128)(2,1)S(1)}, bf16[3,16,256]{2,1,0:T(8,128)(2,1)S(1)}, u32[]{:S(2)}, u32[]{:S(2)}) collective-permute-start(bf16[3,16,256]{2,1,0:T(8,128)(2,1)S(1)} %get-tuple-element.30), channel_id=1, source_target_pairs={{0,40},{1,41},{2,42},{3,43},{4,44},{5,45},{6,46},{7,47},{8,48},{9,... | collective-permute-start | bytes 73736 | tf_op jit(solution)/shard_map/ppermute | solution.py:512
  84.1 4.8 %collective-permute-start.6 = (bf16[3,16,256]{2,1,0:T(8,128)(2,1)S(1)}, bf16[3,16,256]{2,1,0:T(8,128)(2,1)S(1)}, u32[]{:S(2)}, u32[]{:S(2)}) collective-permute-start(bf16[3,16,256]{2,1,0:T(8,128)(2,1)S(1)} %get-tuple-element.30), channel_id=1, source_target_pairs={{0,32},{1,33},{2,34},{3,35},{4,36},{5,37},{6,38},{7,39},{8,40},{9,... | collective-permute-start | bytes 73736 | tf_op jit(solution)/shard_map/ppermute | solution.py:512
  90.3 49.1 %all-to-all-start.3 = ((bf16[8,4,3,16,256]{4,3,2,1,0:T(8,128)(2,1)}), bf16[8,4,3,16,256]{4,3,2,1,0:T(8,128)(2,1)S(1)}, u32[]{:S(2)}, u32[]{:S(2)}) async-start(bf16[8,4,3,16,256]{4,3,2,1,0:T(8,128)(2,1)} %get-tuple-element.31), calls=%async_computation.3 | async-start | bytes 1572864 | tf_op jit(solution)/shard_map/all_to_all | solution.py:526
  94.6 37.6 %collective-permute-start.13 = (bf16[2,512,512]{2,1,0:T(8,128)(2,1)S(1)}, bf16[2,512,512]{2,1,0:T(8,128)(2,1)S(1)}, u32[]{:S(2)}, u32[]{:S(2)}) collective-permute-start(bf16[2,512,512]{2,1,0:T(8,128)(2,1)S(1)} %copy-done.7), channel_id=1, source_target_pairs={{0,1},{1,2},{2,3},{3,4},{4,5},{5,6},{6,7},{7,8},{8,9},{9,10},{10,1... | collective-permute-start | bytes 3145736 | tf_op jit(solution)/shard_map/ppermute | solution.py:521
  98.0 41.3 %collective-permute-start.12 = (bf16[8,3,16,256]{3,2,1,0:T(8,128)(2,1)S(1)}, bf16[8,3,16,256]{3,2,1,0:T(8,128)(2,1)S(1)}, u32[]{:S(2)}, u32[]{:S(2)}) collective-permute-start(bf16[8,3,16,256]{3,2,1,0:T(8,128)(2,1)S(1)} %get-tuple-element.32.own), channel_id=1, source_target_pairs={{0,24},{1,25},{2,26},{3,27},{4,28},{5,29},{6,30},{7,31},{8,0},{9,1... | collective-permute-start | bytes 589832 | tf_op jit(solution)/shard_map/ppermute | solution.py:508
  102.3 37.0 %collective-permute-start.11 = (bf16[8,3,16,256]{3,2,1,0:T(8,128)(2,1)S(1)}, bf16[8,3,16,256]{3,2,1,0:T(8,128)(2,1)S(1)}, u32[]{:S(2)}, u32[]{:S(2)}) collective-permute-start(bf16[8,3,16,256]{3,2,1,0:T(8,128)(2,1)S(1)} %get-tuple-element.32.own), channel_id=1, source_target_pairs={{0,16},{1,17},{2,18},{3,19},{4,20},{5,21},{6,22},{7,23},{8,24},{9,... | collective-permute-start | bytes 589832 | tf_op jit(solution)/shard_map/ppermute | solution.py:508
  104.3 35.1 %collective-permute-start.10 = (bf16[8,3,16,256]{3,2,1,0:T(8,128)(2,1)S(1)}, bf16[8,3,16,256]{3,2,1,0:T(8,128)(2,1)S(1)}, u32[]{:S(2)}, u32[]{:S(2)}) collective-permute-start(bf16[8,3,16,256]{3,2,1,0:T(8,128)(2,1)S(1)} %get-tuple-element.32.own), channel_id=1, source_target_pairs={{0,8},{1,9},{2,10},{3,11},{4,12},{5,13},{6,14},{7,15},{8,16},{9,17... | collective-permute-start | bytes 589832 | tf_op jit(solution)/shard_map/ppermute | solution.py:508
  132.2 1.0 copy-start.6
  133.2 6.2 %copy-start.3 = (bf16[1,512,512]{2,1,0:T(8,128)(2,1)S(1)}, bf16[1,512,512]{2,1,0:T(8,128)(2,1)}, u32[]{:S(2)}) copy-start(bf16[1,512,512]{2,1,0:T(8,128)(2,1)} %q_hbm.3) | copy-start | bytes 1572868
  133.2 6.2 %copy-start.4 = (bf16[512,512]{1,0:T(8,128)(2,1)S(1)}, bf16[512,512]{1,0:T(8,128)(2,1)}, u32[]{:S(2)}) copy-start(bf16[512,512]{1,0:T(8,128)(2,1)} %wc_hbm.1) | copy-start | bytes 1572868
  143.5 16.5 %all-to-all-start.4 = ((bf16[8,64,512]{2,1,0:T(8,128)(2,1)}), bf16[8,64,512]{2,1,0:T(8,128)(2,1)S(1)}, u32[]{:S(2)}, u32[]{:S(2)}) async-start(bf16[8,64,512]{2,1,0:T(8,128)(2,1)} %bitcast.6), calls=%async_computation.4 | async-start | bytes 1048576 | tf_op jit(solution)/shard_map/all_to_all | solution.py:531

commit v8 on v4

--- a/solution.py
+++ b/solution.py
@@ -12,7 +12,7 @@
 GRADS_STEP = 256
 APPLY_STEP = 256
 RENORM_VMEM = 51200 << 10
-RELAY_VMEM = 54800 << 10
+RELAY_VMEM = 53000 << 10
 APPLY_VMEM = 50800 << 10
 BF16 = jnp.bfloat16
 NN = (((1,), (0,)), ((), ()))
@@ -108,9 +108,10 @@
 
 
 def renorm_kernel(
-    rank_ref, recv_ref, wg, wu, wd, out, old_s, new_s, sem_in, sem_out, *, update_len
+    spot_ref, recv_ref, wg, wu, wd, left_hbm, right_hbm,
+    old_s, left_s, right_s, sem_in, sem_left, sem_right, *, update_len,
 ):
-    rows = pl.ds(pl.multiple_of(rank_ref[0] * 16, 16), 16)
+    rows = pl.ds(pl.multiple_of(lax.rem(spot_ref[0], 32) * 16, 16), 16)
     loads = [
         pltpu.make_async_copy(ref.at[0, rows], old_s.at[i], sem_in.at[i])
         for i, ref in enumerate((wg, wu, wd))
@@ -131,19 +132,25 @@
         updated = old + summed * factor
         old_norm = jnp.sqrt(jnp.sum(old * old, axis=-1, keepdims=True))
         new_norm = jnp.sqrt(jnp.sum(updated * updated, axis=-1, keepdims=True) + 1e-6)
-        new_s[which] = (updated * (old_norm / new_norm)).astype(BF16)
-    stores = [pltpu.make_async_copy(new_s, out.at[d], sem_out.at[d]) for d in range(8)]
+        fresh = (updated * (old_norm / new_norm)).astype(BF16)
+        left_s[which] = fresh[:, :256]
+        right_s[which] = fresh[:, 256:]
+    stores = [pltpu.make_async_copy(right_s, right_hbm.at[d], sem_right.at[d]) for d in range(16)]
+    stores.append(pltpu.make_async_copy(left_s, left_hbm, sem_left))
     for store in stores:
         store.start()
     for store in stores:
         store.wait()
 
 
-def renorm(rank, recv, wg, wu, wd, update_len):
+def renorm(spot, recv, wg, wu, wd, update_len):
     hb = pl.BlockSpec(memory_space=pltpu.HBM)
     return pl.pallas_call(
         functools.partial(renorm_kernel, update_len=update_len),
-        out_shape=jax.ShapeDtypeStruct((8, 3, 16, 512), BF16),
+        out_shape=(
+            jax.ShapeDtypeStruct((3, 16, 256), BF16),
+            jax.ShapeDtypeStruct((16, 3, 16, 256), BF16),
+        ),
         in_specs=[
             pl.BlockSpec(memory_space=pltpu.SMEM),
             pl.BlockSpec(memory_space=pltpu.VMEM),
@@ -151,23 +158,25 @@
             hb,
             hb,
         ],
-        out_specs=hb,
+        out_specs=(hb, hb),
         scratch_shapes=[
             pltpu.VMEM((3, 16, 512), BF16),
-            pltpu.VMEM((3, 16, 512), BF16),
+            pltpu.VMEM((3, 16, 256), BF16),
+            pltpu.VMEM((3, 16, 256), BF16),
             pltpu.SemaphoreType.DMA((3,)),
-            pltpu.SemaphoreType.DMA((8,)),
+            pltpu.SemaphoreType.DMA,
+            pltpu.SemaphoreType.DMA((16,)),
         ],
         compiler_params=pltpu.CompilerParams(vmem_limit_bytes=RENORM_VMEM),
         name="renorm",
-    )(rank, recv, wg, wu, wd)
+    )(spot, recv, wg, wu, wd)
 
 
 def attend_kernel(
     pos_ref, doc_ref, q_hbm, k_hbm, v_hbm, pk_hbm, pv_hbm, out_hbm,
     q_ref, k_ref, v_ref, pk_ref, pv_ref, att_s, sem,
 ):
-    base = pos_ref[2]
+    base = pos_ref[0] * 512
     loads = [
         pltpu.make_async_copy(src.at[0], dst, sem.at[i])
         for i, (src, dst) in enumerate(
@@ -225,56 +234,90 @@
     )(pos, doc, q, k, v, pk, pv)
 
 
-def relay_kernel(spot_ref, recv, wg, wu, wd, out, own, sem_in, sem_out):
-    first = spot_ref[0] == 1
-    column = spot_ref[1]
+def relay_kernel(
+    spot_ref, right, zero, one, two, three, wg, wu, wd, left_hbm, right_hbm,
+    left_s, right_s, sem_in, sem_out, sem_right,
+):
+    first = spot_ref[0] < 32
+    layer_z = lax.rem(lax.div(spot_ref[0], 8), 4)
+    column = lax.rem(spot_ref[0], 8)
 
     def send(source):
-        copies = [pltpu.make_async_copy(source, out.at[d], sem_out.at[d]) for d in range(8)]
+        store = pltpu.make_async_copy(source, right_hbm, sem_right)
+        store.start()
+        copies = [pltpu.make_async_copy(left_s, left_hbm.at[d], sem_out.at[d]) for d in range(8)]
         for copy in copies:
             copy.start()
         for copy in copies:
             copy.wait()
+        store.wait()
 
     @pl.when(first)
     def _():
-        copies = [
-            pltpu.make_async_copy(ref.at[:, column], own.at[:, i], sem_in.at[i])
-            for i, ref in enumerate((wg, wu, wd))
-        ]
+        copies = []
+        for i, ref in enumerate((wg, wu, wd)):
+            copies.append(
+                pltpu.make_async_copy(ref.at[:, column, :, pl.ds(0, 256)], left_s.at[:, i], sem_in.at[i])
+            )
+            copies.append(
+                pltpu.make_async_copy(
+                    ref.at[layer_z, :, :, pl.ds(256, 256)], right_s.at[:, i], sem_in.at[i + 3]
+                )
+            )
         for copy in copies:
             copy.start()
         for copy in copies:
             copy.wait()
-        send(own)
+        send(right_s)
 
     @pl.when(jnp.logical_not(first))
     def _():
-        send(recv.at[pl.ds(0, 4)])
-
-
-def relay(spot, recv, wg, wu, wd):
+        copies = [
+            pltpu.make_async_copy(src, left_s.at[lax.rem(layer_z + 4 - d, 4)], sem_in.at[d])
+            for d, src in enumerate((zero, one, two, three))
+        ]
+        for copy in copies:
+            copy.start()
+        for copy in copies:
+            copy.wait()
+        send(right.at[pl.ds(0, 8)])
+
+
+def relay(spot, right, lefts, wg, wu, wd):
+    sm = pl.BlockSpec(memory_space=pltpu.SMEM)
     vm = pl.BlockSpec(memory_space=pltpu.VMEM)
     hb = pl.BlockSpec(memory_space=pltpu.HBM)
     return pl.pallas_call(
         relay_kernel,
-        out_shape=jax.ShapeDtypeStruct((8, 4, 3, 16, 512), BF16),
-        in_specs=[pl.BlockSpec(memory_space=pltpu.SMEM), vm, hb, hb, hb],
-        out_specs=hb,
+        out_shape=(
+            jax.ShapeDtypeStruct((8, 4, 3, 16, 256), BF16),
+            jax.ShapeDtypeStruct((8, 3, 16, 256), BF16),
+        ),
+        in_specs=[sm, vm] + [hb] * 7,
+        out_specs=(hb, hb),
         scratch_shapes=[
-            pltpu.VMEM((4, 3, 16, 512), BF16),
-            pltpu.SemaphoreType.DMA((3,)),
+            pltpu.VMEM((4, 3, 16, 256), BF16),
+            pltpu.VMEM((8, 3, 16, 256), BF16),
+            pltpu.SemaphoreType.DMA((6,)),
             pltpu.SemaphoreType.DMA((8,)),
+            pltpu.SemaphoreType.DMA,
         ],
         compiler_params=pltpu.CompilerParams(vmem_limit_bytes=RELAY_VMEM),
         name="relay",
-    )(spot, recv, *(x.reshape(4, 8, 16, 512) for x in (wg, wu, wd)))
+    )(spot, right, *lefts, *(x.reshape(4, 8, 16, 512) for x in (wg, wu, wd)))
 
 
 def apply_kernel(
-    fresh, q_hbm, att_hbm, wc_hbm, mixed_hbm, part_hbm,
-    q_s, att_s, wc_s, mixed_s, part_s, sem_in, sem_out,
+    spot_ref, left, own, one, two, three, q_hbm, att_hbm, wc_hbm, mixed_hbm, part_hbm,
+    right, q_s, att_s, wc_s, mixed_s, part_s, sem_in, sem_right, sem_out,
 ):
+    layer_z = lax.rem(lax.div(spot_ref[0], 8), 4)
+    slabs = [
+        pltpu.make_async_copy(src, right.at[lax.rem(layer_z + 4 - d, 4)], sem_right.at[d])
+        for d, src in enumerate((own, one, two, three))
+    ]
+    for slab in slabs:
+        slab.start()
     loads = [
         pltpu.make_async_copy(src, dst, sem_in.at[i])
         for i, (src, dst) in enumerate(((q_hbm.at[0], q_s), (att_hbm.at[0], att_s), (wc_hbm, wc_s)))
@@ -284,10 +327,18 @@
 
     def weight(i, low, count):
         spots = [(z, y) for z in range(low // 128, (low + count) // 128) for y in range(8)]
-        return jnp.concatenate([fresh[y, z, i] for z, y in spots], axis=0)
+        return jnp.concatenate(
+            [
+                jnp.concatenate([left[y, z, i] for z, y in spots], axis=0),
+                jnp.concatenate([right[z, y, i] for z, y in spots], axis=0),
+            ],
+            axis=1,
+        )
 
     step = APPLY_STEP
     loads[0].wait()
+    for slab in slabs:
+        slab.wait()
     q = q_s[...]
     hidden = []
     for start in range(0, 512, step):
@@ -312,7 +363,7 @@
         store.wait()
 
 
-def fast_apply(fresh, q, att, wc):
+def fast_apply(spot, left, rights, q, att, wc):
     vm = pl.BlockSpec(memory_space=pltpu.VMEM)
     hb = pl.BlockSpec(memory_space=pltpu.HBM)
     return pl.pallas_call(
@@ -321,20 +372,22 @@
             jax.ShapeDtypeStruct((1, 512, 512), BF16),
             jax.ShapeDtypeStruct((512, 512), BF16),
         ),
-        in_specs=[vm, hb, hb, hb],
+        in_specs=[pl.BlockSpec(memory_space=pltpu.SMEM), vm] + [hb] * 7,
         out_specs=(hb, hb),
         scratch_shapes=[
+            pltpu.VMEM((4, 8, 3, 16, 256), BF16),
             pltpu.VMEM((512, 512), BF16),
             pltpu.VMEM((512, 512), F32),
             pltpu.VMEM((512, 512), BF16),
             pltpu.VMEM((512, 512), BF16),
             pltpu.VMEM((512, 512), BF16),
             pltpu.SemaphoreType.DMA((3,)),
+            pltpu.SemaphoreType.DMA((4,)),
             pltpu.SemaphoreType.DMA((2,)),
         ],
         compiler_params=pltpu.CompilerParams(vmem_limit_bytes=APPLY_VMEM),
         name="fast_apply",
-    )(fresh, q, att, wc)
+    )(spot, left, *rights, q, att, wc)
 
 
 def combine_kernel(recv_ref, flag_ref, out_ref):
@@ -359,25 +412,39 @@
     seq_count = lax.axis_size("seq")
     half = seq_count // 2
     index = lax.axis_index("seq").astype(jnp.int32)
-    first = (index < half).astype(jnp.int32)
-    rank = lax.rem(index, half)
+    place = lambda z, y: z * 8 + y
+    slabs = [[place(z + lift, y) for lift in (0, 4) for y in range(8)] for z in range(4)]
+    rows = [[place(z, y) for y in range(8)] for z in range(8)]
     halves = [list(range(half)), list(range(half, seq_count))]
-    columns = [[z * 8 + y for z in range(8)] for y in range(8)]
-    rows = [[z * 8 + y for y in range(8)] for z in range(8)]
     route = [(i - 1, i) for i in range(1, seq_count)]
 
-    flags = lax.dynamic_slice_in_dim(flag, lax.axis_index("head") * 64, 64, 0)[None]
-    spot = jnp.stack([first, lax.rem(index, 8), index * 512])
-    pk = lax.ppermute(k, "seq", route)
-    pv = lax.ppermute(v, "seq", route)
+    def turn(block, d):
+        pairs = [
+            (place(z + lift, y), place((z + d) % 4 + lift, y))
+            for lift in (0, 4)
+            for z in range(4)
+            for y in range(8)
+        ]
+        return lax.ppermute(block, "seq", pairs)
+
+    def lift_up(block, d):
+        pairs = [(place(z, y), place((z + d) % 4 + 4, y)) for z in range(4) for y in range(8)]
+        return lax.ppermute(block, "seq", pairs)
+
+    spot = index[None]
     terms = grads(k, v, rate, flag[None], wg, wu, wd)
     recv = lax.all_to_all(terms, "seq", 0, 0, axis_index_groups=halves)
-    shard = renorm(rank[None], recv, wg, wu, wd, 512 * half)
-    shard = lax.all_to_all(shard, "seq", 0, 0, axis_index_groups=columns)
-    shard = relay(spot, shard, wg, wu, wd)
-    fresh = lax.all_to_all(shard, "seq", 0, 0, axis_index_groups=rows)
+    pk = lax.ppermute(k, "seq", route)
+    left, right = renorm(spot, recv, wg, wu, wd, 512 * half)
+    right = lax.all_to_all(right, "seq", 0, 0, axis_index_groups=slabs)
+    lefts = [lift_up(left, d) for d in range(4)]
+    pv = lax.ppermute(v, "seq", route)
+    left, right = relay(spot, right, lefts, wg, wu, wd)
+    left = lax.all_to_all(left, "seq", 0, 0, axis_index_groups=rows)
+    rights = [right] + [turn(right, d) for d in range(1, 4)]
     att = attend(spot, q, k, v, doc_start[None], pk, pv)
-    mixed, part = fast_apply(fresh, q, att, wc)
+    mixed, part = fast_apply(spot, left, rights, q, att, wc)
+    flags = lax.dynamic_slice_in_dim(flag, lax.axis_index("head") * 64, 64, 0)[None]
     got = lax.all_to_all(part.reshape(8, 64, 512), "head", 0, 0)
     return mixed, combine(got, flags)
 

time: 177 us -> 164 us (0.927)
  waiting for transfers between devices: 107 us -> 72.4 us
  starting transfers between devices: 44.9 us -> 66.4 us
    ppermute x1, waiting for transfers between devices: 36.8 us -> 9.77 us  [layer(): pk = lax.ppermute(k, 'seq', route)]
    ppermute x0 -> x7, starting transfers between devices: none -> 22.8 us  [the longest x4 12.7 us: lift_up(): return lax.ppermute(block, 'seq', pairs)]
    all_to_all x2, waiting for transfers between devices: 11.3 us -> 0.01 us  [the longest x1 0.01 us: layer(): right = lax.all_to_all(right, 'seq', 0, 0, axis_index_groups=slabs)]
    ppermute x0 -> x7, waiting for transfers between devices: none -> 3.86 us  [the longest x4 3.85 us: lift_up(): return lax.ppermute(block, 'seq', pairs)]
  transfers between devices with their start and end apart: 6 -> 13, of which waited for: 5 -> 6; matrix products, arithmetic and copies ran while one was open for 0% -> 0% of each run, Pallas kernels for 4% -> 4%
where the time goes in v8:
time: 164 us; the launch traced here: 161 us
  waiting for transfers between devices  72.4 us (44%)
  starting transfers between devices  66.4 us (40%)
  Pallas kernels  18.9 us (12%)
  local copies, waits for them, and re-layouts  2.35 us (1%)
    all_to_all x1, waiting for transfers between devices, layer(): recv = lax.all_to_all(terms, 'seq', 0, 0, axis_index_groups=halves)  38.9 us
    all_to_all x1, starting transfers between devices, layer(): recv = lax.all_to_all(terms, 'seq', 0, 0, axis_index_groups=halves)  13.6 us
    ppermute x4, starting transfers between devices, lift_up(): return lax.ppermute(block, 'seq', pairs)  12.7 us
    all_to_all x1, starting transfers between devices, layer(): right = lax.all_to_all(right, 'seq', 0, 0, axis_index_groups=slabs)  12.2 us
    ppermute x1, waiting for transfers between devices, layer(): pv = lax.ppermute(v, 'seq', route)  11.2 us
    ppermute x3, starting transfers between devices, turn(): return lax.ppermute(block, 'seq', pairs)  10.1 us
    ppermute x1, waiting for transfers between devices, layer(): pk = lax.ppermute(k, 'seq', route)  9.77 us
    all_to_all x1, waiting for transfers between devices, layer(): got = lax.all_to_all(part.reshape(8, 64, 512), 'head', 0, 0)  8.6 us
  transfers between devices with their start and end apart: 13, of which 6 were waited for; matrix products, arithmetic and copies ran while one was open for 0% of the time, Pallas kernels for 4%

profile of v8, /device:TPU:1, one launch (start us, length us, event | category | flops | bytes accessed | tf_op | source)
XLA Modules:
  0.0 161.0 jit_solution(17464288673596857990)
XLA Ops:
  0.6 5.4 %grads.1 = bf16[32,200,128]{2,1,0:T(8,128)(2,1)} custom-call(bf16[1,512,512]{2,1,0:T(8,128)(2,1)} %k_hbm.3, bf16[1,512,512]{2,1,0:T(8,128)(2,1)} %v_hbm.3, bf16[1,512,512]{2,1,0:T(8,128)(2,1)} %wg.1, bf16[1,512,512]{2,1,0:T(8,128)(2,1)} %wu.1, bf16[1,512,512]{2,1,0:T(8,128)(2,1)} %wd.1, f32[1,512]{1,0:T(1,128)} %rate_ref.1, s32[1,512]{1,0:T(1,128)} %bitcast.12), custom_call_target="tpu_custom_call" | custom-call | tf_op jit(solution)/shard_map/grads/pallas_call | solution.py:95
  6.0 0.0 copy-start
  6.0 0.0 copy-start.1
  6.0 0.0 copy-start.2
  6.1 13.6 %all-to-all-start = ((bf16[32,200,128]{2,1,0:T(8,128)(2,1)}), bf16[32,200,128]{2,1,0:T(8,128)(2,1)S(1)}, u32[]{:S(2)}, u32[]{:S(2)}) async-start(bf16[32,200,128]{2,1,0:T(8,128)(2,1)} %grads.1), calls=%async_computation | async-start | bytes 3276800 | tf_op jit(solution)/shard_map/all_to_all | solution.py:436
  19.7 38.9 %all-to-all-done.recv_ref = bf16[32,200,128]{2,1,0:T(8,128)(2,1)S(1)} async-done(((bf16[32,200,128]{2,1,0:T(8,128)(2,1)}), bf16[32,200,128]{2,1,0:T(8,128)(2,1)S(1)}, u32[]{:S(2)}, u32[]{:S(2)}) %all-to-all-start) | async-done | bytes 1638432 | tf_op jit(solution)/shard_map/all_to_all | solution.py:436
  58.6 1.2 renorm.1
  59.8 0.0 copy-start.5
  59.8 0.7 copy-done.5
  60.6 12.2 %all-to-all-start.1 = ((bf16[16,3,16,256]{3,2,1,0:T(8,128)(2,1)}), bf16[16,3,16,256]{3,2,1,0:T(8,128)(2,1)S(1)}, u32[]{:S(2)}, u32[]{:S(2)}) async-start(bf16[16,3,16,256]{3,2,1,0:T(8,128)(2,1)} %copy-done.5), calls=%async_computation.1 | async-start | bytes 786432 | tf_op jit(solution)/shard_map/all_to_all | solution.py:439
  72.8 7.2 %collective-permute-start = (bf16[3,16,256]{2,1,0:T(8,128)(2,1)S(1)}, bf16[3,16,256]{2,1,0:T(8,128)(2,1)S(1)}, u32[]{:S(2)}, u32[]{:S(2)}) collective-permute-start(bf16[3,16,256]{2,1,0:T(8,128)(2,1)S(1)} %get-tuple-element.9), channel_id=1, source_target_pairs={{0,32},{1,33},{2,34},{3,35},{4,36},{5,37},{6,38},{7,39},{8,40},{9,... | collective-permute-start | bytes 73736 | tf_op jit(solution)/shard_map/ppermute | solution.py:432
  80.0 2.9 %collective-permute-start.1 = (bf16[3,16,256]{2,1,0:T(8,128)(2,1)S(1)}, bf16[3,16,256]{2,1,0:T(8,128)(2,1)S(1)}, u32[]{:S(2)}, u32[]{:S(2)}) collective-permute-start(bf16[3,16,256]{2,1,0:T(8,128)(2,1)S(1)} %get-tuple-element.9), channel_id=1, source_target_pairs={{0,40},{1,41},{2,42},{3,43},{4,44},{5,45},{6,46},{7,47},{8,48},{9,... | collective-permute-start | bytes 73736 | tf_op jit(solution)/shard_map/ppermute | solution.py:432
  82.8 1.4 collective-permute-start.2
  84.2 1.3 collective-permute-start.3
  85.5 3.0 %collective-permute-done.2.two = bf16[3,16,256]{2,1,0:T(8,128)(2,1)S(1)} collective-permute-done((bf16[3,16,256]{2,1,0:T(8,128)(2,1)S(1)}, bf16[3,16,256]{2,1,0:T(8,128)(2,1)S(1)}, u32[]{:S(2)}, u32[]{:S(2)}) %collective-permute-start.2) | collective-permute-done | bytes 24608 | tf_op jit(solution)/shard_map/ppermute | solution.py:432
  88.6 0.8 collective-permute-done.3.three
  89.4 1.3 relay.1
  90.7 4.2 %all-to-all-start.2 = ((bf16[8,4,3,16,256]{4,3,2,1,0:T(8,128)(2,1)}), bf16[8,4,3,16,256]{4,3,2,1,0:T(8,128)(2,1)S(1)}, u32[]{:S(2)}, u32[]{:S(2)}) async-start(bf16[8,4,3,16,256]{4,3,2,1,0:T(8,128)(2,1)} %get-tuple-element.10), calls=%async_computation.2 | async-start | bytes 1572864 | tf_op jit(solution)/shard_map/all_to_all | solution.py:443
  94.9 3.4 %collective-permute-start.7 = (bf16[1,512,512]{2,1,0:T(8,128)(2,1)S(1)}, bf16[1,512,512]{2,1,0:T(8,128)(2,1)S(1)}, u32[]{:S(2)}, u32[]{:S(2)}) collective-permute-start(bf16[1,512,512]{2,1,0:T(8,128)(2,1)S(1)} %copy-done.6), channel_id=1, source_target_pairs={{0,1},{1,2},{2,3},{3,4},{4,5},{5,6},{6,7},{7,8},{8,9},{9,10},{10,1... | collective-permute-start | bytes 1572872 | tf_op jit(solution)/shard_map/ppermute | solution.py:437
  98.3 3.1 %collective-permute-start.8 = (bf16[1,512,512]{2,1,0:T(8,128)(2,1)S(1)}, bf16[1,512,512]{2,1,0:T(8,128)(2,1)S(1)}, u32[]{:S(2)}, u32[]{:S(2)}) collective-permute-start(bf16[1,512,512]{2,1,0:T(8,128)(2,1)S(1)} %copy-done.7), channel_id=1, source_target_pairs={{0,1},{1,2},{2,3},{3,4},{4,5},{5,6},{6,7},{7,8},{8,9},{9,10},{10,1... | collective-permute-start | bytes 1572872 | tf_op jit(solution)/shard_map/ppermute | solution.py:441
  101.4 2.5 %collective-permute-start.4 = (bf16[8,3,16,256]{3,2,1,0:T(8,128)(2,1)S(1)}, bf16[8,3,16,256]{3,2,1,0:T(8,128)(2,1)S(1)}, u32[]{:S(2)}, u32[]{:S(2)}) collective-permute-start(bf16[8,3,16,256]{3,2,1,0:T(8,128)(2,1)S(1)} %get-tuple-element.11.own), channel_id=1, source_target_pairs={{0,8},{1,9},{2,10},{3,11},{4,12},{5,13},{6,14},{7,15},{8,16},{9,17... | collective-permute-start | bytes 589832 | tf_op jit(solution)/shard_map/ppermute | solution.py:428
  103.9 3.3 %collective-permute-start.5 = (bf16[8,3,16,256]{3,2,1,0:T(8,128)(2,1)S(1)}, bf16[8,3,16,256]{3,2,1,0:T(8,128)(2,1)S(1)}, u32[]{:S(2)}, u32[]{:S(2)}) collective-permute-start(bf16[8,3,16,256]{3,2,1,0:T(8,128)(2,1)S(1)} %get-tuple-element.11.own), channel_id=1, source_target_pairs={{0,16},{1,17},{2,18},{3,19},{4,20},{5,21},{6,22},{7,23},{8,24},{9,... | collective-permute-start | bytes 589832 | tf_op jit(solution)/shard_map/ppermute | solution.py:428
  107.2 4.3 %collective-permute-start.6 = (bf16[8,3,16,256]{3,2,1,0:T(8,128)(2,1)S(1)}, bf16[8,3,16,256]{3,2,1,0:T(8,128)(2,1)S(1)}, u32[]{:S(2)}, u32[]{:S(2)}) collective-permute-start(bf16[8,3,16,256]{3,2,1,0:T(8,128)(2,1)S(1)} %get-tuple-element.11.own), channel_id=1, source_target_pairs={{0,24},{1,25},{2,26},{3,27},{4,28},{5,29},{6,30},{7,31},{8,0},{9,1... | collective-permute-start | bytes 589832 | tf_op jit(solution)/shard_map/ppermute | solution.py:428
  111.5 9.8 %collective-permute-done.7.pk_hbm = bf16[1,512,512]{2,1,0:T(8,128)(2,1)S(1)} collective-permute-done((bf16[1,512,512]{2,1,0:T(8,128)(2,1)S(1)}, bf16[1,512,512]{2,1,0:T(8,128)(2,1)S(1)}, u32[]{:S(2)}, u32[]{:S(2)}) %collective-permute-start.7) | collective-permute-done | bytes 524320 | tf_op jit(solution)/shard_map/ppermute | solution.py:437
  121.3 11.2 %collective-permute-done.8.pv_hbm = bf16[1,512,512]{2,1,0:T(8,128)(2,1)S(1)} collective-permute-done((bf16[1,512,512]{2,1,0:T(8,128)(2,1)S(1)}, bf16[1,512,512]{2,1,0:T(8,128)(2,1)S(1)}, u32[]{:S(2)}, u32[]{:S(2)}) %collective-permute-start.8) | collective-permute-done | bytes 524320 | tf_op jit(solution)/shard_map/ppermute | solution.py:441
  132.5 0.8 copy-done.9
  133.3 6.1 %attend.1.att_hbm = f32[2,512,512]{2,1,0:T(8,128)} custom-call(s32[1]{0:T(128)} %bitcast.spot_ref.pos_ref, s32[1,512]{1,0:T(1,128)} %bitcast.13, bf16[1,512,512]{2,1,0:T(8,128)(2,1)} %q_hbm.3, bf16[1,512,512]{2,1,0:T(8,128)(2,1)} %k_hbm.3, bf16[1,512,512]{2,1,0:T(8,128)(2,1)} %v_hbm.3, bf16[1,512,512]{2,1,0:T(8,128)(2,1)} %copy-done.8, ...), custom_call_target="tpu_custom_call" | custom-call | tf_op jit(solution)/shard_map/attend/pallas_call | solution.py:223
  139.5 4.1 %fast_apply.1 = (bf16[1,512,512]{2,1,0:T(8,128)(2,1)}, bf16[512,512]{1,0:T(8,128)(2,1)}) custom-call(s32[1]{0:T(128)} %bitcast.spot_ref.pos_ref, bf16[8,4,3,16,256]{4,3,2,1,0:T(8,128)(2,1)S(1)} %all-to-all-done.2.left, bf16[8,3,16,256]{3,2,1,0:T(8,128)(2,1)S(1)} %get-tuple-element.11.own, bf16[8,3,16,256]{3,2,1,0:T(8,128)(2,1)S(1)} %collective-permute-done.4.one, ...), custom_call_target="tpu_custom_call" | custom-call | tf_op jit(solution)/shard_map/fast_apply/pallas_call | solution.py:369
  143.6 7.2 %all-to-all-start.3 = ((bf16[8,64,512]{2,1,0:T(8,128)(2,1)}), bf16[8,64,512]{2,1,0:T(8,128)(2,1)S(1)}, u32[]{:S(2)}, u32[]{:S(2)}) async-start(bf16[8,64,512]{2,1,0:T(8,128)(2,1)} %bitcast.6), calls=%async_computation.3 | async-start | bytes 1048576 | tf_op jit(solution)/shard_map/all_to_all | solution.py:448
  150.8 0.8 dynamic-slice_bitcast_fusion.flag_ref
  151.6 8.6 %all-to-all-done.3.recv_ref = bf16[8,64,512]{2,1,0:T(8,128)(2,1)S(1)} async-done(((bf16[8,64,512]{2,1,0:T(8,128)(2,1)}), bf16[8,64,512]{2,1,0:T(8,128)(2,1)S(1)}, u32[]{:S(2)}, u32[]{:S(2)}) %all-to-all-start.3) | async-done | bytes 524320 | tf_op jit(solution)/shard_map/all_to_all | solution.py:448
  160.2 0.8 combine.1
  (21 shorter events, 0.0 us)
Async XLA Ops:
  6.0 52.6 %copy-start = (bf16[1,512,512]{2,1,0:T(8,128)(2,1)S(1)}, bf16[1,512,512]{2,1,0:T(8,128)(2,1)}, u32[]{:S(2)}) copy-start(bf16[1,512,512]{2,1,0:T(8,128)(2,1)} %wg.1) | copy-start | bytes 1572868
  6.0 52.6 %copy-start.1 = (bf16[1,512,512]{2,1,0:T(8,128)(2,1)S(1)}, bf16[1,512,512]{2,1,0:T(8,128)(2,1)}, u32[]{:S(2)}) copy-start(bf16[1,512,512]{2,1,0:T(8,128)(2,1)} %wu.1) | copy-start | bytes 1572868
  6.0 52.6 %copy-start.2 = (bf16[1,512,512]{2,1,0:T(8,128)(2,1)S(1)}, bf16[1,512,512]{2,1,0:T(8,128)(2,1)}, u32[]{:S(2)}) copy-start(bf16[1,512,512]{2,1,0:T(8,128)(2,1)} %wd.1) | copy-start | bytes 1572868
  6.1 52.5 %all-to-all-start = ((bf16[32,200,128]{2,1,0:T(8,128)(2,1)}), bf16[32,200,128]{2,1,0:T(8,128)(2,1)S(1)}, u32[]{:S(2)}, u32[]{:S(2)}) async-start(bf16[32,200,128]{2,1,0:T(8,128)(2,1)} %grads.1), calls=%async_computation | async-start | bytes 3276800 | tf_op jit(solution)/shard_map/all_to_all | solution.py:436
  59.8 0.7 copy-start.5
  60.6 28.8 %all-to-all-start.1 = ((bf16[16,3,16,256]{3,2,1,0:T(8,128)(2,1)}), bf16[16,3,16,256]{3,2,1,0:T(8,128)(2,1)S(1)}, u32[]{:S(2)}, u32[]{:S(2)}) async-start(bf16[16,3,16,256]{3,2,1,0:T(8,128)(2,1)} %copy-done.5), calls=%async_computation.1 | async-start | bytes 786432 | tf_op jit(solution)/shard_map/all_to_all | solution.py:439
  72.8 12.7 %collective-permute-start = (bf16[3,16,256]{2,1,0:T(8,128)(2,1)S(1)}, bf16[3,16,256]{2,1,0:T(8,128)(2,1)S(1)}, u32[]{:S(2)}, u32[]{:S(2)}) collective-permute-start(bf16[3,16,256]{2,1,0:T(8,128)(2,1)S(1)} %get-tuple-element.9), channel_id=1, source_target_pairs={{0,32},{1,33},{2,34},{3,35},{4,36},{5,37},{6,38},{7,39},{8,40},{9,... | collective-permute-start | bytes 73736 | tf_op jit(solution)/shard_map/ppermute | solution.py:432
  80.0 5.6 %collective-permute-start.1 = (bf16[3,16,256]{2,1,0:T(8,128)(2,1)S(1)}, bf16[3,16,256]{2,1,0:T(8,128)(2,1)S(1)}, u32[]{:S(2)}, u32[]{:S(2)}) collective-permute-start(bf16[3,16,256]{2,1,0:T(8,128)(2,1)S(1)} %get-tuple-element.9), channel_id=1, source_target_pairs={{0,40},{1,41},{2,42},{3,43},{4,44},{5,45},{6,46},{7,47},{8,48},{9,... | collective-permute-start | bytes 73736 | tf_op jit(solution)/shard_map/ppermute | solution.py:432
  82.8 5.7 %collective-permute-start.2 = (bf16[3,16,256]{2,1,0:T(8,128)(2,1)S(1)}, bf16[3,16,256]{2,1,0:T(8,128)(2,1)S(1)}, u32[]{:S(2)}, u32[]{:S(2)}) collective-permute-start(bf16[3,16,256]{2,1,0:T(8,128)(2,1)S(1)} %get-tuple-element.9), channel_id=1, source_target_pairs={{0,48},{1,49},{2,50},{3,51},{4,52},{5,53},{6,54},{7,55},{8,56},{9,... | collective-permute-start | bytes 73736 | tf_op jit(solution)/shard_map/ppermute | solution.py:432
  84.2 5.2 %collective-permute-start.3 = (bf16[3,16,256]{2,1,0:T(8,128)(2,1)S(1)}, bf16[3,16,256]{2,1,0:T(8,128)(2,1)S(1)}, u32[]{:S(2)}, u32[]{:S(2)}) collective-permute-start(bf16[3,16,256]{2,1,0:T(8,128)(2,1)S(1)} %get-tuple-element.9), channel_id=1, source_target_pairs={{0,56},{1,57},{2,58},{3,59},{4,60},{5,61},{6,62},{7,63},{8,32},{9,... | collective-permute-start | bytes 73736 | tf_op jit(solution)/shard_map/ppermute | solution.py:432
  89.4 5.5 %copy-start.6 = (bf16[1,512,512]{2,1,0:T(8,128)(2,1)S(1)}, bf16[1,512,512]{2,1,0:T(8,128)(2,1)}, u32[]{:S(2)}) copy-start(bf16[1,512,512]{2,1,0:T(8,128)(2,1)} %k_hbm.3) | copy-start | bytes 1572868
  89.4 8.9 %copy-start.7 = (bf16[1,512,512]{2,1,0:T(8,128)(2,1)S(1)}, bf16[1,512,512]{2,1,0:T(8,128)(2,1)}, u32[]{:S(2)}) copy-start(bf16[1,512,512]{2,1,0:T(8,128)(2,1)} %v_hbm.3) | copy-start | bytes 1572868
  90.7 48.8 %all-to-all-start.2 = ((bf16[8,4,3,16,256]{4,3,2,1,0:T(8,128)(2,1)}), bf16[8,4,3,16,256]{4,3,2,1,0:T(8,128)(2,1)S(1)}, u32[]{:S(2)}, u32[]{:S(2)}) async-start(bf16[8,4,3,16,256]{4,3,2,1,0:T(8,128)(2,1)} %get-tuple-element.10), calls=%async_computation.2 | async-start | bytes 1572864 | tf_op jit(solution)/shard_map/all_to_all | solution.py:443
  94.9 26.4 %collective-permute-start.7 = (bf16[1,512,512]{2,1,0:T(8,128)(2,1)S(1)}, bf16[1,512,512]{2,1,0:T(8,128)(2,1)S(1)}, u32[]{:S(2)}, u32[]{:S(2)}) collective-permute-start(bf16[1,512,512]{2,1,0:T(8,128)(2,1)S(1)} %copy-done.6), channel_id=1, source_target_pairs={{0,1},{1,2},{2,3},{3,4},{4,5},{5,6},{6,7},{7,8},{8,9},{9,10},{10,1... | collective-permute-start | bytes 1572872 | tf_op jit(solution)/shard_map/ppermute | solution.py:437
  98.3 34.2 %collective-permute-start.8 = (bf16[1,512,512]{2,1,0:T(8,128)(2,1)S(1)}, bf16[1,512,512]{2,1,0:T(8,128)(2,1)S(1)}, u32[]{:S(2)}, u32[]{:S(2)}) collective-permute-start(bf16[1,512,512]{2,1,0:T(8,128)(2,1)S(1)} %copy-done.7), channel_id=1, source_target_pairs={{0,1},{1,2},{2,3},{3,4},{4,5},{5,6},{6,7},{7,8},{8,9},{9,10},{10,1... | collective-permute-start | bytes 1572872 | tf_op jit(solution)/shard_map/ppermute | solution.py:441
  101.4 38.1 %collective-permute-start.4 = (bf16[8,3,16,256]{3,2,1,0:T(8,128)(2,1)S(1)}, bf16[8,3,16,256]{3,2,1,0:T(8,128)(2,1)S(1)}, u32[]{:S(2)}, u32[]{:S(2)}) collective-permute-start(bf16[8,3,16,256]{3,2,1,0:T(8,128)(2,1)S(1)} %get-tuple-element.11.own), channel_id=1, source_target_pairs={{0,8},{1,9},{2,10},{3,11},{4,12},{5,13},{6,14},{7,15},{8,16},{9,17... | collective-permute-start | bytes 589832 | tf_op jit(solution)/shard_map/ppermute | solution.py:428
  103.9 35.6 %collective-permute-start.5 = (bf16[8,3,16,256]{3,2,1,0:T(8,128)(2,1)S(1)}, bf16[8,3,16,256]{3,2,1,0:T(8,128)(2,1)S(1)}, u32[]{:S(2)}, u32[]{:S(2)}) collective-permute-start(bf16[8,3,16,256]{3,2,1,0:T(8,128)(2,1)S(1)} %get-tuple-element.11.own), channel_id=1, source_target_pairs={{0,16},{1,17},{2,18},{3,19},{4,20},{5,21},{6,22},{7,23},{8,24},{9,... | collective-permute-start | bytes 589832 | tf_op jit(solution)/shard_map/ppermute | solution.py:428
  107.2 32.3 %collective-permute-start.6 = (bf16[8,3,16,256]{3,2,1,0:T(8,128)(2,1)S(1)}, bf16[8,3,16,256]{3,2,1,0:T(8,128)(2,1)S(1)}, u32[]{:S(2)}, u32[]{:S(2)}) collective-permute-start(bf16[8,3,16,256]{3,2,1,0:T(8,128)(2,1)S(1)} %get-tuple-element.11.own), channel_id=1, source_target_pairs={{0,24},{1,25},{2,26},{3,27},{4,28},{5,29},{6,30},{7,31},{8,0},{9,1... | collective-permute-start | bytes 589832 | tf_op jit(solution)/shard_map/ppermute | solution.py:428
  121.3 11.2 %copy-start.8 = (bf16[1,512,512]{2,1,0:T(8,128)(2,1)}, bf16[1,512,512]{2,1,0:T(8,128)(2,1)S(1)}, u32[]{:S(2)}) copy-start(bf16[1,512,512]{2,1,0:T(8,128)(2,1)S(1)} %collective-permute-done.7.pk_hbm) | copy-start | bytes 1572868
  132.5 0.8 copy-start.9
  133.3 6.2 %copy-start.3 = (bf16[1,512,512]{2,1,0:T(8,128)(2,1)S(1)}, bf16[1,512,512]{2,1,0:T(8,128)(2,1)}, u32[]{:S(2)}) copy-start(bf16[1,512,512]{2,1,0:T(8,128)(2,1)} %q_hbm.3) | copy-start | bytes 1572868
  133.3 6.2 %copy-start.4 = (bf16[512,512]{1,0:T(8,128)(2,1)S(1)}, bf16[512,512]{1,0:T(8,128)(2,1)}, u32[]{:S(2)}) copy-start(bf16[512,512]{1,0:T(8,128)(2,1)} %wc_hbm.1) | copy-start | bytes 1572868
  143.6 16.6 %all-to-all-start.3 = ((bf16[8,64,512]{2,1,0:T(8,128)(2,1)}), bf16[8,64,512]{2,1,0:T(8,128)(2,1)S(1)}, u32[]{:S(2)}, u32[]{:S(2)}) async-start(bf16[8,64,512]{2,1,0:T(8,128)(2,1)} %bitcast.6), calls=%async_computation.3 | async-start | bytes 1048576 | tf_op jit(solution)/shard_map/all_to_all | solution.py:448

commit v9 on v8

--- a/solution.py
+++ b/solution.py
@@ -173,25 +173,36 @@
 
 
 def attend_kernel(
-    pos_ref, doc_ref, q_hbm, k_hbm, v_hbm, pk_hbm, pv_hbm, out_hbm,
+    pos_ref, doc_ref, q_hbm, k_hbm, v_hbm, pk_hbm, pv_hbm, edge_k, edge_v, out_hbm,
     q_ref, k_ref, v_ref, pk_ref, pv_ref, att_s, sem,
 ):
     base = pos_ref[0] * 512
     loads = [
         pltpu.make_async_copy(src.at[0], dst, sem.at[i])
-        for i, (src, dst) in enumerate(
-            (
-                (q_hbm, q_ref),
-                (k_hbm, k_ref),
-                (v_hbm, v_ref),
-                (pk_hbm, pk_ref),
-                (pv_hbm, pv_ref),
-            )
-        )
+        for i, (src, dst) in enumerate(((q_hbm, q_ref), (k_hbm, k_ref), (v_hbm, v_ref)))
     ]
     for load in loads:
         load.start()
 
+    def fetch(src_k, src_v):
+        return (
+            pltpu.make_async_copy(src_k.at[0], pk_ref, sem.at[3]),
+            pltpu.make_async_copy(src_v.at[0], pv_ref, sem.at[4]),
+        )
+
+    at_edge = lax.rem(pos_ref[0], 8) == 0
+
+    @pl.when(at_edge)
+    def _():
+        for copy in fetch(edge_k, edge_v):
+            copy.start()
+
+    @pl.when(jnp.logical_not(at_edge))
+    def _():
+        for copy in fetch(pk_hbm, pv_hbm):
+            copy.start()
+
+    loads += fetch(pk_hbm, pv_hbm)
     for load in loads:
         load.wait()
     step = 128
@@ -217,13 +228,13 @@
     store.wait()
 
 
-def attend(pos, q, k, v, doc, pk, pv):
+def attend(pos, q, k, v, doc, pk, pv, edge_k, edge_v):
     vm = pl.BlockSpec(memory_space=pltpu.VMEM)
     hb = pl.BlockSpec(memory_space=pltpu.HBM)
     return pl.pallas_call(
         attend_kernel,
         out_shape=jax.ShapeDtypeStruct((2, 512, 512), F32),
-        in_specs=[pl.BlockSpec(memory_space=pltpu.SMEM), vm] + [hb] * 5,
+        in_specs=[pl.BlockSpec(memory_space=pltpu.SMEM), vm] + [hb] * 7,
         out_specs=hb,
         scratch_shapes=[pltpu.VMEM((512, 512), BF16)] * 5
         + [
@@ -231,7 +242,7 @@
             pltpu.SemaphoreType.DMA((6,)),
         ],
         name="attend",
-    )(pos, doc, q, k, v, pk, pv)
+    )(pos, doc, q, k, v, pk, pv, edge_k, edge_v)
 
 
 def relay_kernel(
@@ -416,7 +427,8 @@
     slabs = [[place(z + lift, y) for lift in (0, 4) for y in range(8)] for z in range(4)]
     rows = [[place(z, y) for y in range(8)] for z in range(8)]
     halves = [list(range(half)), list(range(half, seq_count))]
-    route = [(i - 1, i) for i in range(1, seq_count)]
+    edge = [(i - 1, i) for i in range(8, seq_count, 8)]
+    route = [(i - 1, i) for i in range(1, seq_count) if i % 8]
 
     def turn(block, d):
         pairs = [
@@ -432,6 +444,8 @@
         return lax.ppermute(block, "seq", pairs)
 
     spot = index[None]
+    edge_k = lax.ppermute(k, "seq", edge)
+    edge_v = lax.ppermute(v, "seq", edge)
     terms = grads(k, v, rate, flag[None], wg, wu, wd)
     recv = lax.all_to_all(terms, "seq", 0, 0, axis_index_groups=halves)
     pk = lax.ppermute(k, "seq", route)
@@ -442,7 +456,7 @@
     left, right = relay(spot, right, lefts, wg, wu, wd)
     left = lax.all_to_all(left, "seq", 0, 0, axis_index_groups=rows)
     rights = [right] + [turn(right, d) for d in range(1, 4)]
-    att = attend(spot, q, k, v, doc_start[None], pk, pv)
+    att = attend(spot, q, k, v, doc_start[None], pk, pv, edge_k, edge_v)
     mixed, part = fast_apply(spot, left, rights, q, att, wc)
     flags = lax.dynamic_slice_in_dim(flag, lax.axis_index("head") * 64, 64, 0)[None]
     got = lax.all_to_all(part.reshape(8, 64, 512), "head", 0, 0)

time: 164 us -> 168 us (1.024)
  the two profiles are of different devices: /device:TPU:1 before, /device:TPU:128 now
where the time goes in v9:
time: 168 us; the launch traced here: 167 us
  waiting for transfers between devices  82.4 us (49%)
  starting transfers between devices  62.5 us (37%)
  Pallas kernels  18.9 us (11%)
  local copies, waits for them, and re-layouts  2.34 us (1%)
    all_to_all x1, waiting for transfers between devices, layer(): recv = lax.all_to_all(terms, 'seq', 0, 0, axis_index_groups=halves)  39.8 us
    ppermute x1, waiting for transfers between devices, layer(): pk = lax.ppermute(k, 'seq', route)  17 us
    all_to_all x1, starting transfers between devices, layer(): right = lax.all_to_all(right, 'seq', 0, 0, axis_index_groups=slabs)  13.5 us
    ppermute x4, starting transfers between devices, lift_up(): return lax.ppermute(block, 'seq', pairs)  11.6 us
    all_to_all x1, starting transfers between devices, layer(): recv = lax.all_to_all(terms, 'seq', 0, 0, axis_index_groups=halves)  11.6 us
    all_to_all x1, waiting for transfers between devices, layer(): got = lax.all_to_all(part.reshape(8, 64, 512), 'head', 0, 0)  9.56 us
    ppermute x3, starting transfers between devices, turn(): return lax.ppermute(block, 'seq', pairs)  7.79 us
    pallas_call x1, Pallas kernels, attend(): pl.pallas_call(attend_kernel, out_shape=jax.ShapeDtypeStruct((2, 512, 512...  6.12 us
  transfers between devices with their start and end apart: 15, of which 8 were waited for; matrix products, arithmetic and copies ran while one was open for 0% of the time, Pallas kernels for 4%

profile of v9, /device:TPU:128, one launch (start us, length us, event | category | flops | bytes accessed | tf_op | source)
XLA Modules:
  0.0 167.0 jit_solution(6832855835237889435)
XLA Ops:
  0.6 5.4 %grads.1 = bf16[32,200,128]{2,1,0:T(8,128)(2,1)} custom-call(bf16[1,512,512]{2,1,0:T(8,128)(2,1)} %k_hbm.3, bf16[1,512,512]{2,1,0:T(8,128)(2,1)} %v_hbm.3, bf16[1,512,512]{2,1,0:T(8,128)(2,1)} %wg.1, bf16[1,512,512]{2,1,0:T(8,128)(2,1)} %wu.1, bf16[1,512,512]{2,1,0:T(8,128)(2,1)} %wd.1, f32[1,512]{1,0:T(1,128)} %rate_ref.1, s32[1,512]{1,0:T(1,128)} %bitcast.12), custom_call_target="tpu_custom_call" | custom-call | tf_op jit(solution)/shard_map/grads/pallas_call | solution.py:95
  6.1 11.6 %all-to-all-start = ((bf16[32,200,128]{2,1,0:T(8,128)(2,1)}), bf16[32,200,128]{2,1,0:T(8,128)(2,1)S(1)}, u32[]{:S(2)}, u32[]{:S(2)}) async-start(bf16[32,200,128]{2,1,0:T(8,128)(2,1)} %grads.1), calls=%async_computation | async-start | bytes 3276800 | tf_op jit(solution)/shard_map/all_to_all | solution.py:450
  17.6 39.8 %all-to-all-done.recv_ref = bf16[32,200,128]{2,1,0:T(8,128)(2,1)S(1)} async-done(((bf16[32,200,128]{2,1,0:T(8,128)(2,1)}), bf16[32,200,128]{2,1,0:T(8,128)(2,1)S(1)}, u32[]{:S(2)}, u32[]{:S(2)}) %all-to-all-start) | async-done | bytes 1638432 | tf_op jit(solution)/shard_map/all_to_all | solution.py:450
  57.4 1.2 renorm.1
  58.7 0.7 copy-done.5
  59.4 13.5 %all-to-all-start.1 = ((bf16[16,3,16,256]{3,2,1,0:T(8,128)(2,1)}), bf16[16,3,16,256]{3,2,1,0:T(8,128)(2,1)S(1)}, u32[]{:S(2)}, u32[]{:S(2)}) async-start(bf16[16,3,16,256]{3,2,1,0:T(8,128)(2,1)} %copy-done.5), calls=%async_computation.1 | async-start | bytes 786432 | tf_op jit(solution)/shard_map/all_to_all | solution.py:453
  72.9 7.2 %collective-permute-start.3 = (bf16[3,16,256]{2,1,0:T(8,128)(2,1)S(1)}, bf16[3,16,256]{2,1,0:T(8,128)(2,1)S(1)}, u32[]{:S(2)}, u32[]{:S(2)}) collective-permute-start(bf16[3,16,256]{2,1,0:T(8,128)(2,1)S(1)} %get-tuple-element.9), channel_id=1, source_target_pairs={{0,56},{1,57},{2,58},{3,59},{4,60},{5,61},{6,62},{7,63},{8,32},{9,... | collective-permute-start | bytes 73736 | tf_op jit(solution)/shard_map/ppermute | solution.py:444
  80.1 1.3 collective-permute-start.2
  81.4 1.3 collective-permute-start.1
  82.7 1.8 %collective-permute-start = (bf16[3,16,256]{2,1,0:T(8,128)(2,1)S(1)}, bf16[3,16,256]{2,1,0:T(8,128)(2,1)S(1)}, u32[]{:S(2)}, u32[]{:S(2)}) collective-permute-start(bf16[3,16,256]{2,1,0:T(8,128)(2,1)S(1)} %get-tuple-element.9), channel_id=1, source_target_pairs={{0,32},{1,33},{2,34},{3,35},{4,36},{5,37},{6,38},{7,39},{8,40},{9,... | collective-permute-start | bytes 73736 | tf_op jit(solution)/shard_map/ppermute | solution.py:444
  84.6 1.5 collective-permute-done.zero
  86.0 2.6 %all-to-all-done.1.right = bf16[16,3,16,256]{3,2,1,0:T(8,128)(2,1)S(1)} async-done(((bf16[16,3,16,256]{3,2,1,0:T(8,128)(2,1)}), bf16[16,3,16,256]{3,2,1,0:T(8,128)(2,1)S(1)}, u32[]{:S(2)}, u32[]{:S(2)}) %all-to-all-start.1) | async-done | bytes 393248 | tf_op jit(solution)/shard_map/all_to_all | solution.py:453
  88.6 1.3 relay.1
  89.9 4.5 %all-to-all-start.2 = ((bf16[8,4,3,16,256]{4,3,2,1,0:T(8,128)(2,1)}), bf16[8,4,3,16,256]{4,3,2,1,0:T(8,128)(2,1)S(1)}, u32[]{:S(2)}, u32[]{:S(2)}) async-start(bf16[8,4,3,16,256]{4,3,2,1,0:T(8,128)(2,1)} %get-tuple-element.10), calls=%async_computation.2 | async-start | bytes 1572864 | tf_op jit(solution)/shard_map/all_to_all | solution.py:457
  94.4 3.9 %collective-permute-start.7 = (bf16[1,512,512]{2,1,0:T(8,128)(2,1)S(1)}, bf16[1,512,512]{2,1,0:T(8,128)(2,1)S(1)}, u32[]{:S(2)}, u32[]{:S(2)}) collective-permute-start(bf16[1,512,512]{2,1,0:T(8,128)(2,1)S(1)} %copy-done.6), channel_id=1, source_target_pairs={{0,1},{1,2},{2,3},{3,4},{4,5},{5,6},{6,7},{8,9},{9,10},{10,11},{11... | collective-permute-start | bytes 1572872 | tf_op jit(solution)/shard_map/ppermute | solution.py:451
  98.3 1.3 collective-permute-start.9
  99.7 2.8 %collective-permute-start.8 = (bf16[1,512,512]{2,1,0:T(8,128)(2,1)S(1)}, bf16[1,512,512]{2,1,0:T(8,128)(2,1)S(1)}, u32[]{:S(2)}, u32[]{:S(2)}) collective-permute-start(bf16[1,512,512]{2,1,0:T(8,128)(2,1)S(1)} %copy-done.7), channel_id=1, source_target_pairs={{0,1},{1,2},{2,3},{3,4},{4,5},{5,6},{6,7},{8,9},{9,10},{10,11},{11... | collective-permute-start | bytes 1572872 | tf_op jit(solution)/shard_map/ppermute | solution.py:455
  102.4 1.3 collective-permute-start.10
  103.7 2.5 %collective-permute-start.6 = (bf16[8,3,16,256]{3,2,1,0:T(8,128)(2,1)S(1)}, bf16[8,3,16,256]{3,2,1,0:T(8,128)(2,1)S(1)}, u32[]{:S(2)}, u32[]{:S(2)}) collective-permute-start(bf16[8,3,16,256]{3,2,1,0:T(8,128)(2,1)S(1)} %get-tuple-element.11.own), channel_id=1, source_target_pairs={{0,24},{1,25},{2,26},{3,27},{4,28},{5,29},{6,30},{7,31},{8,0},{9,1... | collective-permute-start | bytes 589832 | tf_op jit(solution)/shard_map/ppermute | solution.py:440
  106.2 17.0 %collective-permute-done.7.pk_hbm = bf16[1,512,512]{2,1,0:T(8,128)(2,1)S(1)} collective-permute-done((bf16[1,512,512]{2,1,0:T(8,128)(2,1)S(1)}, bf16[1,512,512]{2,1,0:T(8,128)(2,1)S(1)}, u32[]{:S(2)}, u32[]{:S(2)}) %collective-permute-start.7) | collective-permute-done | bytes 524320 | tf_op jit(solution)/shard_map/ppermute | solution.py:451
  123.2 1.9 %collective-permute-start.5 = (bf16[8,3,16,256]{3,2,1,0:T(8,128)(2,1)S(1)}, bf16[8,3,16,256]{3,2,1,0:T(8,128)(2,1)S(1)}, u32[]{:S(2)}, u32[]{:S(2)}) collective-permute-start(bf16[8,3,16,256]{3,2,1,0:T(8,128)(2,1)S(1)} %get-tuple-element.11.own), channel_id=1, source_target_pairs={{0,16},{1,17},{2,18},{3,19},{4,20},{5,21},{6,22},{7,23},{8,24},{9,... | collective-permute-start | bytes 589832 | tf_op jit(solution)/shard_map/ppermute | solution.py:440
  125.1 3.4 %collective-permute-start.4 = (bf16[8,3,16,256]{3,2,1,0:T(8,128)(2,1)S(1)}, bf16[8,3,16,256]{3,2,1,0:T(8,128)(2,1)S(1)}, u32[]{:S(2)}, u32[]{:S(2)}) collective-permute-start(bf16[8,3,16,256]{3,2,1,0:T(8,128)(2,1)S(1)} %get-tuple-element.11.own), channel_id=1, source_target_pairs={{0,8},{1,9},{2,10},{3,11},{4,12},{5,13},{6,14},{7,15},{8,16},{9,17... | collective-permute-start | bytes 589832 | tf_op jit(solution)/shard_map/ppermute | solution.py:440
  128.6 3.4 %collective-permute-done.8.pv_hbm = bf16[1,512,512]{2,1,0:T(8,128)(2,1)S(1)} collective-permute-done((bf16[1,512,512]{2,1,0:T(8,128)(2,1)S(1)}, bf16[1,512,512]{2,1,0:T(8,128)(2,1)S(1)}, u32[]{:S(2)}, u32[]{:S(2)}) %collective-permute-start.8) | collective-permute-done | bytes 524320 | tf_op jit(solution)/shard_map/ppermute | solution.py:455
  132.0 3.1 %collective-permute-done.10.edge_v = bf16[1,512,512]{2,1,0:T(8,128)(2,1)S(1)} collective-permute-done((bf16[1,512,512]{2,1,0:T(8,128)(2,1)S(1)}, bf16[1,512,512]{2,1,0:T(8,128)(2,1)S(1)}, u32[]{:S(2)}, u32[]{:S(2)}) %collective-permute-start.10) | collective-permute-done | bytes 524320 | tf_op jit(solution)/shard_map/ppermute | solution.py:448
  135.1 0.8 copy-done.11
  135.9 6.1 %attend.1.att_hbm = f32[2,512,512]{2,1,0:T(8,128)} custom-call(s32[1]{0:T(128)} %bitcast.spot_ref.pos_ref, s32[1,512]{1,0:T(1,128)} %bitcast.13, bf16[1,512,512]{2,1,0:T(8,128)(2,1)} %q_hbm.3, bf16[1,512,512]{2,1,0:T(8,128)(2,1)} %k_hbm.3, bf16[1,512,512]{2,1,0:T(8,128)(2,1)} %v_hbm.3, bf16[1,512,512]{2,1,0:T(8,128)(2,1)} %copy-done.8, ...), custom_call_target="tpu_custom_call" | custom-call | tf_op jit(solution)/shard_map/attend/pallas_call | solution.py:234
  142.1 5.4 %collective-permute-done.4.one = bf16[8,3,16,256]{3,2,1,0:T(8,128)(2,1)S(1)} collective-permute-done((bf16[8,3,16,256]{3,2,1,0:T(8,128)(2,1)S(1)}, bf16[8,3,16,256]{3,2,1,0:T(8,128)(2,1)S(1)}, u32[]{:S(2)}, u32[]{:S(2)}) %collective-permute-start.4) | collective-permute-done | bytes 196640 | tf_op jit(solution)/shard_map/ppermute | solution.py:440
  147.5 4.1 %fast_apply.1 = (bf16[1,512,512]{2,1,0:T(8,128)(2,1)}, bf16[512,512]{1,0:T(8,128)(2,1)}) custom-call(s32[1]{0:T(128)} %bitcast.spot_ref.pos_ref, bf16[8,4,3,16,256]{4,3,2,1,0:T(8,128)(2,1)S(1)} %all-to-all-done.2.left, bf16[8,3,16,256]{3,2,1,0:T(8,128)(2,1)S(1)} %get-tuple-element.11.own, bf16[8,3,16,256]{3,2,1,0:T(8,128)(2,1)S(1)} %collective-permute-done.4.one, ...), custom_call_target="tpu_custom_call" | custom-call | tf_op jit(solution)/shard_map/fast_apply/pallas_call | solution.py:380
  151.6 4.3 %all-to-all-start.3 = ((bf16[8,64,512]{2,1,0:T(8,128)(2,1)}), bf16[8,64,512]{2,1,0:T(8,128)(2,1)S(1)}, u32[]{:S(2)}, u32[]{:S(2)}) async-start(bf16[8,64,512]{2,1,0:T(8,128)(2,1)} %bitcast.6), calls=%async_computation.3 | async-start | bytes 1048576 | tf_op jit(solution)/shard_map/all_to_all | solution.py:462
  155.9 0.8 dynamic-slice_bitcast_fusion.flag_ref
  156.7 9.6 %all-to-all-done.3.recv_ref = bf16[8,64,512]{2,1,0:T(8,128)(2,1)S(1)} async-done(((bf16[8,64,512]{2,1,0:T(8,128)(2,1)}), bf16[8,64,512]{2,1,0:T(8,128)(2,1)S(1)}, u32[]{:S(2)}, u32[]{:S(2)}) %all-to-all-start.3) | async-done | bytes 524320 | tf_op jit(solution)/shard_map/all_to_all | solution.py:462
  166.2 0.8 combine.1
  (29 shorter events, 0.1 us)
Async XLA Ops:
  6.0 51.4 %copy-start = (bf16[1,512,512]{2,1,0:T(8,128)(2,1)S(1)}, bf16[1,512,512]{2,1,0:T(8,128)(2,1)}, u32[]{:S(2)}) copy-start(bf16[1,512,512]{2,1,0:T(8,128)(2,1)} %wg.1) | copy-start | bytes 1572868
  6.0 51.4 %copy-start.1 = (bf16[1,512,512]{2,1,0:T(8,128)(2,1)S(1)}, bf16[1,512,512]{2,1,0:T(8,128)(2,1)}, u32[]{:S(2)}) copy-start(bf16[1,512,512]{2,1,0:T(8,128)(2,1)} %wu.1) | copy-start | bytes 1572868
  6.0 51.4 %copy-start.2 = (bf16[1,512,512]{2,1,0:T(8,128)(2,1)S(1)}, bf16[1,512,512]{2,1,0:T(8,128)(2,1)}, u32[]{:S(2)}) copy-start(bf16[1,512,512]{2,1,0:T(8,128)(2,1)} %wd.1) | copy-start | bytes 1572868
  6.1 51.4 %all-to-all-start = ((bf16[32,200,128]{2,1,0:T(8,128)(2,1)}), bf16[32,200,128]{2,1,0:T(8,128)(2,1)S(1)}, u32[]{:S(2)}, u32[]{:S(2)}) async-start(bf16[32,200,128]{2,1,0:T(8,128)(2,1)} %grads.1), calls=%async_computation | async-start | bytes 3276800 | tf_op jit(solution)/shard_map/all_to_all | solution.py:450
  58.7 0.7 copy-start.5
  59.4 29.2 %all-to-all-start.1 = ((bf16[16,3,16,256]{3,2,1,0:T(8,128)(2,1)}), bf16[16,3,16,256]{3,2,1,0:T(8,128)(2,1)S(1)}, u32[]{:S(2)}, u32[]{:S(2)}) async-start(bf16[16,3,16,256]{3,2,1,0:T(8,128)(2,1)} %copy-done.5), calls=%async_computation.1 | async-start | bytes 786432 | tf_op jit(solution)/shard_map/all_to_all | solution.py:453
  72.9 11.6 %collective-permute-start.3 = (bf16[3,16,256]{2,1,0:T(8,128)(2,1)S(1)}, bf16[3,16,256]{2,1,0:T(8,128)(2,1)S(1)}, u32[]{:S(2)}, u32[]{:S(2)}) collective-permute-start(bf16[3,16,256]{2,1,0:T(8,128)(2,1)S(1)} %get-tuple-element.9), channel_id=1, source_target_pairs={{0,56},{1,57},{2,58},{3,59},{4,60},{5,61},{6,62},{7,63},{8,32},{9,... | collective-permute-start | bytes 73736 | tf_op jit(solution)/shard_map/ppermute | solution.py:444
  80.1 4.5 %collective-permute-start.2 = (bf16[3,16,256]{2,1,0:T(8,128)(2,1)S(1)}, bf16[3,16,256]{2,1,0:T(8,128)(2,1)S(1)}, u32[]{:S(2)}, u32[]{:S(2)}) collective-permute-start(bf16[3,16,256]{2,1,0:T(8,128)(2,1)S(1)} %get-tuple-element.9), channel_id=1, source_target_pairs={{0,48},{1,49},{2,50},{3,51},{4,52},{5,53},{6,54},{7,55},{8,56},{9,... | collective-permute-start | bytes 73736 | tf_op jit(solution)/shard_map/ppermute | solution.py:444
  81.4 3.2 %collective-permute-start.1 = (bf16[3,16,256]{2,1,0:T(8,128)(2,1)S(1)}, bf16[3,16,256]{2,1,0:T(8,128)(2,1)S(1)}, u32[]{:S(2)}, u32[]{:S(2)}) collective-permute-start(bf16[3,16,256]{2,1,0:T(8,128)(2,1)S(1)} %get-tuple-element.9), channel_id=1, source_target_pairs={{0,40},{1,41},{2,42},{3,43},{4,44},{5,45},{6,46},{7,47},{8,48},{9,... | collective-permute-start | bytes 73736 | tf_op jit(solution)/shard_map/ppermute | solution.py:444
  82.7 3.4 %collective-permute-start = (bf16[3,16,256]{2,1,0:T(8,128)(2,1)S(1)}, bf16[3,16,256]{2,1,0:T(8,128)(2,1)S(1)}, u32[]{:S(2)}, u32[]{:S(2)}) collective-permute-start(bf16[3,16,256]{2,1,0:T(8,128)(2,1)S(1)} %get-tuple-element.9), channel_id=1, source_target_pairs={{0,32},{1,33},{2,34},{3,35},{4,36},{5,37},{6,38},{7,39},{8,40},{9,... | collective-permute-start | bytes 73736 | tf_op jit(solution)/shard_map/ppermute | solution.py:444
  88.6 5.8 %copy-start.6 = (bf16[1,512,512]{2,1,0:T(8,128)(2,1)S(1)}, bf16[1,512,512]{2,1,0:T(8,128)(2,1)}, u32[]{:S(2)}) copy-start(bf16[1,512,512]{2,1,0:T(8,128)(2,1)} %k_hbm.3) | copy-start | bytes 1572868
  88.6 11.0 %copy-start.7 = (bf16[1,512,512]{2,1,0:T(8,128)(2,1)S(1)}, bf16[1,512,512]{2,1,0:T(8,128)(2,1)}, u32[]{:S(2)}) copy-start(bf16[1,512,512]{2,1,0:T(8,128)(2,1)} %v_hbm.3) | copy-start | bytes 1572868
  89.9 57.6 %all-to-all-start.2 = ((bf16[8,4,3,16,256]{4,3,2,1,0:T(8,128)(2,1)}), bf16[8,4,3,16,256]{4,3,2,1,0:T(8,128)(2,1)S(1)}, u32[]{:S(2)}, u32[]{:S(2)}) async-start(bf16[8,4,3,16,256]{4,3,2,1,0:T(8,128)(2,1)} %get-tuple-element.10), calls=%async_computation.2 | async-start | bytes 1572864 | tf_op jit(solution)/shard_map/all_to_all | solution.py:457
  94.4 28.8 %collective-permute-start.7 = (bf16[1,512,512]{2,1,0:T(8,128)(2,1)S(1)}, bf16[1,512,512]{2,1,0:T(8,128)(2,1)S(1)}, u32[]{:S(2)}, u32[]{:S(2)}) collective-permute-start(bf16[1,512,512]{2,1,0:T(8,128)(2,1)S(1)} %copy-done.6), channel_id=1, source_target_pairs={{0,1},{1,2},{2,3},{3,4},{4,5},{5,6},{6,7},{8,9},{9,10},{10,11},{11... | collective-permute-start | bytes 1572872 | tf_op jit(solution)/shard_map/ppermute | solution.py:451
  98.3 26.8 %collective-permute-start.9 = (bf16[1,512,512]{2,1,0:T(8,128)(2,1)S(1)}, bf16[1,512,512]{2,1,0:T(8,128)(2,1)S(1)}, u32[]{:S(2)}, u32[]{:S(2)}) collective-permute-start(bf16[1,512,512]{2,1,0:T(8,128)(2,1)S(1)} %copy-done.6), channel_id=1, source_target_pairs={{7,8},{15,16},{23,24},{31,32},{39,40},{47,48},{55,56},{71,72},{79,... | collective-permute-start | bytes 1572872 | tf_op jit(solution)/shard_map/ppermute | solution.py:447
  99.7 32.3 %collective-permute-start.8 = (bf16[1,512,512]{2,1,0:T(8,128)(2,1)S(1)}, bf16[1,512,512]{2,1,0:T(8,128)(2,1)S(1)}, u32[]{:S(2)}, u32[]{:S(2)}) collective-permute-start(bf16[1,512,512]{2,1,0:T(8,128)(2,1)S(1)} %copy-done.7), channel_id=1, source_target_pairs={{0,1},{1,2},{2,3},{3,4},{4,5},{5,6},{6,7},{8,9},{9,10},{10,11},{11... | collective-permute-start | bytes 1572872 | tf_op jit(solution)/shard_map/ppermute | solution.py:455
  102.4 32.7 %collective-permute-start.10 = (bf16[1,512,512]{2,1,0:T(8,128)(2,1)S(1)}, bf16[1,512,512]{2,1,0:T(8,128)(2,1)S(1)}, u32[]{:S(2)}, u32[]{:S(2)}) collective-permute-start(bf16[1,512,512]{2,1,0:T(8,128)(2,1)S(1)} %copy-done.7), channel_id=1, source_target_pairs={{7,8},{15,16},{23,24},{31,32},{39,40},{47,48},{55,56},{71,72},{79,... | collective-permute-start | bytes 1572872 | tf_op jit(solution)/shard_map/ppermute | solution.py:448
  103.7 38.3 %collective-permute-start.6 = (bf16[8,3,16,256]{3,2,1,0:T(8,128)(2,1)S(1)}, bf16[8,3,16,256]{3,2,1,0:T(8,128)(2,1)S(1)}, u32[]{:S(2)}, u32[]{:S(2)}) collective-permute-start(bf16[8,3,16,256]{3,2,1,0:T(8,128)(2,1)S(1)} %get-tuple-element.11.own), channel_id=1, source_target_pairs={{0,24},{1,25},{2,26},{3,27},{4,28},{5,29},{6,30},{7,31},{8,0},{9,1... | collective-permute-start | bytes 589832 | tf_op jit(solution)/shard_map/ppermute | solution.py:440
  123.2 1.9 %copy-start.8 = (bf16[1,512,512]{2,1,0:T(8,128)(2,1)}, bf16[1,512,512]{2,1,0:T(8,128)(2,1)S(1)}, u32[]{:S(2)}) copy-start(bf16[1,512,512]{2,1,0:T(8,128)(2,1)S(1)} %collective-permute-done.7.pk_hbm) | copy-start | bytes 1572868
  123.2 18.9 %collective-permute-start.5 = (bf16[8,3,16,256]{3,2,1,0:T(8,128)(2,1)S(1)}, bf16[8,3,16,256]{3,2,1,0:T(8,128)(2,1)S(1)}, u32[]{:S(2)}, u32[]{:S(2)}) collective-permute-start(bf16[8,3,16,256]{3,2,1,0:T(8,128)(2,1)S(1)} %get-tuple-element.11.own), channel_id=1, source_target_pairs={{0,16},{1,17},{2,18},{3,19},{4,20},{5,21},{6,22},{7,23},{8,24},{9,... | collective-permute-start | bytes 589832 | tf_op jit(solution)/shard_map/ppermute | solution.py:440
  125.1 10.0 %copy-start.9 = (bf16[1,512,512]{2,1,0:T(8,128)(2,1)}, bf16[1,512,512]{2,1,0:T(8,128)(2,1)S(1)}, u32[]{:S(2)}) copy-start(bf16[1,512,512]{2,1,0:T(8,128)(2,1)S(1)} %collective-permute-done.9.edge_k) | copy-start | bytes 1572868
  125.1 22.4 %collective-permute-start.4 = (bf16[8,3,16,256]{3,2,1,0:T(8,128)(2,1)S(1)}, bf16[8,3,16,256]{3,2,1,0:T(8,128)(2,1)S(1)}, u32[]{:S(2)}, u32[]{:S(2)}) collective-permute-start(bf16[8,3,16,256]{3,2,1,0:T(8,128)(2,1)S(1)} %get-tuple-element.11.own), channel_id=1, source_target_pairs={{0,8},{1,9},{2,10},{3,11},{4,12},{5,13},{6,14},{7,15},{8,16},{9,17... | collective-permute-start | bytes 589832 | tf_op jit(solution)/shard_map/ppermute | solution.py:440
  132.0 3.1 %copy-start.10 = (bf16[1,512,512]{2,1,0:T(8,128)(2,1)}, bf16[1,512,512]{2,1,0:T(8,128)(2,1)S(1)}, u32[]{:S(2)}) copy-start(bf16[1,512,512]{2,1,0:T(8,128)(2,1)S(1)} %collective-permute-done.8.pv_hbm) | copy-start | bytes 1572868
  135.1 0.8 copy-start.11
  135.9 11.6 %copy-start.3 = (bf16[1,512,512]{2,1,0:T(8,128)(2,1)S(1)}, bf16[1,512,512]{2,1,0:T(8,128)(2,1)}, u32[]{:S(2)}) copy-start(bf16[1,512,512]{2,1,0:T(8,128)(2,1)} %q_hbm.3) | copy-start | bytes 1572868
  135.9 11.6 %copy-start.4 = (bf16[512,512]{1,0:T(8,128)(2,1)S(1)}, bf16[512,512]{1,0:T(8,128)(2,1)}, u32[]{:S(2)}) copy-start(bf16[512,512]{1,0:T(8,128)(2,1)} %wc_hbm.1) | copy-start | bytes 1572868
  151.6 14.6 %all-to-all-start.3 = ((bf16[8,64,512]{2,1,0:T(8,128)(2,1)}), bf16[8,64,512]{2,1,0:T(8,128)(2,1)S(1)}, u32[]{:S(2)}, u32[]{:S(2)}) async-start(bf16[8,64,512]{2,1,0:T(8,128)(2,1)} %bitcast.6), calls=%async_computation.3 | async-start | bytes 1048576 | tf_op jit(solution)/shard_map/all_to_all | solution.py:462
